TPU v7x, 256 devices: a whole 4x4x8 slice. The times are simulated.
256 devices in a mesh: blk: 16 (over z, x_hi), grp: 16 (over y, x_lo, core).
Axes of the slice: x: 4 (x_hi: 2, x_lo: 2; x = x_hi * 2 + x_lo), y: 4, z: 8, core: 2. Of those that a mesh axis runs over, the one named last changes fastest.
Arguments:
- coil_pos: float32 [3, 10240], P(None, ('blk', 'grp')), may hold values from -1 to 1
- coil_radius: float32 [10240], P(('blk', 'grp')), may hold values from 0.02 to 0.08
- coil_current: bfloat16 [64, 10240], P(None, ('blk', 'grp')), may hold values from -0.109375 to 0.109375
- blank_pos: float32 [3, 32768], P(None, ('blk', 'grp')), may hold values from -1 to 1
- blank_rule: int32 [32768], P(('blk', 'grp')), may hold values from 0 to 7
- blank_cond: float32 [32768], P(('blk', 'grp')), may hold values from 0.3 to 3
- quad_offset: float32 [3, 8, 2], replicated, may hold values from -0.1 to 0.1
- quad_weight: float32 [8, 2], replicated, may hold values from 0.3 to 0.7
Outputs:
- blank_current: bfloat16 [64, 32768], P(None, ('blk', 'grp'))
- coil_reaction: float32 [64, 10240], P(None, ('blk', 'grp'))
All inputs are finite; a program needn't handle non-finite values.
Results may differ from a plain program's by a relative error of at most 0.0066.
Values may be sent and summed in bfloat16 or wider, within the bound.
No kernel may reach another device: no remote copies, remote signals or barrier semaphores. Data moves between devices by JAX's collectives and lax.ppermute only.
A program may use at most 64 MiB of HBM per device.

v0:
```python
import jax
import jax.numpy as jnp
from jax import lax
from jax.sharding import Mesh
from jax.sharding import PartitionSpec as P

BLK = ("blk_0", "blk_1")
BLK_GRP = ("blk_0", "blk_1", "grp")


def split_up(shard, dim, size):
    before, after = (shard.shape[:dim], shard.shape[dim + 1 :])
    return jnp.moveaxis(shard.reshape(*before, size, -1, *after), dim, 0)


def sent_and_summed(shard, axis, dim):
    pieces = split_up(shard, dim, lax.axis_size(axis))
    arrived = lax.all_to_all(pieces, axis, split_axis=0, concat_axis=0, tiled=True)
    return arrived.astype(jnp.float32).sum(axis=0)


def from_everyone(shard, axis):
    size = lax.axis_size(axis)
    return lax.all_to_all(
        jnp.broadcast_to(shard[None], (size, *shard.shape)), axis, 0, 0, tiled=True
    )


def laid_out(pieces, dim):
    shape = list(pieces.shape[1:])
    shape[dim] *= pieces.shape[0]
    return jnp.moveaxis(pieces, 0, dim).reshape(shape)


def gather_directly(shard, axis, dim):
    pieces = from_everyone(shard, axis)
    return laid_out(pieces, dim)


def from_behind(shard, axis, by):
    size = lax.axis_size(axis)
    return lax.ppermute(shard, axis, [(i, (i + by) % size) for i in range(size)])


def whole_of(shard, axes, dim):
    out = shard
    for number in range(len(axes) - 1, -1, -1):
        out = lax.all_gather(out, axes[number], axis=dim, tiled=True)
    return out


def blank_geometry(blank_pos, blank_rule, quad_offset, quad_weight):
    rules = quad_weight.shape[0]
    points = quad_weight.shape[1]
    onehot = (blank_rule[None, :] == jnp.arange(rules, dtype=jnp.int32)[:, None]).astype(
        jnp.float32
    )
    table_rows = []
    base_rows = []
    zeros_row = jnp.zeros_like(blank_pos[0])
    for point in range(points):
        table_rows += [
            quad_offset[0, :, point],
            quad_offset[1, :, point],
            quad_offset[2, :, point],
            quad_weight[:, point],
        ]
        base_rows += [blank_pos[0], blank_pos[1], blank_pos[2], zeros_row]
    table = jnp.stack(table_rows, 0)
    base = jnp.stack(base_rows, 0)
    return base + jnp.dot(table, onehot, precision=lax.Precision.HIGHEST)


def kernel_block(coil_geometry, geometry):
    points = geometry.shape[0] // 4
    running = jnp.zeros((coil_geometry.shape[1], geometry.shape[1]), jnp.float32)
    for point in range(points):
        delta_x = coil_geometry[0][:, None] - geometry[4 * point][None, :]
        delta_y = coil_geometry[1][:, None] - geometry[4 * point + 1][None, :]
        delta_z = coil_geometry[2][:, None] - geometry[4 * point + 2][None, :]
        squared = (
            delta_x * delta_x + delta_y * delta_y + delta_z * delta_z + coil_geometry[3][:, None]
        )
        running = running + geometry[4 * point + 3][None, :] * lax.rsqrt(squared)
    return running


def form_block(induced, group_geometry, stored, anchor, coil_geometry, coil_current):
    group_width = group_geometry.shape[1]
    kernel_tile = kernel_block(coil_geometry, group_geometry).astype(jnp.bfloat16)
    column = anchor * group_width
    stored = lax.dynamic_update_slice(stored, kernel_tile, (jnp.int32(0), column))
    partial_value = jnp.dot(coil_current, kernel_tile, preferred_element_type=jnp.float32)
    induced = induced + sent_and_summed(partial_value.astype(jnp.bfloat16), "grp", 1)
    return (induced, stored)


def per_device(
    coil_pos, coil_radius, coil_current, blank_pos, blank_rule, blank_cond, quad_offset, quad_weight
):
    coil_geometry = jnp.concatenate([coil_pos, (coil_radius * coil_radius)[None, :]], 0)
    geometry = blank_geometry(blank_pos, blank_rule, quad_offset, quad_weight)
    samples = coil_current.shape[0]
    coil_count = coil_current.shape[1]
    local_blanks = geometry.shape[1]
    total_blanks = local_blanks * lax.axis_size(BLK) * lax.axis_size("grp")
    cycle_count = lax.axis_size(BLK)
    position = lax.axis_index(BLK)
    stored = jnp.zeros((coil_count, total_blanks), jnp.bfloat16)
    induced = jnp.zeros((samples, local_blanks), jnp.float32)
    group_geometry = gather_directly(geometry, "grp", 1)

    def advance(turn_index, carried):
        running, moving, kept = carried
        anchor = (position - turn_index) % cycle_count
        running, kept = form_block(running, moving, kept, anchor, coil_geometry, coil_current)
        running, moving = from_behind((running, moving), BLK, 1)
        return (running, moving, kept)

    induced, _, stored = lax.fori_loop(0, cycle_count, advance, (induced, group_geometry, stored))
    blank_current = induced.astype(jnp.bfloat16)
    weighted = (blank_cond[None, :] * blank_current.astype(jnp.float32)).astype(jnp.bfloat16)
    group_weighted = gather_directly(weighted, "grp", 1)
    reaction = lax.dot_general(
        whole_of(group_weighted, BLK, 1),
        stored,
        (((1,), (1,)), ((), ())),
        preferred_element_type=jnp.float32,
    )
    coil_reaction = reaction * (2.0 / total_blanks)
    return (blank_current, coil_reaction)


def solution(mesh):
    split = Mesh(mesh.devices.reshape(8, 2, mesh.shape["grp"]), ("blk_0", "blk_1", "grp"))
    return jax.shard_map(
        per_device,
        mesh=split,
        in_specs=(
            P(None, BLK_GRP),
            P(BLK_GRP),
            P(None, BLK_GRP),
            P(None, BLK_GRP),
            P(BLK_GRP),
            P(BLK_GRP),
            P(),
            P(),
        ),
        out_specs=(P(None, BLK_GRP), P(None, BLK_GRP)),
        check_vma=False,
    )
```

profile of v0, /device:TPU:1, one launch (start us, length us, event | category | flops | bytes accessed | tf_op | source)
XLA Modules:
  0.0 445.8 jit_solution(18146350402105474659)
XLA Ops:
  10.3 6.9 %all-to-all-start.1 = ((f32[16,8,128]{2,1,0:T(8,128)}), f32[16,8,128]{2,1,0:T(8,128)S(1)}, u32[]{:S(2)}, u32[]{:S(2)}) async-start(f32[16,8,128]{2,1,0:T(8,128)} %broadcast_in_dim.9), calls=%async_computation.1 | async-start | bytes 131072 | tf_op jit(solution)/shard_map/all_to_all | solution.py:24
  23.2 337.9 %while.19 = (s32[]{:T(128)}, f32[64,128]{1,0:T(8,128)S(1)}, f32[8,2048]{1,0:T(8,128)S(1)}, bf16[40,32768]{1,0:T(8,128)(2,1)S(1)}, f32[3,40]{1,0:T(4,128)S(1)}, /...) while((s32[]{:T(128)}, f32[64,128]{1,0:T(8,128)S(1)}, ...), condition=%wide.region_2.3_spmd, body=%wide.region_0.2_spmd.sunk | while | flops 14483474 | bytes 2925536 | solution.py:120
  38.5 7.7 %collective-permute-done = f32[64,128]{1,0:T(8,128)S(1)} collective-permute-done((f32[64,128]{1,0:T(8,128)S(1)}, f32[64,128]{1,0:T(8,128)S(1)}, u32[]{:S(2)}, u32[]{:S(2)}) %collective-permute-start) | collective-permute-done | bytes 32800 | tf_op jit(solution)/shard_map/while/body/eval_jaxpr/ppermute | solution.py:42
  52.7 7.5 %all-to-all-done = bf16[16,64,128]{2,1,0:T(8,128)(2,1)S(1)} async-done(((bf16[16,64,128]{2,1,0:T(8,128)(2,1)}), bf16[16,64,128]{2,1,0:T(8,128)(2,1)S(1)}, u32[]{:S(2)}, u32[]{:S(2)}) %all-to-all-start) | async-done | bytes 262176 | tf_op jit(solution)/shard_map/while/body/eval_jaxpr/all_to_all | solution.py:18
  73.7 7.5 %all-to-all-done = bf16[16,64,128]{2,1,0:T(8,128)(2,1)S(1)} async-done(((bf16[16,64,128]{2,1,0:T(8,128)(2,1)}), bf16[16,64,128]{2,1,0:T(8,128)(2,1)S(1)}, u32[]{:S(2)}, u32[]{:S(2)}) %all-to-all-start) | async-done | bytes 262176 | tf_op jit(solution)/shard_map/while/body/eval_jaxpr/all_to_all | solution.py:18
  81.7 6.0 %collective-permute-done = f32[64,128]{1,0:T(8,128)S(1)} collective-permute-done((f32[64,128]{1,0:T(8,128)S(1)}, f32[64,128]{1,0:T(8,128)S(1)}, u32[]{:S(2)}, u32[]{:S(2)}) %collective-permute-start) | collective-permute-done | bytes 32800 | tf_op jit(solution)/shard_map/while/body/eval_jaxpr/ppermute | solution.py:42
  94.8 7.5 %all-to-all-done = bf16[16,64,128]{2,1,0:T(8,128)(2,1)S(1)} async-done(((bf16[16,64,128]{2,1,0:T(8,128)(2,1)}), bf16[16,64,128]{2,1,0:T(8,128)(2,1)S(1)}, u32[]{:S(2)}, u32[]{:S(2)}) %all-to-all-start) | async-done | bytes 262176 | tf_op jit(solution)/shard_map/while/body/eval_jaxpr/all_to_all | solution.py:18
  102.8 6.0 %collective-permute-done = f32[64,128]{1,0:T(8,128)S(1)} collective-permute-done((f32[64,128]{1,0:T(8,128)S(1)}, f32[64,128]{1,0:T(8,128)S(1)}, u32[]{:S(2)}, u32[]{:S(2)}) %collective-permute-start) | collective-permute-done | bytes 32800 | tf_op jit(solution)/shard_map/while/body/eval_jaxpr/ppermute | solution.py:42
  115.8 7.5 %all-to-all-done = bf16[16,64,128]{2,1,0:T(8,128)(2,1)S(1)} async-done(((bf16[16,64,128]{2,1,0:T(8,128)(2,1)}), bf16[16,64,128]{2,1,0:T(8,128)(2,1)S(1)}, u32[]{:S(2)}, u32[]{:S(2)}) %all-to-all-start) | async-done | bytes 262176 | tf_op jit(solution)/shard_map/while/body/eval_jaxpr/all_to_all | solution.py:18
  136.8 7.5 %all-to-all-done = bf16[16,64,128]{2,1,0:T(8,128)(2,1)S(1)} async-done(((bf16[16,64,128]{2,1,0:T(8,128)(2,1)}), bf16[16,64,128]{2,1,0:T(8,128)(2,1)S(1)}, u32[]{:S(2)}, u32[]{:S(2)}) %all-to-all-start) | async-done | bytes 262176 | tf_op jit(solution)/shard_map/while/body/eval_jaxpr/all_to_all | solution.py:18
  157.9 7.5 %all-to-all-done = bf16[16,64,128]{2,1,0:T(8,128)(2,1)S(1)} async-done(((bf16[16,64,128]{2,1,0:T(8,128)(2,1)}), bf16[16,64,128]{2,1,0:T(8,128)(2,1)S(1)}, u32[]{:S(2)}, u32[]{:S(2)}) %all-to-all-start) | async-done | bytes 262176 | tf_op jit(solution)/shard_map/while/body/eval_jaxpr/all_to_all | solution.py:18
  165.9 6.0 %collective-permute-done = f32[64,128]{1,0:T(8,128)S(1)} collective-permute-done((f32[64,128]{1,0:T(8,128)S(1)}, f32[64,128]{1,0:T(8,128)S(1)}, u32[]{:S(2)}, u32[]{:S(2)}) %collective-permute-start) | collective-permute-done | bytes 32800 | tf_op jit(solution)/shard_map/while/body/eval_jaxpr/ppermute | solution.py:42
  178.9 7.5 %all-to-all-done = bf16[16,64,128]{2,1,0:T(8,128)(2,1)S(1)} async-done(((bf16[16,64,128]{2,1,0:T(8,128)(2,1)}), bf16[16,64,128]{2,1,0:T(8,128)(2,1)S(1)}, u32[]{:S(2)}, u32[]{:S(2)}) %all-to-all-start) | async-done | bytes 262176 | tf_op jit(solution)/shard_map/while/body/eval_jaxpr/all_to_all | solution.py:18
  199.9 7.5 %all-to-all-done = bf16[16,64,128]{2,1,0:T(8,128)(2,1)S(1)} async-done(((bf16[16,64,128]{2,1,0:T(8,128)(2,1)}), bf16[16,64,128]{2,1,0:T(8,128)(2,1)S(1)}, u32[]{:S(2)}, u32[]{:S(2)}) %all-to-all-start) | async-done | bytes 262176 | tf_op jit(solution)/shard_map/while/body/eval_jaxpr/all_to_all | solution.py:18
  221.0 7.5 %all-to-all-done = bf16[16,64,128]{2,1,0:T(8,128)(2,1)S(1)} async-done(((bf16[16,64,128]{2,1,0:T(8,128)(2,1)}), bf16[16,64,128]{2,1,0:T(8,128)(2,1)S(1)}, u32[]{:S(2)}, u32[]{:S(2)}) %all-to-all-start) | async-done | bytes 262176 | tf_op jit(solution)/shard_map/while/body/eval_jaxpr/all_to_all | solution.py:18
  242.0 7.5 %all-to-all-done = bf16[16,64,128]{2,1,0:T(8,128)(2,1)S(1)} async-done(((bf16[16,64,128]{2,1,0:T(8,128)(2,1)}), bf16[16,64,128]{2,1,0:T(8,128)(2,1)S(1)}, u32[]{:S(2)}, u32[]{:S(2)}) %all-to-all-start) | async-done | bytes 262176 | tf_op jit(solution)/shard_map/while/body/eval_jaxpr/all_to_all | solution.py:18
  263.0 7.5 %all-to-all-done = bf16[16,64,128]{2,1,0:T(8,128)(2,1)S(1)} async-done(((bf16[16,64,128]{2,1,0:T(8,128)(2,1)}), bf16[16,64,128]{2,1,0:T(8,128)(2,1)S(1)}, u32[]{:S(2)}, u32[]{:S(2)}) %all-to-all-start) | async-done | bytes 262176 | tf_op jit(solution)/shard_map/while/body/eval_jaxpr/all_to_all | solution.py:18
  284.0 7.5 %all-to-all-done = bf16[16,64,128]{2,1,0:T(8,128)(2,1)S(1)} async-done(((bf16[16,64,128]{2,1,0:T(8,128)(2,1)}), bf16[16,64,128]{2,1,0:T(8,128)(2,1)S(1)}, u32[]{:S(2)}, u32[]{:S(2)}) %all-to-all-start) | async-done | bytes 262176 | tf_op jit(solution)/shard_map/while/body/eval_jaxpr/all_to_all | solution.py:18
  305.1 7.5 %all-to-all-done = bf16[16,64,128]{2,1,0:T(8,128)(2,1)S(1)} async-done(((bf16[16,64,128]{2,1,0:T(8,128)(2,1)}), bf16[16,64,128]{2,1,0:T(8,128)(2,1)S(1)}, u32[]{:S(2)}, u32[]{:S(2)}) %all-to-all-start) | async-done | bytes 262176 | tf_op jit(solution)/shard_map/while/body/eval_jaxpr/all_to_all | solution.py:18
  326.1 7.5 %all-to-all-done = bf16[16,64,128]{2,1,0:T(8,128)(2,1)S(1)} async-done(((bf16[16,64,128]{2,1,0:T(8,128)(2,1)}), bf16[16,64,128]{2,1,0:T(8,128)(2,1)S(1)}, u32[]{:S(2)}, u32[]{:S(2)}) %all-to-all-start) | async-done | bytes 262176 | tf_op jit(solution)/shard_map/while/body/eval_jaxpr/all_to_all | solution.py:18
  347.1 7.5 %all-to-all-done = bf16[16,64,128]{2,1,0:T(8,128)(2,1)S(1)} async-done(((bf16[16,64,128]{2,1,0:T(8,128)(2,1)}), bf16[16,64,128]{2,1,0:T(8,128)(2,1)S(1)}, u32[]{:S(2)}, u32[]{:S(2)}) %all-to-all-start) | async-done | bytes 262176 | tf_op jit(solution)/shard_map/while/body/eval_jaxpr/all_to_all | solution.py:18
  361.8 12.0 %all_to_all.23 = bf16[16,64,128]{2,1,0:T(8,128)(2,1)S(1)} all-to-all(bf16[16,64,128]{2,1,0:T(8,128)(2,1)S(1)} %broadcast_in_dim.11), channel_id=1, replica_groups=mesh['blk_0'=8,'blk_1'=2,'grp'=16] {'grp'}, dimensions={0} | all-to-all | bytes 524288 | tf_op jit(solution)/shard_map/all_to_all | solution.py:24
  373.8 9.1 %all_gather.6 = bf16[64,4096]{1,0:T(8,128)(2,1)} all-gather(bf16[64,2048]{1,0:T(8,128)(2,1)S(1)} %copy_bitcast_fusion), channel_id=1, replica_groups=mesh['blk_0'=8,'blk_1'=2,'grp'=16] {'blk_1'}, dimensions={1}, use_global_device_ids=true | all-gather | bytes 786432 | tf_op jit(solution)/shard_map/all_gather | solution.py:48
  382.9 52.0 %all-gather.2.cloned.1.call-done = bf16[64,32768]{1,0:T(8,128)(2,1)} async-done(((bf16[64,4096]{1,0:T(8,128)(2,1)}), bf16[64,32768]{1,0:T(8,128)(2,1)}) %all-gather.2.cloned.1.call-update) | async-done | bytes 4194320 | tf_op jit(solution)/shard_map/all_gather | solution.py:48
  (227 shorter events, 212.5 us)
Async XLA Ops:
  10.3 12.7 %all-to-all-start.1 = ((f32[16,8,128]{2,1,0:T(8,128)}), f32[16,8,128]{2,1,0:T(8,128)S(1)}, u32[]{:S(2)}, u32[]{:S(2)}) async-start(f32[16,8,128]{2,1,0:T(8,128)} %broadcast_in_dim.9), calls=%async_computation.1 | async-start | bytes 131072 | tf_op jit(solution)/shard_map/all_to_all | solution.py:24
  17.2 417.8 %all-gather.2.cloned.1.call-start = ((), (), s32[]{:S(2)}) async-start(), calls=%async_computation.3 | async-start | bytes 4718592 | tf_op jit(solution)/shard_map/all_gather | solution.py:48
  24.6 11.0 %all-to-all-start = ((bf16[16,64,128]{2,1,0:T(8,128)(2,1)}), bf16[16,64,128]{2,1,0:T(8,128)(2,1)S(1)}, u32[]{:S(2)}, u32[]{:S(2)}) async-start(bf16[16,64,128]{2,1,0:T(8,128)(2,1)} %bitcast.77), calls=%async_computation | async-start | bytes 524288 | tf_op jit(solution)/shard_map/while/body/eval_jaxpr/all_to_all | solution.py:18
  28.3 10.2 %collective-permute-start.1 = (f32[8,2048]{1,0:T(8,128)S(1)}, f32[8,2048]{1,0:T(8,128)S(1)}, u32[]{:S(2)}, u32[]{:S(2)}) collective-permute-start(f32[8,2048]{1,0:T(8,128)S(1)} %copy.26), channel_id=1, source_target_pairs={{0,16},{16,32},{32,48},{48,64},{64,80},{80,96},{96,112},{112,128},... | collective-permute-start | bytes 196616 | tf_op jit(solution)/shard_map/while/body/eval_jaxpr/ppermute | solution.py:42
  35.6 10.5 %collective-permute-start = (f32[64,128]{1,0:T(8,128)S(1)}, f32[64,128]{1,0:T(8,128)S(1)}, u32[]{:S(2)}, u32[]{:S(2)}) collective-permute-start(f32[64,128]{1,0:T(8,128)S(1)} %add.218), channel_id=1, source_target_pairs={{0,16},{16,32},{32,48},{48,64},{64,80},{80,96},{96,112},{112,128},... | collective-permute-start | bytes 98312 | tf_op jit(solution)/shard_map/while/body/eval_jaxpr/ppermute | solution.py:42
  47.5 12.7 %all-to-all-start = ((bf16[16,64,128]{2,1,0:T(8,128)(2,1)}), bf16[16,64,128]{2,1,0:T(8,128)(2,1)S(1)}, u32[]{:S(2)}, u32[]{:S(2)}) async-start(bf16[16,64,128]{2,1,0:T(8,128)(2,1)} %bitcast.77), calls=%async_computation | async-start | bytes 524288 | tf_op jit(solution)/shard_map/while/body/eval_jaxpr/all_to_all | solution.py:18
  68.1 13.2 %all-to-all-start = ((bf16[16,64,128]{2,1,0:T(8,128)(2,1)}), bf16[16,64,128]{2,1,0:T(8,128)(2,1)S(1)}, u32[]{:S(2)}, u32[]{:S(2)}) async-start(bf16[16,64,128]{2,1,0:T(8,128)(2,1)} %bitcast.77), calls=%async_computation | async-start | bytes 524288 | tf_op jit(solution)/shard_map/while/body/eval_jaxpr/all_to_all | solution.py:18
  73.7 8.0 %collective-permute-start.1 = (f32[8,2048]{1,0:T(8,128)S(1)}, f32[8,2048]{1,0:T(8,128)S(1)}, u32[]{:S(2)}, u32[]{:S(2)}) collective-permute-start(f32[8,2048]{1,0:T(8,128)S(1)} %copy.26), channel_id=1, source_target_pairs={{0,16},{16,32},{32,48},{48,64},{64,80},{80,96},{96,112},{112,128},... | collective-permute-start | bytes 196616 | tf_op jit(solution)/shard_map/while/body/eval_jaxpr/ppermute | solution.py:42
  89.1 13.2 %all-to-all-start = ((bf16[16,64,128]{2,1,0:T(8,128)(2,1)}), bf16[16,64,128]{2,1,0:T(8,128)(2,1)S(1)}, u32[]{:S(2)}, u32[]{:S(2)}) async-start(bf16[16,64,128]{2,1,0:T(8,128)(2,1)} %bitcast.77), calls=%async_computation | async-start | bytes 524288 | tf_op jit(solution)/shard_map/while/body/eval_jaxpr/all_to_all | solution.py:18
  110.1 13.2 %all-to-all-start = ((bf16[16,64,128]{2,1,0:T(8,128)(2,1)}), bf16[16,64,128]{2,1,0:T(8,128)(2,1)S(1)}, u32[]{:S(2)}, u32[]{:S(2)}) async-start(bf16[16,64,128]{2,1,0:T(8,128)(2,1)} %bitcast.77), calls=%async_computation | async-start | bytes 524288 | tf_op jit(solution)/shard_map/while/body/eval_jaxpr/all_to_all | solution.py:18
  131.2 13.2 %all-to-all-start = ((bf16[16,64,128]{2,1,0:T(8,128)(2,1)}), bf16[16,64,128]{2,1,0:T(8,128)(2,1)S(1)}, u32[]{:S(2)}, u32[]{:S(2)}) async-start(bf16[16,64,128]{2,1,0:T(8,128)(2,1)} %bitcast.77), calls=%async_computation | async-start | bytes 524288 | tf_op jit(solution)/shard_map/while/body/eval_jaxpr/all_to_all | solution.py:18
  152.2 13.2 %all-to-all-start = ((bf16[16,64,128]{2,1,0:T(8,128)(2,1)}), bf16[16,64,128]{2,1,0:T(8,128)(2,1)S(1)}, u32[]{:S(2)}, u32[]{:S(2)}) async-start(bf16[16,64,128]{2,1,0:T(8,128)(2,1)} %bitcast.77), calls=%async_computation | async-start | bytes 524288 | tf_op jit(solution)/shard_map/while/body/eval_jaxpr/all_to_all | solution.py:18
  157.8 8.0 %collective-permute-start.1 = (f32[8,2048]{1,0:T(8,128)S(1)}, f32[8,2048]{1,0:T(8,128)S(1)}, u32[]{:S(2)}, u32[]{:S(2)}) collective-permute-start(f32[8,2048]{1,0:T(8,128)S(1)} %copy.26), channel_id=1, source_target_pairs={{0,16},{16,32},{32,48},{48,64},{64,80},{80,96},{96,112},{112,128},... | collective-permute-start | bytes 196616 | tf_op jit(solution)/shard_map/while/body/eval_jaxpr/ppermute | solution.py:42
  173.2 13.2 %all-to-all-start = ((bf16[16,64,128]{2,1,0:T(8,128)(2,1)}), bf16[16,64,128]{2,1,0:T(8,128)(2,1)S(1)}, u32[]{:S(2)}, u32[]{:S(2)}) async-start(bf16[16,64,128]{2,1,0:T(8,128)(2,1)} %bitcast.77), calls=%async_computation | async-start | bytes 524288 | tf_op jit(solution)/shard_map/while/body/eval_jaxpr/all_to_all | solution.py:18
  194.2 13.2 %all-to-all-start = ((bf16[16,64,128]{2,1,0:T(8,128)(2,1)}), bf16[16,64,128]{2,1,0:T(8,128)(2,1)S(1)}, u32[]{:S(2)}, u32[]{:S(2)}) async-start(bf16[16,64,128]{2,1,0:T(8,128)(2,1)} %bitcast.77), calls=%async_computation | async-start | bytes 524288 | tf_op jit(solution)/shard_map/while/body/eval_jaxpr/all_to_all | solution.py:18
  215.3 13.2 %all-to-all-start = ((bf16[16,64,128]{2,1,0:T(8,128)(2,1)}), bf16[16,64,128]{2,1,0:T(8,128)(2,1)S(1)}, u32[]{:S(2)}, u32[]{:S(2)}) async-start(bf16[16,64,128]{2,1,0:T(8,128)(2,1)} %bitcast.77), calls=%async_computation | async-start | bytes 524288 | tf_op jit(solution)/shard_map/while/body/eval_jaxpr/all_to_all | solution.py:18
  236.3 13.2 %all-to-all-start = ((bf16[16,64,128]{2,1,0:T(8,128)(2,1)}), bf16[16,64,128]{2,1,0:T(8,128)(2,1)S(1)}, u32[]{:S(2)}, u32[]{:S(2)}) async-start(bf16[16,64,128]{2,1,0:T(8,128)(2,1)} %bitcast.77), calls=%async_computation | async-start | bytes 524288 | tf_op jit(solution)/shard_map/while/body/eval_jaxpr/all_to_all | solution.py:18
  257.3 13.2 %all-to-all-start = ((bf16[16,64,128]{2,1,0:T(8,128)(2,1)}), bf16[16,64,128]{2,1,0:T(8,128)(2,1)S(1)}, u32[]{:S(2)}, u32[]{:S(2)}) async-start(bf16[16,64,128]{2,1,0:T(8,128)(2,1)} %bitcast.77), calls=%async_computation | async-start | bytes 524288 | tf_op jit(solution)/shard_map/while/body/eval_jaxpr/all_to_all | solution.py:18
  278.4 13.2 %all-to-all-start = ((bf16[16,64,128]{2,1,0:T(8,128)(2,1)}), bf16[16,64,128]{2,1,0:T(8,128)(2,1)S(1)}, u32[]{:S(2)}, u32[]{:S(2)}) async-start(bf16[16,64,128]{2,1,0:T(8,128)(2,1)} %bitcast.77), calls=%async_computation | async-start | bytes 524288 | tf_op jit(solution)/shard_map/while/body/eval_jaxpr/all_to_all | solution.py:18
  299.4 13.2 %all-to-all-start = ((bf16[16,64,128]{2,1,0:T(8,128)(2,1)}), bf16[16,64,128]{2,1,0:T(8,128)(2,1)S(1)}, u32[]{:S(2)}, u32[]{:S(2)}) async-start(bf16[16,64,128]{2,1,0:T(8,128)(2,1)} %bitcast.77), calls=%async_computation | async-start | bytes 524288 | tf_op jit(solution)/shard_map/while/body/eval_jaxpr/all_to_all | solution.py:18
  305.0 8.0 %collective-permute-start.1 = (f32[8,2048]{1,0:T(8,128)S(1)}, f32[8,2048]{1,0:T(8,128)S(1)}, u32[]{:S(2)}, u32[]{:S(2)}) collective-permute-start(f32[8,2048]{1,0:T(8,128)S(1)} %copy.26), channel_id=1, source_target_pairs={{0,16},{16,32},{32,48},{48,64},{64,80},{80,96},{96,112},{112,128},... | collective-permute-start | bytes 196616 | tf_op jit(solution)/shard_map/while/body/eval_jaxpr/ppermute | solution.py:42
  320.4 13.2 %all-to-all-start = ((bf16[16,64,128]{2,1,0:T(8,128)(2,1)}), bf16[16,64,128]{2,1,0:T(8,128)(2,1)S(1)}, u32[]{:S(2)}, u32[]{:S(2)}) async-start(bf16[16,64,128]{2,1,0:T(8,128)(2,1)} %bitcast.77), calls=%async_computation | async-start | bytes 524288 | tf_op jit(solution)/shard_map/while/body/eval_jaxpr/all_to_all | solution.py:18
  326.1 8.0 %collective-permute-start.1 = (f32[8,2048]{1,0:T(8,128)S(1)}, f32[8,2048]{1,0:T(8,128)S(1)}, u32[]{:S(2)}, u32[]{:S(2)}) collective-permute-start(f32[8,2048]{1,0:T(8,128)S(1)} %copy.26), channel_id=1, source_target_pairs={{0,16},{16,32},{32,48},{48,64},{64,80},{80,96},{96,112},{112,128},... | collective-permute-start | bytes 196616 | tf_op jit(solution)/shard_map/while/body/eval_jaxpr/ppermute | solution.py:42
  341.5 13.2 %all-to-all-start = ((bf16[16,64,128]{2,1,0:T(8,128)(2,1)}), bf16[16,64,128]{2,1,0:T(8,128)(2,1)S(1)}, u32[]{:S(2)}, u32[]{:S(2)}) async-start(bf16[16,64,128]{2,1,0:T(8,128)(2,1)} %bitcast.77), calls=%async_computation | async-start | bytes 524288 | tf_op jit(solution)/shard_map/while/body/eval_jaxpr/all_to_all | solution.py:18
  (29 other events, 555.0 us)
Sparse Core Ops, SparseCore 0:
  383.1 51.8 all-gather.1
where the time goes:
time: 448 us; the launch traced here: 446 us
  waiting for transfers between devices  272 us (61%)
  starting transfers between devices  101 us (23%)
  blocking collectives  21.1 us (5%)
  local copies, waits for them, and re-layouts  15.7 us (4%)
  between operations  14.1 us (3%)
  matrix products  12.9 us (3%)
  other arithmetic  7.52 us (2%)
    all_to_all x16, waiting for transfers between devices, sent_and_summed(): lax.all_to_all(pieces, axis, split_axis=0, concat_axis=0, tiled=True)  117 us
    ppermute x32, waiting for transfers between devices, from_behind(): lax.ppermute(shard, axis, [(i, (i + by) % size) for i in range(size)])  97.8 us
    all_to_all x16, starting transfers between devices, sent_and_summed(): lax.all_to_all(pieces, axis, split_axis=0, concat_axis=0, tiled=True)  88 us
    all_gather x1, waiting for transfers between devices, whole_of(): out = lax.all_gather(out, axes[number], axis=dim, tiled=True)  52 us
    reshape x16, local copies, waits for them, and re-layouts, split_up(): return jnp.moveaxis(shard.reshape(*before, size, -1, *after), dim, 0)  12.4 us
    all_to_all x1, blocking collectives, from_everyone(): lax.all_to_all(jnp.broadcast_to(shard[None], (size, *shard.shape)), axis,...  12 us
    all_gather x1, blocking collectives, whole_of(): out = lax.all_gather(out, axes[number], axis=dim, tiled=True)  9.09 us
  transfers between devices with their start and end apart: 50, of which 34 were waited for; matrix products, arithmetic and copies ran while one was open for 2% of the time, Pallas kernels for 0%

commit v1 on v0

v1 whole, which is shorter than its diff:
```python
import jax
import jax.numpy as jnp
from jax import lax
from jax.experimental import pallas as pl
from jax.experimental.pallas import tpu as pltpu
from jax.sharding import Mesh
from jax.sharding import PartitionSpec as P

AXES = ("zh", "zl", "xh", "y", "xl", "core")
SIZES = (4, 2, 2, 4, 2, 2)
ROWS = ("zh",)
COLS = ("zl", "xh", "y", "xl")
LANES = 128
BF16 = jnp.bfloat16
F32 = jnp.float32


def parts_of(value):
    high = value.astype(BF16).astype(F32)
    rest = value - high
    mid = rest.astype(BF16).astype(F32)
    low = (rest - mid).astype(BF16).astype(F32)
    return [high, mid, low]


def prepare(pos_ref, radius_ref, current_ref, blank_ref, rule_ref, cond_ref, payload_ref, tile_ref):
    samples = current_ref.shape[1]
    coils = current_ref.shape[0]
    x, y, z = (pos_ref[pl.ds(axis, 1), :] for axis in range(3))
    radius = radius_ref[...]
    square = x * x + y * y + z * z + radius * radius
    rows = []
    for value in (x, y, z):
        for part in parts_of(value):
            rows += [part, part, part]
    rows += parts_of(square)
    rows += [jnp.ones_like(x)] * 3
    rows.append(jnp.zeros((LANES - samples - len(rows), coils), F32))
    geometry = jnp.concatenate(rows, 0).T
    payload = jnp.concatenate([current_ref[...].astype(F32), geometry], 1).astype(BF16)
    for copy in range(payload_ref.shape[0]):
        payload_ref[copy] = payload
    rule = rule_ref[...].astype(F32)
    tile_ref[...] = jnp.concatenate(
        [blank_ref[...], rule, cond_ref[...], jnp.zeros((3, rule.shape[1]), F32)], 0
    )


def blank_features(samples, offset_ref, weight_ref, *refs):
    tiles, (feature_ref, row_ref) = refs[:-2], refs[-2:]
    rules, points = weight_ref.shape
    base = [jnp.concatenate([tile[pl.ds(row, 1), :] for tile in tiles], 1) for row in range(5)]
    rule, cond = base[3], base[4]
    weights = []
    for point in range(points):
        place = []
        offsets = [jnp.zeros_like(rule) for _ in range(3)]
        weight = jnp.zeros_like(rule)
        for number in range(rules):
            here = rule == float(number)
            for axis in range(3):
                offsets[axis] = jnp.where(here, offset_ref[axis, number, point], offsets[axis])
            weight = jnp.where(here, weight_ref[number, point], weight)
        weights.append(weight)
        place = [base[axis] + offsets[axis] for axis in range(3)]
        square = place[0] * place[0] + place[1] * place[1] + place[2] * place[2]
        rows = [jnp.zeros((samples, rule.shape[1]), F32)]
        for value in place:
            rows += [-2.0 * part for part in parts_of(value)] * 3
        rows += [jnp.ones_like(rule)] * 3
        rows += parts_of(square)
        filled = sum(row.shape[0] for row in rows)
        rows.append(jnp.zeros((LANES - filled, rule.shape[1]), F32))
        feature_ref[point] = jnp.concatenate(rows, 0).astype(BF16)
    row_ref[...] = jnp.concatenate([*weights, cond, jnp.zeros((5, rule.shape[1]), F32)], 0)


def form(first, tile, payload_ref, feature_ref, row_ref, *refs):
    if first:
        kernel_ref, out_ref = refs
    else:
        before_ref, kernel_ref, out_ref = refs
    samples = out_ref.shape[0]
    points = feature_ref.shape[0]
    total = None
    for step in range(payload_ref.shape[0] // tile):
        at = pl.ds(step * tile, tile)
        payload = payload_ref[at, :]
        block = None
        for point in range(points):
            squared = jnp.dot(payload, feature_ref[point], preferred_element_type=F32)
            term = row_ref[pl.ds(point, 1), :] * lax.rsqrt(squared)
            block = term if block is None else block + term
        block = block.astype(BF16)
        kernel_ref[at, :] = block
        product = lax.dot_general(
            payload, block, (((0,), (0,)), ((), ())), preferred_element_type=F32
        )
        total = product if total is None else total + product
    total = total[:samples]
    if not first:
        total = total + before_ref[...]
    out_ref[...] = total.astype(out_ref.dtype)


def react(row_ref, *refs):
    arrivals = refs[:-6]
    own_kernel_ref, other_kernel_ref, current_ref, weighted_ref, own_ref, other_ref = refs[-6:]
    count = len(arrivals)
    width = current_ref.shape[1]
    blocks = []
    for block in range(count):
        total = None
        for behind in range(count):
            piece = arrivals[behind][:, pl.ds((block - behind) % count * width, width)].astype(F32)
            total = piece if total is None else total + piece
        blocks.append(total.astype(BF16))
    current_ref[...] = blocks[0]
    current = jnp.concatenate(blocks, 1).astype(F32)
    weighted = (row_ref[pl.ds(2, 1), :] * current).astype(BF16)
    weighted_ref[...] = weighted
    for kernel_ref, out_ref in ((other_kernel_ref, other_ref), (own_kernel_ref, own_ref)):
        out_ref[...] = lax.dot_general(
            kernel_ref[...], weighted, (((1,), (1,)), ((), ())), preferred_element_type=F32
        ).astype(out_ref.dtype)


def from_behind(value, axis, by):
    size = lax.axis_size(axis)
    return lax.ppermute(value, axis, [(i, (i + by) % size) for i in range(size)])


def shaped(shape, dtype):
    return jax.ShapeDtypeStruct(shape, dtype)


def per_device(
    coil_pos, coil_radius, coil_current, blank_pos, blank_rule, blank_cond, quad_offset, quad_weight
):
    samples, coils = coil_current.shape
    blanks = blank_pos.shape[1]
    total_blanks = blanks * lax.axis_size(AXES)
    cols = lax.axis_size(COLS)
    rows = lax.axis_size(ROWS)
    points = quad_weight.shape[1]
    held = cols * coils
    width = rows * blanks

    payload, tile = pl.pallas_call(
        prepare,
        out_shape=(shaped((cols, coils, LANES), BF16), shaped((8, blanks), F32)),
        name="prepare",
    )(
        coil_pos,
        coil_radius[None, :],
        coil_current.T,
        blank_pos,
        blank_rule[None, :],
        blank_cond[None, :],
    )
    own = lax.all_to_all(payload, COLS, 0, 0, tiled=True).reshape(held, LANES)
    tiles = [tile] + [from_behind(tile, ROWS, by) for by in range(1, rows)]
    smem = pl.BlockSpec(memory_space=pltpu.SMEM)
    vmem = pl.BlockSpec(memory_space=pltpu.VMEM)
    features, table = pl.pallas_call(
        lambda *refs: blank_features(samples, *refs),
        out_shape=(shaped((points, LANES, width), BF16), shaped((8, width), F32)),
        in_specs=[smem, smem] + [vmem] * rows,
        name="blank_features",
    )(quad_offset, quad_weight, *tiles)

    other = from_behind(own, "core", 1)
    cost = pl.CostEstimate(
        flops=2 * held * width * LANES * (points + 1),
        transcendentals=points * held * width,
        bytes_accessed=2 * held * (width + LANES),
    )
    step = 256 if held % 256 == 0 else held
    own_kernel, partial = pl.pallas_call(
        lambda *refs: form(True, step, *refs),
        out_shape=(shaped((held, width), BF16), shaped((samples, width), F32)),
        cost_estimate=cost,
        name="form_own",
    )(own, features, table)
    other_kernel, partial = pl.pallas_call(
        lambda *refs: form(False, step, *refs),
        out_shape=(shaped((held, width), BF16), shaped((samples, width), BF16)),
        cost_estimate=cost,
        name="form_other",
    )(other, features, table, partial)

    arrivals = [partial] + [from_behind(partial, ROWS, by) for by in range(1, rows)]
    blank_current, _, own_reaction, other_reaction = pl.pallas_call(
        react,
        out_shape=(
            shaped((samples, blanks), BF16),
            shaped((samples, width), BF16),
            shaped((held, samples), F32),
            shaped((held, samples), BF16),
        ),
        name="react",
    )(table, *arrivals, own_kernel, other_kernel)
    reaction = own_reaction + from_behind(other_reaction, "core", 1).astype(F32)
    pieces = reaction.astype(BF16).reshape(cols, coils, samples)
    arrived = lax.all_to_all(pieces, COLS, 0, 0, tiled=True)
    summed = arrived.astype(F32).sum(axis=0) * (2.0 / total_blanks)
    return (blank_current, summed.T)


def solution(mesh):
    split = Mesh(mesh.devices.reshape(SIZES), AXES)
    whole = P(None, AXES)
    return jax.shard_map(
        per_device,
        mesh=split,
        in_specs=(whole, P(AXES), whole, whole, P(AXES), P(AXES), P(), P()),
        out_specs=(whole, whole),
        check_vma=False,
    )
```

time: 448 us -> 79.2 us (0.18)
  waiting for transfers between devices: 272 us -> 9.11 us
  starting transfers between devices: 101 us -> 16.8 us
  Pallas kernels: 0 us -> 14.4 us
  between operations: 14.1 us -> 0.68 us
  matrix products: 12.9 us -> 0 us
  local copies, waits for them, and re-layouts: 15.7 us -> 5.69 us
  blocking collectives: 21.1 us -> 30.1 us
  other arithmetic: 7.52 us -> 1.85 us
    all_to_all x17 -> x0, waiting for transfers between devices: 122 us -> none  [the longest x16 117 us: sent_and_summed(): lax.all_to_all(pieces, axis, split_axis=0, concat_axis=0, tiled=True)]
    all_to_all x17 -> x0, starting transfers between devices: 95 us -> none  [the longest x16 88 us: sent_and_summed(): lax.all_to_all(pieces, axis, split_axis=0, concat_axis=0, tiled=True)]
    ppermute x32 -> x8, waiting for transfers between devices: 97.8 us -> 9.11 us  [from_behind(): lax.ppermute(value, axis, [(i, (i + by) % size) for i in range(size)])]
    all_gather x1 -> x0, waiting for transfers between devices: 52 us -> none  [whole_of(): out = lax.all_gather(out, axes[number], axis=dim, tiled=True)]
    all_to_all x1 -> x2, blocking collectives: 12 us -> 30.1 us  [the longest x1 18.1 us: per_device(): own = lax.all_to_all(payload, COLS, 0, 0, tiled=True).reshape(held, LANES)]
    pallas_call x0 -> x5, Pallas kernels: none -> 14.4 us  [the longest x1 3.62 us: per_device(): pl.pallas_call(react, out_shape=(shaped((samples, blanks), BF16), shaped(...]
    dot_general x18 -> x0, matrix products: 12.9 us -> none  [the longest x16 8.01 us: form_block(): jnp.dot(coil_current, kernel_tile, preferred_element_type=jnp.float32)]
    reshape x17 -> x0, local copies, waits for them, and re-layouts: 12.4 us -> none  [the longest x16 12.4 us: split_up(): return jnp.moveaxis(shard.reshape(*before, size, -1, *after), dim, 0)]
  transfers between devices with their start and end apart: 50 -> 8, of which waited for: 34 -> 4; matrix products, arithmetic and copies ran while one was open for 2% -> 3% of each run, Pallas kernels for 0% -> 7%
where the time goes in v1:
time: 79.2 us; the launch traced here: 78.7 us
  blocking collectives  30.1 us (38%)
  starting transfers between devices  16.8 us (21%)
  Pallas kernels  14.4 us (18%)
  waiting for transfers between devices  9.11 us (12%)
  local copies, waits for them, and re-layouts  5.69 us (7%)
  other arithmetic  1.85 us (2%)
    all_to_all x1, blocking collectives, per_device(): own = lax.all_to_all(payload, COLS, 0, 0, tiled=True).reshape(held, LANES)  18.1 us
    ppermute x8, starting transfers between devices, from_behind(): lax.ppermute(value, axis, [(i, (i + by) % size) for i in range(size)])  16.8 us
    all_to_all x1, blocking collectives, per_device(): arrived = lax.all_to_all(pieces, COLS, 0, 0, tiled=True)  12 us
    ppermute x8, waiting for transfers between devices, from_behind(): lax.ppermute(value, axis, [(i, (i + by) % size) for i in range(size)])  9.11 us
    unnamed x20, local copies, waits for them, and re-layouts  5.69 us
    pallas_call x1, Pallas kernels, per_device(): pl.pallas_call(react, out_shape=(shaped((samples, blanks), BF16), shaped(...  3.62 us
    pallas_call x1, Pallas kernels, per_device(): pl.pallas_call(lambda *refs: form(False, step, *refs), out_shape=(shaped(...  3.62 us
    pallas_call x1, Pallas kernels, per_device(): pl.pallas_call(lambda *refs: form(True, step, *refs), out_shape=(shaped((...  3.61 us
  transfers between devices with their start and end apart: 8, of which 4 were waited for; matrix products, arithmetic and copies ran while one was open for 3% of the time, Pallas kernels for 7%

profile of v1, /device:TPU:1, one launch (start us, length us, event | category | flops | bytes accessed | tf_op | source)
XLA Modules:
  0.0 78.7 jit_solution(880718565648603680)
XLA Ops:
  0.6 1.7 %prepare.1 = (bf16[32,40,128]{2,1,0:T(8,128)(2,1)}, f32[8,128]{1,0:T(8,128)}) custom-call(f32[3,40]{1,0:T(4,128)} %pos_ref.1, f32[1,40]{1,0:T(1,128)} %bitcast.12, bf16[40,64]{1,0:T(8,128)(2,1)} %bitcast.11, f32[3,128]{1,0:T(4,128)} %blank_ref.1, s32[1,128]{1,0:T(1,128)} %bitcast.13, f32[1,128]{1,0:T(1,128)} %bitcast.14), custom_call_target="tpu_custom_call" | custom-call | tf_op jit(solution)/shard_map/prepare/pallas_call | solution.py:149
  2.3 18.1 %all_to_all.10 = bf16[32,40,128]{2,1,0:T(8,128)(2,1)S(1)} all-to-all(bf16[32,40,128]{2,1,0:T(8,128)(2,1)} %get-tuple-element.15), channel_id=1, replica_groups=mesh['zh'=4,'zl'=2,'xh'=2,'y'=4,'xl'=2,'core'=2] {'zl','xh','y','xl'}, dimensions={0} | all-to-all | bytes 655360 | tf_op jit(solution)/shard_map/all_to_all | solution.py:161
  20.4 2.0 %collective-permute-start.3 = (bf16[1280,128]{1,0:T(8,128)(2,1)S(1)}, bf16[1280,128]{1,0:T(8,128)(2,1)S(1)}, u32[]{:S(2)}, u32[]{:S(2)}) collective-permute-start(bf16[1280,128]{1,0:T(8,128)(2,1)S(1)} %bitcast.9), channel_id=1, source_target_pairs={{0,1},{1,0},{2,3},{3,2},{4,5},{5,4},{6,7},{7,6},{8,9},{9,8},{10,11... | collective-permute-start | bytes 983048 | tf_op jit(solution)/shard_map/ppermute | solution.py:130
  22.5 5.1 %collective-permute-start.2 = (f32[8,128]{1,0:T(8,128)}, f32[8,128]{1,0:T(8,128)S(1)}, u32[]{:S(2)}, u32[]{:S(2)}) collective-permute-start(f32[8,128]{1,0:T(8,128)} %get-tuple-element.13.refs_2_), channel_id=1, source_target_pairs={{0,192},{64,0},{128,64},{192,128},{1,193},{65,1},{129,65},{193,129... | collective-permute-start | bytes 12296 | tf_op jit(solution)/shard_map/ppermute | solution.py:130
  27.6 1.2 %collective-permute-start.1 = (f32[8,128]{1,0:T(8,128)}, f32[8,128]{1,0:T(8,128)S(1)}, u32[]{:S(2)}, u32[]{:S(2)}) collective-permute-start(f32[8,128]{1,0:T(8,128)} %get-tuple-element.13.refs_2_), channel_id=1, source_target_pairs={{0,128},{64,192},{128,0},{192,64},{1,129},{65,193},{129,1},{193,65... | collective-permute-start | bytes 12296 | tf_op jit(solution)/shard_map/ppermute | solution.py:130
  28.8 2.1 %collective-permute-start = (f32[8,128]{1,0:T(8,128)}, f32[8,128]{1,0:T(8,128)S(1)}, u32[]{:S(2)}, u32[]{:S(2)}) collective-permute-start(f32[8,128]{1,0:T(8,128)} %get-tuple-element.13.refs_2_), channel_id=1, source_target_pairs={{0,64},{64,128},{128,192},{192,0},{1,65},{65,129},{129,193},{193,1... | collective-permute-start | bytes 12296 | tf_op jit(solution)/shard_map/ppermute | solution.py:130
  30.8 1.3 %copy.11.refs_1_ = f32[8,2]{1,0:T(8,128)} copy(f32[8,2]{0,1:T(2,128)} %param.15) | data formatting | bytes 128 | tf_op args[7]
  32.2 1.4 %copy.10.refs_0_ = f32[3,8,2]{2,1,0:T(8,128)} copy(f32[3,8,2]{1,2,0:T(2,128)} %param.14) | data formatting | bytes 384 | tf_op args[6]
  33.6 0.6 collective-permute-done.1.refs_4_
  35.4 1.9 %blank_features.1 = (bf16[2,128,512]{2,1,0:T(8,128)(2,1)}, f32[8,512]{1,0:T(8,128)}) custom-call(f32[3,8,2]{2,1,0:T(8,128)} %copy.10.refs_0_, f32[8,2]{1,0:T(8,128)} %copy.11.refs_1_, f32[8,128]{1,0:T(8,128)} %get-tuple-element.13.refs_2_, f32[8,128]{1,0:T(8,128)} %copy-done.6, f32[8,128]{1,0:T(8,128)} %copy-done.5, f32[8,128]{1,0:T(8,128)} %copy-done.4), custom_call_target="tpu_custom_call" | custom-call | tf_op jit(solution)/shard_map/blank_features/pallas_call | solution.py:165
  37.3 3.6 %form_own.1 = (bf16[1280,512]{1,0:T(8,128)(2,1)}, f32[64,512]{1,0:T(8,128)}) custom-call(bf16[1280,128]{1,0:T(8,128)(2,1)} %bitcast.10, bf16[2,128,512]{2,1,0:T(8,128)(2,1)} %get-tuple-element.16.refs_1_, f32[8,512]{1,0:T(8,128)} %get-tuple-element.14.refs_2_.row_ref), custom_call_target="tpu_custom_call" | custom-call | flops 503316480 | bytes 1638400 | tf_op jit(solution)/shard_map/form_own/pallas_call | solution.py:179
  40.9 0.7 copy-done.7
  41.6 3.6 %form_other.1 = (bf16[1280,512]{1,0:T(8,128)(2,1)}, bf16[64,512]{1,0:T(8,128)(2,1)}) custom-call(bf16[1280,128]{1,0:T(8,128)(2,1)} %copy-done.7, bf16[2,128,512]{2,1,0:T(8,128)(2,1)} %get-tuple-element.16.refs_1_, f32[8,512]{1,0:T(8,128)} %get-tuple-element.14.refs_2_.row_ref, f32[64,512]{1,0:T(8,128)} %get-tuple-element.17.refs_3_), custom_call_target="tpu_custom_call" | custom-call | flops 503316480 | bytes 1638400 | tf_op jit(solution)/shard_map/form_other/pallas_call | solution.py:185
  45.3 1.2 %collective-permute-start.6 = (bf16[64,512]{1,0:T(8,128)(2,1)}, bf16[64,512]{1,0:T(8,128)(2,1)S(1)}, u32[]{:S(2)}, u32[]{:S(2)}) collective-permute-start(bf16[64,512]{1,0:T(8,128)(2,1)} %get-tuple-element.18.refs_0_), channel_id=1, source_target_pairs={{0,192},{64,0},{128,64},{192,128},{1,193},{65,1},{129,65},{193,129... | collective-permute-start | bytes 196616 | tf_op jit(solution)/shard_map/ppermute | solution.py:130
  46.5 3.9 %collective-permute-start.5 = (bf16[64,512]{1,0:T(8,128)(2,1)}, bf16[64,512]{1,0:T(8,128)(2,1)S(1)}, u32[]{:S(2)}, u32[]{:S(2)}) collective-permute-start(bf16[64,512]{1,0:T(8,128)(2,1)} %get-tuple-element.18.refs_0_), channel_id=1, source_target_pairs={{0,128},{64,192},{128,0},{192,64},{1,129},{65,193},{129,1},{193,65... | collective-permute-start | bytes 196616 | tf_op jit(solution)/shard_map/ppermute | solution.py:130
  50.6 3.1 %collective-permute-done.5.refs_2_ = bf16[64,512]{1,0:T(8,128)(2,1)S(1)} collective-permute-done((bf16[64,512]{1,0:T(8,128)(2,1)}, bf16[64,512]{1,0:T(8,128)(2,1)S(1)}, u32[]{:S(2)}, u32[]{:S(2)}) %collective-permute-start.5) | collective-permute-done | bytes 65568 | tf_op jit(solution)/shard_map/ppermute | solution.py:130
  53.7 3.9 %collective-permute-done.4.refs_1_ = bf16[64,512]{1,0:T(8,128)(2,1)S(1)} collective-permute-done((bf16[64,512]{1,0:T(8,128)(2,1)}, bf16[64,512]{1,0:T(8,128)(2,1)S(1)}, u32[]{:S(2)}, u32[]{:S(2)}) %collective-permute-start.4) | collective-permute-done | bytes 65568 | tf_op jit(solution)/shard_map/ppermute | solution.py:130
  57.7 0.6 copy-done.3
  58.3 3.6 %react.1 = (bf16[64,128]{1,0:T(8,128)(2,1)}, bf16[64,512]{1,0:T(8,128)(2,1)}, f32[1280,64]{1,0:T(8,128)}, bf16[1280,64]{1,0:T(8,128)(2,1)}) custom-call(f32[8,512]{1,0:T(8,128)} %get-tuple-element.14.refs_2_.row_ref, bf16[64,512]{1,0:T(8,128)(2,1)} %get-tuple-element.18.refs_0_, bf16[64,512]{1,0:T(8,128)(2,1)} %copy-done.3, bf16[64,512]{1,0:T(8,128)(2,1)} %copy-done.2, ...), custom_call_target="tpu_custom_call" | custom-call | tf_op jit(solution)/shard_map/react/pallas_call | solution.py:193
  61.9 1.0 %collective-permute-start.7 = (bf16[1280,64]{1,0:T(8,128)(2,1)}, bf16[1280,64]{1,0:T(8,128)(2,1)S(1)}, u32[]{:S(2)}, u32[]{:S(2)}) collective-permute-start(bf16[1280,64]{1,0:T(8,128)(2,1)} %get-tuple-element.23), channel_id=1, source_target_pairs={{0,1},{1,0},{2,3},{3,2},{4,5},{5,4},{6,7},{7,6},{8,9},{9,8},{10,11... | collective-permute-start | bytes 491528 | tf_op jit(solution)/shard_map/ppermute | solution.py:130
  62.9 1.5 %collective-permute-done.7 = bf16[1280,64]{1,0:T(8,128)(2,1)S(1)} collective-permute-done((bf16[1280,64]{1,0:T(8,128)(2,1)}, bf16[1280,64]{1,0:T(8,128)(2,1)S(1)}, u32[]{:S(2)}, u32[]{:S(2)}) %collective-permute-start.7) | collective-permute-done | bytes 163872 | tf_op jit(solution)/shard_map/ppermute | solution.py:130
  64.4 1.2 %add_convert_fusion = bf16[1280,64]{1,0:T(8,128)(2,1)S(1)} fusion(f32[1280,64]{1,0:T(8,128)} %get-tuple-element.22, bf16[1280,64]{1,0:T(8,128)(2,1)S(1)} %collective-permute-done.7), kind=kLoop, calls=%fused_computation.1 | loop fusion | flops 245760 | bytes 655360 | tf_op jit(solution)/shard_map/convert_element_type | solution.py:204
  65.8 12.0 %all_to_all.11 = bf16[32,2,1280]{2,1,0:T(2,128)(2,1)S(1)} all-to-all(bf16[32,2,1280]{2,1,0:T(2,128)(2,1)S(1)} %reshape.12), channel_id=1, replica_groups=mesh['zh'=4,'zl'=2,'xh'=2,'y'=4,'xl'=2,'core'=2] {'zl','xh','y','xl'}, dimensions={0} | all-to-all | bytes 327680 | tf_op jit(solution)/shard_map/all_to_all | solution.py:205
  78.1 0.6 multiply_bitcast_fusion
  (22 shorter events, 2.0 us)
Async XLA Ops:
  20.4 16.9 %copy-start = (bf16[32,40,128]{2,1,0:T(8,128)(2,1)}, bf16[32,40,128]{2,1,0:T(8,128)(2,1)S(1)}, u32[]{:S(2)}) copy-start(bf16[32,40,128]{2,1,0:T(8,128)(2,1)S(1)} %all_to_all.10) | copy-start | bytes 983044
  20.4 20.5 %collective-permute-start.3 = (bf16[1280,128]{1,0:T(8,128)(2,1)S(1)}, bf16[1280,128]{1,0:T(8,128)(2,1)S(1)}, u32[]{:S(2)}, u32[]{:S(2)}) collective-permute-start(bf16[1280,128]{1,0:T(8,128)(2,1)S(1)} %bitcast.9), channel_id=1, source_target_pairs={{0,1},{1,0},{2,3},{3,2},{4,5},{5,4},{6,7},{7,6},{8,9},{9,8},{10,11... | collective-permute-start | bytes 983048 | tf_op jit(solution)/shard_map/ppermute | solution.py:130
  22.5 11.1 %collective-permute-start.2 = (f32[8,128]{1,0:T(8,128)}, f32[8,128]{1,0:T(8,128)S(1)}, u32[]{:S(2)}, u32[]{:S(2)}) collective-permute-start(f32[8,128]{1,0:T(8,128)} %get-tuple-element.13.refs_2_), channel_id=1, source_target_pairs={{0,192},{64,0},{128,64},{192,128},{1,193},{65,1},{129,65},{193,129... | collective-permute-start | bytes 12296 | tf_op jit(solution)/shard_map/ppermute | solution.py:130
  27.6 6.6 %collective-permute-start.1 = (f32[8,128]{1,0:T(8,128)}, f32[8,128]{1,0:T(8,128)S(1)}, u32[]{:S(2)}, u32[]{:S(2)}) collective-permute-start(f32[8,128]{1,0:T(8,128)} %get-tuple-element.13.refs_2_), channel_id=1, source_target_pairs={{0,128},{64,192},{128,0},{192,64},{1,129},{65,193},{129,1},{193,65... | collective-permute-start | bytes 12296 | tf_op jit(solution)/shard_map/ppermute | solution.py:130
  28.8 5.4 %collective-permute-start = (f32[8,128]{1,0:T(8,128)}, f32[8,128]{1,0:T(8,128)S(1)}, u32[]{:S(2)}, u32[]{:S(2)}) collective-permute-start(f32[8,128]{1,0:T(8,128)} %get-tuple-element.13.refs_2_), channel_id=1, source_target_pairs={{0,64},{64,128},{128,192},{192,0},{1,65},{65,129},{129,193},{193,1... | collective-permute-start | bytes 12296 | tf_op jit(solution)/shard_map/ppermute | solution.py:130
  33.6 0.6 copy-start.4
  34.2 0.6 copy-start.5
  34.8 0.6 copy-start.6
  40.9 0.7 copy-start.7
  45.3 5.4 %collective-permute-start.6 = (bf16[64,512]{1,0:T(8,128)(2,1)}, bf16[64,512]{1,0:T(8,128)(2,1)S(1)}, u32[]{:S(2)}, u32[]{:S(2)}) collective-permute-start(bf16[64,512]{1,0:T(8,128)(2,1)} %get-tuple-element.18.refs_0_), channel_id=1, source_target_pairs={{0,192},{64,0},{128,64},{192,128},{1,193},{65,1},{129,65},{193,129... | collective-permute-start | bytes 196616 | tf_op jit(solution)/shard_map/ppermute | solution.py:130
  46.5 7.3 %collective-permute-start.5 = (bf16[64,512]{1,0:T(8,128)(2,1)}, bf16[64,512]{1,0:T(8,128)(2,1)S(1)}, u32[]{:S(2)}, u32[]{:S(2)}) collective-permute-start(bf16[64,512]{1,0:T(8,128)(2,1)} %get-tuple-element.18.refs_0_), channel_id=1, source_target_pairs={{0,128},{64,192},{128,0},{192,64},{1,129},{65,193},{129,1},{193,65... | collective-permute-start | bytes 196616 | tf_op jit(solution)/shard_map/ppermute | solution.py:130
  50.4 7.3 %collective-permute-start.4 = (bf16[64,512]{1,0:T(8,128)(2,1)}, bf16[64,512]{1,0:T(8,128)(2,1)S(1)}, u32[]{:S(2)}, u32[]{:S(2)}) collective-permute-start(bf16[64,512]{1,0:T(8,128)(2,1)} %get-tuple-element.18.refs_0_), channel_id=1, source_target_pairs={{0,64},{64,128},{128,192},{192,0},{1,65},{65,129},{129,193},{193,1... | collective-permute-start | bytes 196616 | tf_op jit(solution)/shard_map/ppermute | solution.py:130
  50.6 7.0 %copy-start.1 = (bf16[64,512]{1,0:T(8,128)(2,1)}, bf16[64,512]{1,0:T(8,128)(2,1)S(1)}, u32[]{:S(2)}) copy-start(bf16[64,512]{1,0:T(8,128)(2,1)S(1)} %collective-permute-done.6.refs_3_) | copy-start | bytes 196612
  53.7 3.9 %copy-start.2 = (bf16[64,512]{1,0:T(8,128)(2,1)}, bf16[64,512]{1,0:T(8,128)(2,1)S(1)}, u32[]{:S(2)}) copy-start(bf16[64,512]{1,0:T(8,128)(2,1)S(1)} %collective-permute-done.5.refs_2_) | copy-start | bytes 196612
  57.7 0.6 copy-start.3
  61.9 2.5 %collective-permute-start.7 = (bf16[1280,64]{1,0:T(8,128)(2,1)}, bf16[1280,64]{1,0:T(8,128)(2,1)S(1)}, u32[]{:S(2)}, u32[]{:S(2)}) collective-permute-start(bf16[1280,64]{1,0:T(8,128)(2,1)} %get-tuple-element.23), channel_id=1, source_target_pairs={{0,1},{1,0},{2,3},{3,2},{4,5},{5,4},{6,7},{7,6},{8,9},{9,8},{10,11... | collective-permute-start | bytes 491528 | tf_op jit(solution)/shard_map/ppermute | solution.py:130

commit v2 on v1

--- a/solution.py
+++ b/solution.py
@@ -13,6 +13,7 @@
 LANES = 128
 BF16 = jnp.bfloat16
 F32 = jnp.float32
+ROOM = pltpu.CompilerParams(vmem_limit_bytes=16 << 20)
 
 
 def parts_of(value):
@@ -48,7 +49,7 @@
 
 def blank_features(samples, offset_ref, weight_ref, *refs):
     tiles, (feature_ref, row_ref) = refs[:-2], refs[-2:]
-    rules, points = weight_ref.shape
+    points, rules = weight_ref.shape
     base = [jnp.concatenate([tile[pl.ds(row, 1), :] for tile in tiles], 1) for row in range(5)]
     rule, cond = base[3], base[4]
     weights = []
@@ -59,8 +60,8 @@
         for number in range(rules):
             here = rule == float(number)
             for axis in range(3):
-                offsets[axis] = jnp.where(here, offset_ref[axis, number, point], offsets[axis])
-            weight = jnp.where(here, weight_ref[number, point], weight)
+                offsets[axis] = jnp.where(here, offset_ref[axis, point, number], offsets[axis])
+            weight = jnp.where(here, weight_ref[point, number], weight)
         weights.append(weight)
         place = [base[axis] + offsets[axis] for axis in range(3)]
         square = place[0] * place[0] + place[1] * place[1] + place[2] * place[2]
@@ -103,9 +104,9 @@
     out_ref[...] = total.astype(out_ref.dtype)
 
 
-def react(row_ref, *refs):
-    arrivals = refs[:-6]
-    own_kernel_ref, other_kernel_ref, current_ref, weighted_ref, own_ref, other_ref = refs[-6:]
+def weigh(scale, row_ref, *refs):
+    arrivals = refs[:-4]
+    kernel_ref, current_ref, weighted_ref, out_ref = refs[-4:]
     count = len(arrivals)
     width = current_ref.shape[1]
     blocks = []
@@ -119,10 +120,15 @@
     current = jnp.concatenate(blocks, 1).astype(F32)
     weighted = (row_ref[pl.ds(2, 1), :] * current).astype(BF16)
     weighted_ref[...] = weighted
-    for kernel_ref, out_ref in ((other_kernel_ref, other_ref), (own_kernel_ref, own_ref)):
-        out_ref[...] = lax.dot_general(
-            kernel_ref[...], weighted, (((1,), (1,)), ((), ())), preferred_element_type=F32
-        ).astype(out_ref.dtype)
+    out_ref[...] = (scale * contract(kernel_ref[...], weighted)).astype(out_ref.dtype)
+
+
+def contract(kernel, weighted):
+    return lax.dot_general(kernel, weighted, (((1,), (1,)), ((), ())), preferred_element_type=F32)
+
+
+def react(scale, weighted_ref, kernel_ref, out_ref):
+    out_ref[...] = scale * contract(kernel_ref[...], weighted_ref[...])
 
 
 def from_behind(value, axis, by):
@@ -166,8 +172,10 @@
         lambda *refs: blank_features(samples, *refs),
         out_shape=(shaped((points, LANES, width), BF16), shaped((8, width), F32)),
         in_specs=[smem, smem] + [vmem] * rows,
+        compiler_params=ROOM,
         name="blank_features",
-    )(quad_offset, quad_weight, *tiles)
+    )(quad_offset.transpose(0, 2, 1), quad_weight.T, *tiles)
+    own, features, table = lax.optimization_barrier((own, features, table))
 
     other = from_behind(own, "core", 1)
     cost = pl.CostEstimate(
@@ -179,31 +187,48 @@
     own_kernel, partial = pl.pallas_call(
         lambda *refs: form(True, step, *refs),
         out_shape=(shaped((held, width), BF16), shaped((samples, width), F32)),
+        compiler_params=ROOM,
         cost_estimate=cost,
         name="form_own",
     )(own, features, table)
     other_kernel, partial = pl.pallas_call(
         lambda *refs: form(False, step, *refs),
         out_shape=(shaped((held, width), BF16), shaped((samples, width), BF16)),
+        compiler_params=ROOM,
         cost_estimate=cost,
         name="form_other",
     )(other, features, table, partial)
 
     arrivals = [partial] + [from_behind(partial, ROWS, by) for by in range(1, rows)]
-    blank_current, _, own_reaction, other_reaction = pl.pallas_call(
-        react,
+    scale = 2.0 / total_blanks
+    react_cost = pl.CostEstimate(
+        flops=2 * held * width * samples,
+        transcendentals=0,
+        bytes_accessed=2 * held * (width + 2 * samples),
+    )
+    blank_current, weighted, reaction = pl.pallas_call(
+        lambda *refs: weigh(scale, *refs),
         out_shape=(
             shaped((samples, blanks), BF16),
             shaped((samples, width), BF16),
-            shaped((held, samples), F32),
             shaped((held, samples), BF16),
         ),
+        compiler_params=ROOM,
+        cost_estimate=react_cost,
+        name="weigh",
+    )(table, *arrivals, other_kernel)
+    crossed = from_behind(reaction, "core", 1)
+    reaction = pl.pallas_call(
+        lambda *refs: react(scale, *refs),
+        out_shape=shaped((held, samples), F32),
+        compiler_params=ROOM,
+        cost_estimate=react_cost,
         name="react",
-    )(table, *arrivals, own_kernel, other_kernel)
-    reaction = own_reaction + from_behind(other_reaction, "core", 1).astype(F32)
+    )(weighted, own_kernel)
+    reaction = reaction + crossed.astype(F32)
     pieces = reaction.astype(BF16).reshape(cols, coils, samples)
     arrived = lax.all_to_all(pieces, COLS, 0, 0, tiled=True)
-    summed = arrived.astype(F32).sum(axis=0) * (2.0 / total_blanks)
+    summed = arrived.astype(F32).sum(axis=0)
     return (blank_current, summed.T)
 
 

time: 79.2 us -> 63.9 us (0.81)
  blocking collectives: 30.1 us -> 15.8 us
  starting transfers between devices: 16.8 us -> 28.3 us
  Pallas kernels: 14.4 us -> 6.78 us
  local copies, waits for them, and re-layouts: 5.69 us -> 2.49 us
  other arithmetic: 1.85 us -> 0.76 us
    all_to_all x1 -> x0, blocking collectives: 18.1 us -> none  [per_device(): own = lax.all_to_all(payload, COLS, 0, 0, tiled=True).reshape(held, LANES)]
    all_to_all x0 -> x1, starting transfers between devices: none -> 9.22 us  [per_device(): own = lax.all_to_all(payload, COLS, 0, 0, tiled=True).reshape(held, LANES)]
    all_to_all x1, blocking collectives: 12 us -> 15.8 us  [per_device(): arrived = lax.all_to_all(pieces, COLS, 0, 0, tiled=True)]
    unnamed x20 -> x8, local copies, waits for them, and re-layouts: 5.69 us -> 2.49 us
    pallas_call x1 -> x2, Pallas kernels: 3.62 us -> 1.2 us  [the longest x1 0.72 us: per_device(): pl.pallas_call(lambda *refs: weigh(scale, *refs), out_shape=(shaped((samp...]
    ppermute x8, starting transfers between devices: 16.8 us -> 19.1 us  [from_behind(): lax.ppermute(value, axis, [(i, (i + by) % size) for i in range(size)])]
    pallas_call x1, Pallas kernels: 3.62 us -> 1.57 us  [per_device(): pl.pallas_call(lambda *refs: form(False, step, *refs), out_shape=(shaped(...]
    pallas_call x1, Pallas kernels: 3.61 us -> 1.58 us  [per_device(): pl.pallas_call(lambda *refs: form(True, step, *refs), out_shape=(shaped((...]
  transfers between devices with their start and end apart: 8 -> 9, of which waited for: 4 -> 4; matrix products, arithmetic and copies ran while one was open for 3% -> 0% of each run, Pallas kernels for 7% -> 4%
where the time goes in v2:
time: 63.9 us; the launch traced here: 63.6 us
  starting transfers between devices  28.3 us (44%)
  blocking collectives  15.8 us (25%)
  waiting for transfers between devices  8.7 us (14%)
  Pallas kernels  6.78 us (11%)
  local copies, waits for them, and re-layouts  2.49 us (4%)
  other arithmetic  0.76 us (1%)
  between operations  0.72 us (1%)
    ppermute x8, starting transfers between devices, from_behind(): lax.ppermute(value, axis, [(i, (i + by) % size) for i in range(size)])  19.1 us
    all_to_all x1, blocking collectives, per_device(): arrived = lax.all_to_all(pieces, COLS, 0, 0, tiled=True)  15.8 us
    all_to_all x1, starting transfers between devices, per_device(): own = lax.all_to_all(payload, COLS, 0, 0, tiled=True).reshape(held, LANES)  9.22 us
    ppermute x8, waiting for transfers between devices, from_behind(): lax.ppermute(value, axis, [(i, (i + by) % size) for i in range(size)])  8.69 us
    unnamed x8, local copies, waits for them, and re-layouts  2.49 us
    pallas_call x1, Pallas kernels, per_device(): pl.pallas_call(prepare, out_shape=(shaped((cols, coils, LANES), BF16), sh...  1.65 us
    pallas_call x1, Pallas kernels, per_device(): pl.pallas_call(lambda *refs: form(True, step, *refs), out_shape=(shaped((...  1.58 us
    pallas_call x1, Pallas kernels, per_device(): pl.pallas_call(lambda *refs: form(False, step, *refs), out_shape=(shaped(...  1.57 us
  transfers between devices with their start and end apart: 9, of which 4 were waited for; matrix products, arithmetic and copies ran while one was open for 0% of the time, Pallas kernels for 4%

profile of v2, /device:TPU:1, one launch (start us, length us, event | category | flops | bytes accessed | tf_op | source)
XLA Modules:
  0.0 63.6 jit_solution(3563798678377624243)
XLA Ops:
  0.6 1.6 %prepare.1 = (bf16[32,40,128]{2,1,0:T(8,128)(2,1)}, f32[8,128]{1,0:T(8,128)}) custom-call(f32[3,40]{1,0:T(4,128)} %pos_ref.1, f32[1,40]{1,0:T(1,128)} %bitcast.16, bf16[40,64]{1,0:T(8,128)(2,1)} %bitcast.15, f32[3,128]{1,0:T(4,128)} %blank_ref.1, s32[1,128]{1,0:T(1,128)} %bitcast.17, f32[1,128]{1,0:T(1,128)} %bitcast.18), custom_call_target="tpu_custom_call" | custom-call | tf_op jit(solution)/shard_map/prepare/pallas_call | solution.py:155
  2.3 9.2 %all-to-all-start = ((bf16[32,40,128]{2,1,0:T(8,128)(2,1)}), bf16[32,40,128]{2,1,0:T(8,128)(2,1)S(1)}, u32[]{:S(2)}, u32[]{:S(2)}) async-start(bf16[32,40,128]{2,1,0:T(8,128)(2,1)} %get-tuple-element.16), calls=%async_computation | async-start | bytes 655360 | tf_op jit(solution)/shard_map/all_to_all | solution.py:167
  11.5 5.2 %collective-permute-start.2 = (f32[8,128]{1,0:T(8,128)}, f32[8,128]{1,0:T(8,128)S(1)}, u32[]{:S(2)}, u32[]{:S(2)}) collective-permute-start(f32[8,128]{1,0:T(8,128)} %get-tuple-element.17.refs_2_), channel_id=1, source_target_pairs={{0,192},{64,0},{128,64},{192,128},{1,193},{65,1},{129,65},{193,129... | collective-permute-start | bytes 12296 | tf_op jit(solution)/shard_map/ppermute | solution.py:136
  16.7 1.2 %collective-permute-start.1 = (f32[8,128]{1,0:T(8,128)}, f32[8,128]{1,0:T(8,128)S(1)}, u32[]{:S(2)}, u32[]{:S(2)}) collective-permute-start(f32[8,128]{1,0:T(8,128)} %get-tuple-element.17.refs_2_), channel_id=1, source_target_pairs={{0,128},{64,192},{128,0},{192,64},{1,129},{65,193},{129,1},{193,65... | collective-permute-start | bytes 12296 | tf_op jit(solution)/shard_map/ppermute | solution.py:136
  17.9 2.1 %collective-permute-start = (f32[8,128]{1,0:T(8,128)}, f32[8,128]{1,0:T(8,128)S(1)}, u32[]{:S(2)}, u32[]{:S(2)}) collective-permute-start(f32[8,128]{1,0:T(8,128)} %get-tuple-element.17.refs_2_), channel_id=1, source_target_pairs={{0,64},{64,128},{128,192},{192,0},{1,65},{65,129},{129,193},{193,1... | collective-permute-start | bytes 12296 | tf_op jit(solution)/shard_map/ppermute | solution.py:136
  20.0 3.3 %collective-permute-done.1.refs_4_ = f32[8,128]{1,0:T(8,128)S(1)} collective-permute-done((f32[8,128]{1,0:T(8,128)}, f32[8,128]{1,0:T(8,128)S(1)}, u32[]{:S(2)}, u32[]{:S(2)}) %collective-permute-start.1) | collective-permute-done | bytes 4128 | tf_op jit(solution)/shard_map/ppermute | solution.py:136
  23.3 0.7 %copy-done = f32[8,128]{1,0:T(8,128)S(1)} copy-done((f32[8,128]{1,0:T(8,128)S(1)}, f32[8,128]{1,0:T(8,128)}, u32[]{:S(2)}) %copy-start) | copy-done | bytes 4120
  24.0 0.7 %copy-done.1 = f32[3,8,2]{1,2,0:T(2,128)S(1)} copy-done((f32[3,8,2]{1,2,0:T(2,128)S(1)}, f32[3,8,2]{1,2,0:T(2,128)}, u32[]{:S(2)}) %copy-start.1) | copy-done | bytes 216
  24.7 0.7 %copy-done.2 = f32[8,2]{0,1:T(2,128)S(1)} copy-done((f32[8,2]{0,1:T(2,128)S(1)}, f32[8,2]{0,1:T(2,128)}, u32[]{:S(2)}) %copy-start.2) | copy-done | bytes 88
  25.3 0.8 %blank_features.1 = (bf16[2,128,512]{2,1,0:T(8,128)(2,1)S(1)}, f32[8,512]{1,0:T(8,128)S(1)}) custom-call(f32[3,2,8]{2,1,0:T(2,128)S(1)} %bitcast.11, f32[2,8]{1,0:T(2,128)S(1)} %bitcast.12, f32[8,128]{1,0:T(8,128)S(1)} %copy-done, f32[8,128]{1,0:T(8,128)S(1)} %collective-permute-done.refs_3_, f32[8,128]{1,0:T(8,128)S(1)} %collective-permute-done.1.refs_4_, ...), custom_call_target="tpu_custom_call" | custom-call | tf_op jit(solution)/shard_map/blank_features/pallas_call | solution.py:171
  26.1 2.5 %collective-permute-start.3 = (bf16[1280,128]{1,0:T(8,128)(2,1)S(1)}, bf16[1280,128]{1,0:T(8,128)(2,1)S(1)}, u32[]{:S(2)}, u32[]{:S(2)}) collective-permute-start(bf16[1280,128]{1,0:T(8,128)(2,1)S(1)} %bitcast.9), channel_id=1, source_target_pairs={{0,1},{1,0},{2,3},{3,2},{4,5},{5,4},{6,7},{7,6},{8,9},{9,8},{10,11... | collective-permute-start | bytes 983048 | tf_op jit(solution)/shard_map/ppermute | solution.py:136
  28.6 1.6 %form_own.1 = (bf16[1280,512]{1,0:T(8,128)(2,1)S(1)}, f32[64,512]{1,0:T(8,128)S(1)}) custom-call(bf16[1280,128]{1,0:T(8,128)(2,1)S(1)} %bitcast.10, bf16[2,128,512]{2,1,0:T(8,128)(2,1)S(1)} %get-tuple-element.22.refs_1_, f32[8,512]{1,0:T(8,128)S(1)} %get-tuple-element.20.refs_2_.refs_0_), custom_call_target="tpu_custom_call" | custom-call | flops 503316480 | bytes 1638400 | tf_op jit(solution)/shard_map/form_own/pallas_call | solution.py:187
  30.2 1.6 %form_other.1 = (bf16[1280,512]{1,0:T(8,128)(2,1)S(1)}, bf16[64,512]{1,0:T(8,128)(2,1)S(1)}) custom-call(bf16[1280,128]{1,0:T(8,128)(2,1)S(1)} %collective-permute-done.3.refs_0_, bf16[2,128,512]{2,1,0:T(8,128)(2,1)S(1)} %get-tuple-element.22.refs_1_, f32[8,512]{1,0:T(8,128)S(1)} %get-tuple-element.20.refs_2_.refs_0_, f32[64,512]{1,0:T(8,128)S(1)} %get-tuple-element.23.refs_3_), custom_call_target="tpu_custom_call" | custom-call | flops 503316480 | bytes 1638400 | tf_op jit(solution)/shard_map/form_other/pallas_call | solution.py:194
  31.8 1.3 %collective-permute-start.6 = (bf16[64,512]{1,0:T(8,128)(2,1)S(1)}, bf16[64,512]{1,0:T(8,128)(2,1)S(1)}, u32[]{:S(2)}, u32[]{:S(2)}) collective-permute-start(bf16[64,512]{1,0:T(8,128)(2,1)S(1)} %get-tuple-element.24.refs_1_), channel_id=1, source_target_pairs={{0,192},{64,0},{128,64},{192,128},{1,193},{65,1},{129,65},{193,129... | collective-permute-start | bytes 196616 | tf_op jit(solution)/shard_map/ppermute | solution.py:136
  33.1 2.8 %collective-permute-start.5 = (bf16[64,512]{1,0:T(8,128)(2,1)S(1)}, bf16[64,512]{1,0:T(8,128)(2,1)S(1)}, u32[]{:S(2)}, u32[]{:S(2)}) collective-permute-start(bf16[64,512]{1,0:T(8,128)(2,1)S(1)} %get-tuple-element.24.refs_1_), channel_id=1, source_target_pairs={{0,128},{64,192},{128,0},{192,64},{1,129},{65,193},{129,1},{193,65... | collective-permute-start | bytes 196616 | tf_op jit(solution)/shard_map/ppermute | solution.py:136
  35.8 2.3 %collective-permute-start.4 = (bf16[64,512]{1,0:T(8,128)(2,1)S(1)}, bf16[64,512]{1,0:T(8,128)(2,1)S(1)}, u32[]{:S(2)}, u32[]{:S(2)}) collective-permute-start(bf16[64,512]{1,0:T(8,128)(2,1)S(1)} %get-tuple-element.24.refs_1_), channel_id=1, source_target_pairs={{0,64},{64,128},{128,192},{192,0},{1,65},{65,129},{129,193},{193,1... | collective-permute-start | bytes 196616 | tf_op jit(solution)/shard_map/ppermute | solution.py:136
  38.1 2.1 %collective-permute-done.5.refs_3_ = bf16[64,512]{1,0:T(8,128)(2,1)S(1)} collective-permute-done((bf16[64,512]{1,0:T(8,128)(2,1)S(1)}, bf16[64,512]{1,0:T(8,128)(2,1)S(1)}, u32[]{:S(2)}, u32[]{:S(2)}) %collective-permute-start.5) | collective-permute-done | bytes 65568 | tf_op jit(solution)/shard_map/ppermute | solution.py:136
  40.2 2.5 %collective-permute-done.4.refs_2_ = bf16[64,512]{1,0:T(8,128)(2,1)S(1)} collective-permute-done((bf16[64,512]{1,0:T(8,128)(2,1)S(1)}, bf16[64,512]{1,0:T(8,128)(2,1)S(1)}, u32[]{:S(2)}, u32[]{:S(2)}) %collective-permute-start.4) | collective-permute-done | bytes 65568 | tf_op jit(solution)/shard_map/ppermute | solution.py:136
  42.7 0.7 %weigh.1 = (bf16[64,128]{1,0:T(8,128)(2,1)}, bf16[64,512]{1,0:T(8,128)(2,1)S(1)}, bf16[1280,64]{1,0:T(8,128)(2,1)S(1)}) custom-call(f32[8,512]{1,0:T(8,128)S(1)} %get-tuple-element.20.refs_2_.refs_0_, bf16[64,512]{1,0:T(8,128)(2,1)S(1)} %get-tuple-element.24.refs_1_, bf16[64,512]{1,0:T(8,128)(2,1)S(1)} %collective-permute-done.4.refs_2_, ...), custom_call_target="tpu_custom_call" | custom-call | flops 83886080 | bytes 1638400 | tf_op jit(solution)/shard_map/weigh/pallas_call | solution.py:209
  43.4 1.9 %collective-permute-start.7 = (bf16[1280,64]{1,0:T(8,128)(2,1)S(1)}, bf16[1280,64]{1,0:T(8,128)(2,1)S(1)}, u32[]{:S(2)}, u32[]{:S(2)}) collective-permute-start(bf16[1280,64]{1,0:T(8,128)(2,1)S(1)} %get-tuple-element.29), channel_id=1, source_target_pairs={{0,1},{1,0},{2,3},{3,2},{4,5},{5,4},{6,7},{7,6},{8,9},{9,8},{10,11... | collective-permute-start | bytes 491528 | tf_op jit(solution)/shard_map/ppermute | solution.py:136
  45.3 0.5 react.1
  45.8 0.8 %collective-permute-done.7 = bf16[1280,64]{1,0:T(8,128)(2,1)S(1)} collective-permute-done((bf16[1280,64]{1,0:T(8,128)(2,1)S(1)}, bf16[1280,64]{1,0:T(8,128)(2,1)S(1)}, u32[]{:S(2)}, u32[]{:S(2)}) %collective-permute-start.7) | collective-permute-done | bytes 163872 | tf_op jit(solution)/shard_map/ppermute | solution.py:136
  46.8 15.8 %all_to_all.10 = bf16[32,2,1280]{2,1,0:T(2,128)(2,1)S(1)} all-to-all(bf16[32,2,1280]{2,1,0:T(2,128)(2,1)S(1)} %reshape.12), channel_id=1, replica_groups=mesh['zh'=4,'zl'=2,'xh'=2,'y'=4,'xl'=2,'core'=2] {'zl','xh','y','xl'}, dimensions={0} | all-to-all | bytes 327680 | tf_op jit(solution)/shard_map/all_to_all | solution.py:230
  62.9 0.7 %convert_reduce_fusion = f32[40,64]{1,0:T(8,128)} fusion(bf16[32,40,64]{2,1,0:T(8,128)(2,1)S(1)} %reshape.13), kind=kLoop, calls=%fused_computation | loop fusion | flops 161280 | bytes 174080 | tf_op jit(solution)/shard_map/reduce_sum | solution.py:231
  (11 shorter events, 0.5 us)
Async XLA Ops:
  2.3 23.9 %all-to-all-start = ((bf16[32,40,128]{2,1,0:T(8,128)(2,1)}), bf16[32,40,128]{2,1,0:T(8,128)(2,1)S(1)}, u32[]{:S(2)}, u32[]{:S(2)}) async-start(bf16[32,40,128]{2,1,0:T(8,128)(2,1)} %get-tuple-element.16), calls=%async_computation | async-start | bytes 655360 | tf_op jit(solution)/shard_map/all_to_all | solution.py:167
  11.5 8.5 %collective-permute-start.2 = (f32[8,128]{1,0:T(8,128)}, f32[8,128]{1,0:T(8,128)S(1)}, u32[]{:S(2)}, u32[]{:S(2)}) collective-permute-start(f32[8,128]{1,0:T(8,128)} %get-tuple-element.17.refs_2_), channel_id=1, source_target_pairs={{0,192},{64,0},{128,64},{192,128},{1,193},{65,1},{129,65},{193,129... | collective-permute-start | bytes 12296 | tf_op jit(solution)/shard_map/ppermute | solution.py:136
  16.7 6.6 %collective-permute-start.1 = (f32[8,128]{1,0:T(8,128)}, f32[8,128]{1,0:T(8,128)S(1)}, u32[]{:S(2)}, u32[]{:S(2)}) collective-permute-start(f32[8,128]{1,0:T(8,128)} %get-tuple-element.17.refs_2_), channel_id=1, source_target_pairs={{0,128},{64,192},{128,0},{192,64},{1,129},{65,193},{129,1},{193,65... | collective-permute-start | bytes 12296 | tf_op jit(solution)/shard_map/ppermute | solution.py:136
  17.9 5.4 %collective-permute-start = (f32[8,128]{1,0:T(8,128)}, f32[8,128]{1,0:T(8,128)S(1)}, u32[]{:S(2)}, u32[]{:S(2)}) collective-permute-start(f32[8,128]{1,0:T(8,128)} %get-tuple-element.17.refs_2_), channel_id=1, source_target_pairs={{0,64},{64,128},{128,192},{192,0},{1,65},{65,129},{129,193},{193,1... | collective-permute-start | bytes 12296 | tf_op jit(solution)/shard_map/ppermute | solution.py:136
  23.3 0.7 %copy-start = (f32[8,128]{1,0:T(8,128)S(1)}, f32[8,128]{1,0:T(8,128)}, u32[]{:S(2)}) copy-start(f32[8,128]{1,0:T(8,128)} %get-tuple-element.17.refs_2_) | copy-start | bytes 12292
  24.0 0.7 %copy-start.1 = (f32[3,8,2]{1,2,0:T(2,128)S(1)}, f32[3,8,2]{1,2,0:T(2,128)}, u32[]{:S(2)}) copy-start(f32[3,8,2]{1,2,0:T(2,128)} %param.14) | copy-start | bytes 580
  24.7 0.7 %copy-start.2 = (f32[8,2]{0,1:T(2,128)S(1)}, f32[8,2]{0,1:T(2,128)}, u32[]{:S(2)}) copy-start(f32[8,2]{0,1:T(2,128)} %param.15) | copy-start | bytes 196
  26.1 4.1 %collective-permute-start.3 = (bf16[1280,128]{1,0:T(8,128)(2,1)S(1)}, bf16[1280,128]{1,0:T(8,128)(2,1)S(1)}, u32[]{:S(2)}, u32[]{:S(2)}) collective-permute-start(bf16[1280,128]{1,0:T(8,128)(2,1)S(1)} %bitcast.9), channel_id=1, source_target_pairs={{0,1},{1,0},{2,3},{3,2},{4,5},{5,4},{6,7},{7,6},{8,9},{9,8},{10,11... | collective-permute-start | bytes 983048 | tf_op jit(solution)/shard_map/ppermute | solution.py:136
  31.8 6.3 %collective-permute-start.6 = (bf16[64,512]{1,0:T(8,128)(2,1)S(1)}, bf16[64,512]{1,0:T(8,128)(2,1)S(1)}, u32[]{:S(2)}, u32[]{:S(2)}) collective-permute-start(bf16[64,512]{1,0:T(8,128)(2,1)S(1)} %get-tuple-element.24.refs_1_), channel_id=1, source_target_pairs={{0,192},{64,0},{128,64},{192,128},{1,193},{65,1},{129,65},{193,129... | collective-permute-start | bytes 196616 | tf_op jit(solution)/shard_map/ppermute | solution.py:136
  33.1 7.1 %collective-permute-start.5 = (bf16[64,512]{1,0:T(8,128)(2,1)S(1)}, bf16[64,512]{1,0:T(8,128)(2,1)S(1)}, u32[]{:S(2)}, u32[]{:S(2)}) collective-permute-start(bf16[64,512]{1,0:T(8,128)(2,1)S(1)} %get-tuple-element.24.refs_1_), channel_id=1, source_target_pairs={{0,128},{64,192},{128,0},{192,64},{1,129},{65,193},{129,1},{193,65... | collective-permute-start | bytes 196616 | tf_op jit(solution)/shard_map/ppermute | solution.py:136
  35.8 6.9 %collective-permute-start.4 = (bf16[64,512]{1,0:T(8,128)(2,1)S(1)}, bf16[64,512]{1,0:T(8,128)(2,1)S(1)}, u32[]{:S(2)}, u32[]{:S(2)}) collective-permute-start(bf16[64,512]{1,0:T(8,128)(2,1)S(1)} %get-tuple-element.24.refs_1_), channel_id=1, source_target_pairs={{0,64},{64,128},{128,192},{192,0},{1,65},{65,129},{129,193},{193,1... | collective-permute-start | bytes 196616 | tf_op jit(solution)/shard_map/ppermute | solution.py:136
  43.4 3.1 %collective-permute-start.7 = (bf16[1280,64]{1,0:T(8,128)(2,1)S(1)}, bf16[1280,64]{1,0:T(8,128)(2,1)S(1)}, u32[]{:S(2)}, u32[]{:S(2)}) collective-permute-start(bf16[1280,64]{1,0:T(8,128)(2,1)S(1)} %get-tuple-element.29), channel_id=1, source_target_pairs={{0,1},{1,0},{2,3},{3,2},{4,5},{5,4},{6,7},{7,6},{8,9},{9,8},{10,11... | collective-permute-start | bytes 491528 | tf_op jit(solution)/shard_map/ppermute | solution.py:136

commit v3 on v2

v3 whole, which is shorter than its diff:
```python
import jax
import jax.numpy as jnp
from jax import lax
from jax.experimental import pallas as pl
from jax.experimental.pallas import tpu as pltpu
from jax.sharding import Mesh
from jax.sharding import PartitionSpec as P

AXES = ("zh", "zl", "xh", "y", "xl", "core")
SIZES = (4, 2, 2, 4, 2, 2)
ROWS = ("y",)
COLS = ("zh", "zl", "xh", "xl")
LANES = 128
SUBLANES = 8
SLOT = 32
BF16 = jnp.bfloat16
F32 = jnp.float32
ROOM = pltpu.CompilerParams(vmem_limit_bytes=16 << 20)


def parts_of(value):
    high = value.astype(BF16).astype(F32)
    rest = value - high
    mid = rest.astype(BF16).astype(F32)
    low = (rest - mid).astype(BF16).astype(F32)
    return [high, mid, low]


def prepare(
    offset_ref,
    weight_ref,
    pos_ref,
    radius_ref,
    current_ref,
    blank_ref,
    rule_ref,
    cond_ref,
    payload_ref,
    tile_ref,
):
    coils, samples = current_ref.shape
    groups = coils // SUBLANES
    x, y, z = (pos_ref[pl.ds(axis, 1), :] for axis in range(3))
    radius = radius_ref[...]
    square = x * x + y * y + z * z + radius * radius
    rows = [part for value in (x, y, z, square) for part in parts_of(value)]
    count = len(rows)
    rows.append(jnp.zeros((16 - count, coils), F32))
    columns = jnp.concatenate(rows, 0).T
    geometry = [columns[SUBLANES * g : SUBLANES * (g + 1), :count] for g in range(groups)]
    geometry.append(jnp.zeros((SUBLANES, samples - count * groups), F32))
    geometry = jnp.concatenate(geometry, 1)
    current = current_ref[...].astype(F32)
    half = payload_ref.shape[1]
    left = current[:half]
    right = jnp.concatenate([current[half:], geometry], 0)
    payload = jnp.concatenate([left, right], 1).astype(BF16)
    for copy in range(payload_ref.shape[0]):
        payload_ref[copy] = payload
    points, rules = weight_ref.shape
    rule = rule_ref[...]
    rows = []
    for point in range(points):
        offsets = [jnp.zeros(rule.shape, F32) for _ in range(3)]
        weight = jnp.zeros(rule.shape, F32)
        for number in range(rules):
            here = rule == number
            for axis in range(3):
                offsets[axis] = jnp.where(here, offset_ref[axis, point, number], offsets[axis])
            weight = jnp.where(here, weight_ref[point, number], weight)
        rows += [blank_ref[pl.ds(axis, 1), :] + offsets[axis] for axis in range(3)]
        rows.append(weight)
    rows.append(cond_ref[...])
    rows.append(jnp.zeros((tile_ref.shape[0] - len(rows), rule.shape[1]), F32))
    tile_ref[...] = jnp.concatenate(rows, 0)


def blank_features(points, *refs):
    tiles, (feature_ref, row_ref) = refs[:-2], refs[-2:]
    whole = jnp.concatenate([tile[...] for tile in tiles], 1)
    width = whole.shape[1]
    for point in range(points):
        place = [whole[4 * point + axis : 4 * point + axis + 1] for axis in range(3)]
        square = place[0] * place[0] + place[1] * place[1] + place[2] * place[2]
        parts = [parts_of(value) for value in place]
        rows = []
        for level in range(3):
            for axis in range(3):
                rows += [-2.0 * parts[axis][level]] * 3
            rows += [jnp.full((1, width), 1.0 if level == 0 else 0.0, F32)] * 3
            rows.append(jnp.zeros((SLOT - 12, width), F32))
        rows += parts_of(square)
        rows.append(jnp.zeros((SLOT - 3, width), F32))
        feature_ref[point] = jnp.concatenate(rows, 0).astype(BF16)
    row_ref[...] = whole


def group_rows(payload, group):
    at = SUBLANES * (group % 3)
    rows = payload[:, at : at + SUBLANES, :]
    return rows.reshape(rows.shape[0] * SUBLANES, LANES)


def coil_features(geometry, group):
    lane = lax.broadcasted_iota(jnp.int32, geometry.shape, 1)
    at = LANES // 2 + 12 * group
    copies = [pltpu.roll(geometry, (SLOT * slot - at) % LANES, 1) for slot in range(3)]
    out = jnp.where(lane < SLOT, copies[0], jnp.where(lane < 2 * SLOT, copies[1], copies[2]))
    return jnp.where(lane < 3 * SLOT, out, 1.0).astype(BF16)


def form(first, payload_ref, feature_ref, row_ref, *refs):
    if first:
        kernel_ref, out_ref = refs
    else:
        before_ref, kernel_ref, out_ref = refs
    samples = out_ref.shape[0]
    points = feature_ref.shape[0]
    groups = kernel_ref.shape[0]
    payload = payload_ref[...]
    geometry = group_rows(payload, 2).astype(F32)
    total = None if first else before_ref[...]
    for group in range(groups):
        coils = coil_features(geometry, group)
        block = None
        for point in range(points):
            squared = jnp.dot(coils, feature_ref[point], preferred_element_type=F32)
            term = row_ref[pl.ds(4 * point + 3, 1), :] * lax.rsqrt(squared)
            block = term if block is None else block + term
        block = block.astype(BF16)
        kernel_ref[group] = block
        product = lax.dot_general(
            group_rows(payload, group), block, (((0,), (0,)), ((), ())), preferred_element_type=F32
        )
        product = product[:samples] if group < 3 else product[samples:]
        total = product if total is None else total + product
    out_ref[...] = total.astype(out_ref.dtype)


def contract(kernel_ref, weighted):
    groups = kernel_ref.shape[0]
    twice = jnp.concatenate([weighted, weighted], 0)
    whole = [
        lax.dot_general(
            kernel_ref[group], twice, (((1,), (1,)), ((), ())), preferred_element_type=F32
        )
        for group in range(groups)
    ]
    lane = lax.broadcasted_iota(jnp.int32, whole[0].shape, 1)
    rows = []
    for group in range(3):
        other = whole[group + 3] if group + 3 < groups else jnp.zeros_like(whole[group])
        both = jnp.where(lane < LANES // 2, whole[group], other)
        rows.append(both.reshape(both.shape[0] // SUBLANES, SUBLANES, LANES))
    return jnp.concatenate(rows, 1)


def weigh(scale, row_ref, *refs):
    arrivals = refs[:-4]
    kernel_ref, current_ref, weighted_ref, out_ref = refs[-4:]
    count = len(arrivals)
    width = current_ref.shape[1]
    blocks = []
    for block in range(count):
        total = None
        for flip in range(count):
            piece = arrivals[flip][:, pl.ds((block ^ flip) * width, width)].astype(F32)
            total = piece if total is None else total + piece
        blocks.append(total.astype(BF16))
    current_ref[...] = blocks[0]
    current = jnp.concatenate(blocks, 1).astype(F32)
    weighted = (row_ref[pl.ds(8, 1), :] * current).astype(BF16)
    weighted_ref[...] = weighted
    out_ref[...] = (scale * contract(kernel_ref, weighted)).astype(out_ref.dtype)


def react(scale, weighted_ref, kernel_ref, out_ref):
    out_ref[...] = scale * contract(kernel_ref, weighted_ref[...])


def finish(arrived_ref, out_ref):
    total = jnp.sum(arrived_ref[...].astype(F32), 0)
    half, samples = total.shape[0], out_ref.shape[1]
    out_ref[...] = jnp.concatenate(
        [total[:, :samples], total[: out_ref.shape[0] - half, samples:]], 0
    )


def from_partner(value, axis, flip):
    size = lax.axis_size(axis)
    return lax.ppermute(value, axis, [(i, i ^ flip) for i in range(size)])


def shaped(shape, dtype):
    return jax.ShapeDtypeStruct(shape, dtype)


def per_device(
    coil_pos, coil_radius, coil_current, blank_pos, blank_rule, blank_cond, quad_offset, quad_weight
):
    samples, coils = coil_current.shape
    blanks = blank_pos.shape[1]
    total_blanks = blanks * lax.axis_size(AXES)
    cols = lax.axis_size(COLS)
    rows = lax.axis_size(ROWS)
    points = quad_weight.shape[1]
    width = rows * blanks
    packed = (cols, 24, LANES)
    kernel_shape = shaped((coils // SUBLANES, cols * SUBLANES, width), BF16)
    smem = pl.BlockSpec(memory_space=pltpu.SMEM)
    vmem = pl.BlockSpec(memory_space=pltpu.VMEM)

    payload, tile = pl.pallas_call(
        prepare,
        out_shape=(shaped(packed, BF16), shaped((16, blanks), F32)),
        in_specs=[smem, smem] + [vmem] * 6,
        name="prepare",
    )(
        quad_offset.transpose(0, 2, 1),
        quad_weight.T,
        coil_pos,
        coil_radius[None, :],
        coil_current.T,
        blank_pos,
        blank_rule[None, :],
        blank_cond[None, :],
    )
    own = lax.all_to_all(payload, COLS, 0, 0, tiled=True)
    tiles = [tile] + [from_partner(tile, ROWS, flip) for flip in range(1, rows)]
    features, table = pl.pallas_call(
        lambda *refs: blank_features(points, *refs),
        out_shape=(shaped((points, LANES, width), BF16), shaped((16, width), F32)),
        compiler_params=ROOM,
        name="blank_features",
    )(*tiles)
    own, features, table = lax.optimization_barrier((own, features, table))
    other = from_partner(own, "core", 1)
    held = cols * coils
    cost = pl.CostEstimate(
        flops=2 * held * width * LANES * (points + 1),
        transcendentals=points * held * width,
        bytes_accessed=2 * held * (width + LANES),
    )
    own_kernel, partial = pl.pallas_call(
        lambda *refs: form(True, *refs),
        out_shape=(kernel_shape, shaped((samples, width), F32)),
        compiler_params=ROOM,
        cost_estimate=cost,
        name="form_own",
    )(own, features, table)
    other_kernel, partial = pl.pallas_call(
        lambda *refs: form(False, *refs),
        out_shape=(kernel_shape, shaped((samples, width), BF16)),
        compiler_params=ROOM,
        cost_estimate=cost,
        name="form_other",
    )(other, features, table, partial)

    arrivals = [partial] + [from_partner(partial, ROWS, flip) for flip in range(1, rows)]
    scale = 2.0 / total_blanks
    react_cost = pl.CostEstimate(
        flops=2 * held * width * samples,
        transcendentals=0,
        bytes_accessed=2 * held * (width + 2 * samples),
    )
    blank_current, weighted, reaction = pl.pallas_call(
        lambda *refs: weigh(scale, *refs),
        out_shape=(
            shaped((samples, blanks), BF16),
            shaped((samples, width), BF16),
            shaped(packed, BF16),
        ),
        compiler_params=ROOM,
        cost_estimate=react_cost,
        name="weigh",
    )(table, *arrivals, other_kernel)
    crossed = from_partner(reaction, "core", 1)
    reaction = pl.pallas_call(
        lambda *refs: react(scale, *refs),
        out_shape=shaped(packed, F32),
        compiler_params=ROOM,
        cost_estimate=react_cost,
        name="react",
    )(weighted, own_kernel)
    pieces = (reaction + crossed.astype(F32)).astype(BF16)
    arrived = lax.all_to_all(pieces, COLS, 0, 0, tiled=True)
    coil_reaction = pl.pallas_call(
        finish,
        out_shape=shaped((coils, samples), F32),
        compiler_params=ROOM,
        name="finish",
    )(arrived)
    return (blank_current, coil_reaction.T)


def solution(mesh):
    split = Mesh(mesh.devices.reshape(SIZES), AXES)
    whole = P(None, AXES)
    return jax.shard_map(
        per_device,
        mesh=split,
        in_specs=(whole, P(AXES), whole, whole, P(AXES), P(AXES), P(), P()),
        out_specs=(whole, whole),
        check_vma=False,
    )
```

time: 63.9 us -> 59 us (0.923)
  starting transfers between devices: 28.3 us -> 23.7 us
  local copies, waits for them, and re-layouts: 2.49 us -> 0.7 us
  waiting for transfers between devices: 8.7 us -> 10.2 us
  Pallas kernels: 6.78 us -> 7.7 us
  other arithmetic: 0.76 us -> 0.04 us
    ppermute x8, starting transfers between devices: 19.1 us -> 11.8 us  [from_partner(): return lax.ppermute(value, axis, [(i, i ^ flip) for i in range(size)])]
    all_to_all x1, starting transfers between devices: 9.22 us -> 11.9 us  [per_device(): own = lax.all_to_all(payload, COLS, 0, 0, tiled=True)]
    all_to_all x1, waiting for transfers between devices: 0.01 us -> 1.8 us  [per_device(): own = lax.all_to_all(payload, COLS, 0, 0, tiled=True)]
    unnamed x8 -> x2, local copies, waits for them, and re-layouts: 2.49 us -> 0.7 us
    reduce_sum x1 -> x0, other arithmetic: 0.69 us -> none  [per_device(): summed = arrived.astype(F32).sum(axis=0)]
    pallas_call x5 -> x6, Pallas kernels: 6.06 us -> 6.67 us  [the longest x1 1.82 us: per_device(): pl.pallas_call(prepare, out_shape=(shaped(packed, BF16), shaped((16, blan...]
  transfers between devices with their start and end apart: 9 -> 9, of which waited for: 4 -> 6; matrix products, arithmetic and copies ran while one was open for 0% -> 0% of each run, Pallas kernels for 4% -> 4%
where the time goes in v3:
time: 59 us; the launch traced here: 58.7 us
  starting transfers between devices  23.7 us (40%)
  blocking collectives  15.8 us (27%)
  waiting for transfers between devices  10.2 us (17%)
  Pallas kernels  7.7 us (13%)
  local copies, waits for them, and re-layouts  0.7 us (1%)
  between operations  0.69 us (1%)
    all_to_all x1, blocking collectives, per_device(): arrived = lax.all_to_all(pieces, COLS, 0, 0, tiled=True)  15.8 us
    all_to_all x1, starting transfers between devices, per_device(): own = lax.all_to_all(payload, COLS, 0, 0, tiled=True)  11.9 us
    ppermute x8, starting transfers between devices, from_partner(): return lax.ppermute(value, axis, [(i, i ^ flip) for i in range(size)])  11.8 us
    ppermute x8, waiting for transfers between devices, from_partner(): return lax.ppermute(value, axis, [(i, i ^ flip) for i in range(size)])  8.35 us
    pallas_call x1, Pallas kernels, per_device(): pl.pallas_call(prepare, out_shape=(shaped(packed, BF16), shaped((16, blan...  1.82 us
    all_to_all x1, waiting for transfers between devices, per_device(): own = lax.all_to_all(payload, COLS, 0, 0, tiled=True)  1.8 us
    pallas_call x1, Pallas kernels, per_device(): pl.pallas_call(lambda *refs: form(False, *refs), out_shape=(kernel_shape,...  1.78 us
    pallas_call x1, Pallas kernels, per_device(): pl.pallas_call(lambda *refs: form(True, *refs), out_shape=(kernel_shape,...  1.78 us
  transfers between devices with their start and end apart: 9, of which 6 were waited for; matrix products, arithmetic and copies ran while one was open for 0% of the time, Pallas kernels for 4%

profile of v3, /device:TPU:1, one launch (start us, length us, event | category | flops | bytes accessed | tf_op | source)
XLA Modules:
  0.0 58.7 jit_solution(15145224037248051114)
XLA Ops:
  0.6 1.8 %prepare.1 = (bf16[32,24,128]{2,1,0:T(8,128)(2,1)}, f32[16,128]{1,0:T(8,128)}) custom-call(f32[3,2,8]{2,1,0:T(2,128)} %bitcast.9, f32[2,8]{1,0:T(2,128)} %bitcast.10, f32[3,40]{1,0:T(4,128)} %pos_ref.1, f32[1,40]{1,0:T(1,128)} %bitcast.11, bf16[40,64]{1,0:T(8,128)(2,1)} %bitcast.8, f32[3,128]{1,0:T(4,128)} %blank_ref.1, s32[1,128]{1,0:T(1,128)} %bitcast.12, ...), custom_call_target="tpu_custom_call" | custom-call | tf_op jit(solution)/shard_map/prepare/pallas_call | solution.py:213
  2.5 11.9 %all-to-all-start = ((bf16[32,24,128]{2,1,0:T(8,128)(2,1)}), bf16[32,24,128]{2,1,0:T(8,128)(2,1)S(1)}, u32[]{:S(2)}, u32[]{:S(2)}) async-start(bf16[32,24,128]{2,1,0:T(8,128)(2,1)} %get-tuple-element.16), calls=%async_computation | async-start | bytes 393216 | tf_op jit(solution)/shard_map/all_to_all | solution.py:228
  14.3 2.8 %collective-permute-start.2 = (f32[16,128]{1,0:T(8,128)}, f32[16,128]{1,0:T(8,128)S(1)}, u32[]{:S(2)}, u32[]{:S(2)}) collective-permute-start(f32[16,128]{1,0:T(8,128)} %get-tuple-element.17.refs_0_), channel_id=1, source_target_pairs={{0,12},{4,8},{8,4},{12,0},{1,13},{5,9},{9,5},{13,1},{2,14},{6,10},... | collective-permute-start | bytes 24584 | tf_op jit(solution)/shard_map/ppermute | solution.py:191
  17.1 0.3 collective-permute-start.1
  17.5 0.3 collective-permute-start
  17.8 0.6 collective-permute-done.2.refs_3_
  18.4 3.3 %collective-permute-done.1.refs_2_ = f32[16,128]{1,0:T(8,128)S(1)} collective-permute-done((f32[16,128]{1,0:T(8,128)}, f32[16,128]{1,0:T(8,128)S(1)}, u32[]{:S(2)}, u32[]{:S(2)}) %collective-permute-start.1) | collective-permute-done | bytes 8224 | tf_op jit(solution)/shard_map/ppermute | solution.py:191
  21.7 0.7 %copy-done = f32[16,128]{1,0:T(8,128)S(1)} copy-done((f32[16,128]{1,0:T(8,128)S(1)}, f32[16,128]{1,0:T(8,128)}, u32[]{:S(2)}) %copy-start) | copy-done | bytes 8216
  22.4 0.1 blank_features.1
  22.4 1.8 %all-to-all-done.refs_0_ = bf16[32,24,128]{2,1,0:T(8,128)(2,1)S(1)} async-done(((bf16[32,24,128]{2,1,0:T(8,128)(2,1)}), bf16[32,24,128]{2,1,0:T(8,128)(2,1)S(1)}, u32[]{:S(2)}, u32[]{:S(2)}) %all-to-all-start) | async-done | bytes 196640 | tf_op jit(solution)/shard_map/all_to_all | solution.py:228
  24.2 2.7 %collective-permute-start.3 = (bf16[32,24,128]{2,1,0:T(8,128)(2,1)S(1)}, bf16[32,24,128]{2,1,0:T(8,128)(2,1)S(1)}, u32[]{:S(2)}, u32[]{:S(2)}) collective-permute-start(bf16[32,24,128]{2,1,0:T(8,128)(2,1)S(1)} %all-to-all-done.refs_0_), channel_id=1, source_target_pairs={{0,1},{1,0},{2,3},{3,2},{4,5},{5,4},{6,7},{7,6},{8,9},{9,8},{10,11... | collective-permute-start | bytes 589832 | tf_op jit(solution)/shard_map/ppermute | solution.py:191
  27.0 1.8 %form_own.1 = (bf16[5,256,512]{2,1,0:T(8,128)(2,1)S(1)}, f32[64,512]{1,0:T(8,128)S(1)}) custom-call(bf16[32,24,128]{2,1,0:T(8,128)(2,1)S(1)} %all-to-all-done.refs_0_, bf16[2,128,512]{2,1,0:T(8,128)(2,1)S(1)} %get-tuple-element.22.refs_1_, f32[16,512]{1,0:T(8,128)S(1)} %get-tuple-element.20.refs_2_.refs_0_), custom_call_target="tpu_custom_call" | custom-call | flops 503316480 | bytes 1638400 | tf_op jit(solution)/shard_map/form_own/pallas_call | solution.py:244
  28.8 1.8 %form_other.1 = (bf16[5,256,512]{2,1,0:T(8,128)(2,1)S(1)}, bf16[64,512]{1,0:T(8,128)(2,1)S(1)}) custom-call(bf16[32,24,128]{2,1,0:T(8,128)(2,1)S(1)} %collective-permute-done.3.refs_0_, bf16[2,128,512]{2,1,0:T(8,128)(2,1)S(1)} %get-tuple-element.22.refs_1_, f32[16,512]{1,0:T(8,128)S(1)} %get-tuple-element.20.refs_2_.refs_0_, ...), custom_call_target="tpu_custom_call" | custom-call | flops 503316480 | bytes 1638400 | tf_op jit(solution)/shard_map/form_other/pallas_call | solution.py:251
  30.6 2.8 %collective-permute-start.6 = (bf16[64,512]{1,0:T(8,128)(2,1)S(1)}, bf16[64,512]{1,0:T(8,128)(2,1)S(1)}, u32[]{:S(2)}, u32[]{:S(2)}) collective-permute-start(bf16[64,512]{1,0:T(8,128)(2,1)S(1)} %get-tuple-element.24.refs_1_), channel_id=1, source_target_pairs={{0,12},{4,8},{8,4},{12,0},{1,13},{5,9},{9,5},{13,1},{2,14},{6,10},... | collective-permute-start | bytes 196616 | tf_op jit(solution)/shard_map/ppermute | solution.py:191
  33.4 0.3 collective-permute-start.5
  33.7 0.3 collective-permute-start.4
  34.1 2.0 %collective-permute-done.6.refs_4_ = bf16[64,512]{1,0:T(8,128)(2,1)S(1)} collective-permute-done((bf16[64,512]{1,0:T(8,128)(2,1)S(1)}, bf16[64,512]{1,0:T(8,128)(2,1)S(1)}, u32[]{:S(2)}, u32[]{:S(2)}) %collective-permute-start.6) | collective-permute-done | bytes 65568 | tf_op jit(solution)/shard_map/ppermute | solution.py:191
  36.0 2.0 %collective-permute-done.5.refs_3_ = bf16[64,512]{1,0:T(8,128)(2,1)S(1)} collective-permute-done((bf16[64,512]{1,0:T(8,128)(2,1)S(1)}, bf16[64,512]{1,0:T(8,128)(2,1)S(1)}, u32[]{:S(2)}, u32[]{:S(2)}) %collective-permute-start.5) | collective-permute-done | bytes 65568 | tf_op jit(solution)/shard_map/ppermute | solution.py:191
  38.0 1.0 %weigh.1 = (bf16[64,128]{1,0:T(8,128)(2,1)}, bf16[64,512]{1,0:T(8,128)(2,1)S(1)}, bf16[32,24,128]{2,1,0:T(8,128)(2,1)S(1)}) custom-call(f32[16,512]{1,0:T(8,128)S(1)} %get-tuple-element.20.refs_2_.refs_0_, bf16[64,512]{1,0:T(8,128)(2,1)S(1)} %get-tuple-element.24.refs_1_, bf16[64,512]{1,0:T(8,128)(2,1)S(1)} %collective-permute-done.4.refs_2_, ...), custom_call_target="tpu_custom_call" | custom-call | flops 83886080 | bytes 1638400 | tf_op jit(solution)/shard_map/weigh/pallas_call | solution.py:266
  39.0 2.1 %collective-permute-start.7 = (bf16[32,24,128]{2,1,0:T(8,128)(2,1)S(1)}, bf16[32,24,128]{2,1,0:T(8,128)(2,1)S(1)}, u32[]{:S(2)}, u32[]{:S(2)}) collective-permute-start(bf16[32,24,128]{2,1,0:T(8,128)(2,1)S(1)} %get-tuple-element.29), channel_id=1, source_target_pairs={{0,1},{1,0},{2,3},{3,2},{4,5},{5,4},{6,7},{7,6},{8,9},{9,8},{10,11... | collective-permute-start | bytes 589832 | tf_op jit(solution)/shard_map/ppermute | solution.py:191
  41.1 0.5 react.1
  41.6 0.6 collective-permute-done.7
  42.2 15.8 %all_to_all.10.arrived_ref = bf16[32,24,128]{2,1,0:T(8,128)(2,1)S(1)} all-to-all(bf16[32,24,128]{2,1,0:T(8,128)(2,1)S(1)} %add_convert_fusion), channel_id=1, replica_groups=mesh['zh'=4,'zl'=2,'xh'=2,'y'=4,'xl'=2,'core'=2] {'zh','zl','xh','xl'}, dimensions={0} | all-to-all | bytes 393216 | tf_op jit(solution)/shard_map/all_to_all | solution.py:286
  58.0 0.7 %finish.1 = f32[40,64]{1,0:T(8,128)} custom-call(bf16[32,24,128]{2,1,0:T(8,128)(2,1)S(1)} %all_to_all.10.arrived_ref), custom_call_target="tpu_custom_call" | custom-call | tf_op jit(solution)/shard_map/finish/pallas_call | solution.py:287
  (5 shorter events, 0.1 us)
Async XLA Ops:
  2.5 21.8 %all-to-all-start = ((bf16[32,24,128]{2,1,0:T(8,128)(2,1)}), bf16[32,24,128]{2,1,0:T(8,128)(2,1)S(1)}, u32[]{:S(2)}, u32[]{:S(2)}) async-start(bf16[32,24,128]{2,1,0:T(8,128)(2,1)} %get-tuple-element.16), calls=%async_computation | async-start | bytes 393216 | tf_op jit(solution)/shard_map/all_to_all | solution.py:228
  14.3 4.1 %collective-permute-start.2 = (f32[16,128]{1,0:T(8,128)}, f32[16,128]{1,0:T(8,128)S(1)}, u32[]{:S(2)}, u32[]{:S(2)}) collective-permute-start(f32[16,128]{1,0:T(8,128)} %get-tuple-element.17.refs_0_), channel_id=1, source_target_pairs={{0,12},{4,8},{8,4},{12,0},{1,13},{5,9},{9,5},{13,1},{2,14},{6,10},... | collective-permute-start | bytes 24584 | tf_op jit(solution)/shard_map/ppermute | solution.py:191
  17.1 4.5 %collective-permute-start.1 = (f32[16,128]{1,0:T(8,128)}, f32[16,128]{1,0:T(8,128)S(1)}, u32[]{:S(2)}, u32[]{:S(2)}) collective-permute-start(f32[16,128]{1,0:T(8,128)} %get-tuple-element.17.refs_0_), channel_id=1, source_target_pairs={{0,8},{4,12},{8,0},{12,4},{1,9},{5,13},{9,1},{13,5},{2,10},{6,14},... | collective-permute-start | bytes 24584 | tf_op jit(solution)/shard_map/ppermute | solution.py:191
  17.5 4.2 %collective-permute-start = (f32[16,128]{1,0:T(8,128)}, f32[16,128]{1,0:T(8,128)S(1)}, u32[]{:S(2)}, u32[]{:S(2)}) collective-permute-start(f32[16,128]{1,0:T(8,128)} %get-tuple-element.17.refs_0_), channel_id=1, source_target_pairs={{0,4},{4,0},{8,12},{12,8},{1,5},{5,1},{9,13},{13,9},{2,6},{6,2},{1... | collective-permute-start | bytes 24584 | tf_op jit(solution)/shard_map/ppermute | solution.py:191
  21.7 0.7 %copy-start = (f32[16,128]{1,0:T(8,128)S(1)}, f32[16,128]{1,0:T(8,128)}, u32[]{:S(2)}) copy-start(f32[16,128]{1,0:T(8,128)} %get-tuple-element.17.refs_0_) | copy-start | bytes 24580
  24.2 4.5 %collective-permute-start.3 = (bf16[32,24,128]{2,1,0:T(8,128)(2,1)S(1)}, bf16[32,24,128]{2,1,0:T(8,128)(2,1)S(1)}, u32[]{:S(2)}, u32[]{:S(2)}) collective-permute-start(bf16[32,24,128]{2,1,0:T(8,128)(2,1)S(1)} %all-to-all-done.refs_0_), channel_id=1, source_target_pairs={{0,1},{1,0},{2,3},{3,2},{4,5},{5,4},{6,7},{7,6},{8,9},{9,8},{10,11... | collective-permute-start | bytes 589832 | tf_op jit(solution)/shard_map/ppermute | solution.py:191
  30.6 5.5 %collective-permute-start.6 = (bf16[64,512]{1,0:T(8,128)(2,1)S(1)}, bf16[64,512]{1,0:T(8,128)(2,1)S(1)}, u32[]{:S(2)}, u32[]{:S(2)}) collective-permute-start(bf16[64,512]{1,0:T(8,128)(2,1)S(1)} %get-tuple-element.24.refs_1_), channel_id=1, source_target_pairs={{0,12},{4,8},{8,4},{12,0},{1,13},{5,9},{9,5},{13,1},{2,14},{6,10},... | collective-permute-start | bytes 196616 | tf_op jit(solution)/shard_map/ppermute | solution.py:191
  33.4 4.6 %collective-permute-start.5 = (bf16[64,512]{1,0:T(8,128)(2,1)S(1)}, bf16[64,512]{1,0:T(8,128)(2,1)S(1)}, u32[]{:S(2)}, u32[]{:S(2)}) collective-permute-start(bf16[64,512]{1,0:T(8,128)(2,1)S(1)} %get-tuple-element.24.refs_1_), channel_id=1, source_target_pairs={{0,8},{4,12},{8,0},{12,4},{1,9},{5,13},{9,1},{13,5},{2,10},{6,14},... | collective-permute-start | bytes 196616 | tf_op jit(solution)/shard_map/ppermute | solution.py:191
  33.7 4.3 %collective-permute-start.4 = (bf16[64,512]{1,0:T(8,128)(2,1)S(1)}, bf16[64,512]{1,0:T(8,128)(2,1)S(1)}, u32[]{:S(2)}, u32[]{:S(2)}) collective-permute-start(bf16[64,512]{1,0:T(8,128)(2,1)S(1)} %get-tuple-element.24.refs_1_), channel_id=1, source_target_pairs={{0,4},{4,0},{8,12},{12,8},{1,5},{5,1},{9,13},{13,9},{2,6},{6,2},{1... | collective-permute-start | bytes 196616 | tf_op jit(solution)/shard_map/ppermute | solution.py:191
  39.0 3.2 %collective-permute-start.7 = (bf16[32,24,128]{2,1,0:T(8,128)(2,1)S(1)}, bf16[32,24,128]{2,1,0:T(8,128)(2,1)S(1)}, u32[]{:S(2)}, u32[]{:S(2)}) collective-permute-start(bf16[32,24,128]{2,1,0:T(8,128)(2,1)S(1)} %get-tuple-element.29), channel_id=1, source_target_pairs={{0,1},{1,0},{2,3},{3,2},{4,5},{5,4},{6,7},{7,6},{8,9},{9,8},{10,11... | collective-permute-start | bytes 589832 | tf_op jit(solution)/shard_map/ppermute | solution.py:191

commit v4 on v3

--- a/solution.py
+++ b/solution.py
@@ -9,7 +9,7 @@
 AXES = ("zh", "zl", "xh", "y", "xl", "core")
 SIZES = (4, 2, 2, 4, 2, 2)
 ROWS = ("y",)
-COLS = ("zh", "zl", "xh", "xl")
+COLS = ("xh", "xl", "zh", "zl")
 LANES = 128
 SUBLANES = 8
 SLOT = 32
@@ -119,7 +119,6 @@
     groups = kernel_ref.shape[0]
     payload = payload_ref[...]
     geometry = group_rows(payload, 2).astype(F32)
-    total = None if first else before_ref[...]
     for group in range(groups):
         coils = coil_features(geometry, group)
         block = None
@@ -127,13 +126,16 @@
             squared = jnp.dot(coils, feature_ref[point], preferred_element_type=F32)
             term = row_ref[pl.ds(4 * point + 3, 1), :] * lax.rsqrt(squared)
             block = term if block is None else block + term
-        block = block.astype(BF16)
-        kernel_ref[group] = block
-        product = lax.dot_general(
-            group_rows(payload, group), block, (((0,), (0,)), ((), ())), preferred_element_type=F32
-        )
-        product = product[:samples] if group < 3 else product[samples:]
-        total = product if total is None else total + product
+        kernel_ref[group] = block.astype(BF16)
+    turned = [group_rows(payload, group).T for group in range(3)]
+    current = [
+        turned[group % 3][:samples] if group < 3 else turned[group % 3][samples:]
+        for group in range(groups)
+    ]
+    kernel = kernel_ref[...].reshape(groups * kernel_ref.shape[1], kernel_ref.shape[2])
+    total = jnp.dot(jnp.concatenate(current, 1), kernel, preferred_element_type=F32)
+    if not first:
+        total = total + before_ref[...]
     out_ref[...] = total.astype(out_ref.dtype)
 
 
@@ -146,13 +148,18 @@
         )
         for group in range(groups)
     ]
-    lane = lax.broadcasted_iota(jnp.int32, whole[0].shape, 1)
-    rows = []
-    for group in range(3):
-        other = whole[group + 3] if group + 3 < groups else jnp.zeros_like(whole[group])
-        both = jnp.where(lane < LANES // 2, whole[group], other)
-        rows.append(both.reshape(both.shape[0] // SUBLANES, SUBLANES, LANES))
-    return jnp.concatenate(rows, 1)
+    shards = whole[0].shape[0] // SUBLANES
+    whole = [part.reshape(shards, SUBLANES, LANES) for part in whole]
+    lane = lax.broadcasted_iota(jnp.int32, whole[0].shape, 2)
+    others = [whole[3], whole[4], pltpu.roll(whole[2], SUBLANES // 2, 1)]
+    return [jnp.where(lane < LANES // 2, whole[group], others[group]) for group in range(3)]
+
+
+def store_rows(out_ref, groups):
+    for pair in range(out_ref.shape[2] // LANES):
+        at = 2 * (pair % 4)
+        rows = groups[pair // 4][:, at : at + 2, :]
+        out_ref[:, :, pl.ds(pair * LANES, LANES)] = rows.astype(out_ref.dtype)
 
 
 def weigh(scale, row_ref, *refs):
@@ -171,18 +178,21 @@
     current = jnp.concatenate(blocks, 1).astype(F32)
     weighted = (row_ref[pl.ds(8, 1), :] * current).astype(BF16)
     weighted_ref[...] = weighted
-    out_ref[...] = (scale * contract(kernel_ref, weighted)).astype(out_ref.dtype)
-
-
-def react(scale, weighted_ref, kernel_ref, out_ref):
-    out_ref[...] = scale * contract(kernel_ref, weighted_ref[...])
+    store_rows(out_ref, [scale * part for part in contract(kernel_ref, weighted)])
+
+
+def react(scale, weighted_ref, kernel_ref, current_ref, out_ref, blank_ref):
+    store_rows(out_ref, [scale * part for part in contract(kernel_ref, weighted_ref[...])])
+    blank_ref[...] = current_ref[...]
 
 
 def finish(arrived_ref, out_ref):
     total = jnp.sum(arrived_ref[...].astype(F32), 0)
-    half, samples = total.shape[0], out_ref.shape[1]
+    rows = [total[:, LANES * pair : LANES * (pair + 1)] for pair in range(total.shape[1] // LANES)]
+    rows = jnp.concatenate(rows, 0)
+    samples = out_ref.shape[1]
     out_ref[...] = jnp.concatenate(
-        [total[:, :samples], total[: out_ref.shape[0] - half, samples:]], 0
+        [rows[:, :samples], rows[16:, samples:], rows[:16, samples:]], 0
     )
 
 
@@ -206,6 +216,7 @@
     points = quad_weight.shape[1]
     width = rows * blanks
     packed = (cols, 24, LANES)
+    dense = (cols, 2, coils * samples // 2)
     kernel_shape = shaped((coils // SUBLANES, cols * SUBLANES, width), BF16)
     smem = pl.BlockSpec(memory_space=pltpu.SMEM)
     vmem = pl.BlockSpec(memory_space=pltpu.VMEM)
@@ -268,20 +279,20 @@
         out_shape=(
             shaped((samples, blanks), BF16),
             shaped((samples, width), BF16),
-            shaped(packed, BF16),
+            shaped(dense, BF16),
         ),
         compiler_params=ROOM,
         cost_estimate=react_cost,
         name="weigh",
     )(table, *arrivals, other_kernel)
     crossed = from_partner(reaction, "core", 1)
-    reaction = pl.pallas_call(
+    reaction, blank_current = pl.pallas_call(
         lambda *refs: react(scale, *refs),
-        out_shape=shaped(packed, F32),
+        out_shape=(shaped(dense, F32), shaped((samples, blanks), BF16)),
         compiler_params=ROOM,
         cost_estimate=react_cost,
         name="react",
-    )(weighted, own_kernel)
+    )(weighted, own_kernel, blank_current)
     pieces = (reaction + crossed.astype(F32)).astype(BF16)
     arrived = lax.all_to_all(pieces, COLS, 0, 0, tiled=True)
     coil_reaction = pl.pallas_call(

time: 59 us -> 57.1 us (0.968)
  waiting for transfers between devices: 10.2 us -> 9.07 us
  Pallas kernels: 7.7 us -> 6.75 us
  blocking collectives: 15.8 us -> 15.2 us
    all_to_all x1, blocking collectives: 15.8 us -> 15.2 us  [per_device(): arrived = lax.all_to_all(pieces, COLS, 0, 0, tiled=True)]
    pallas_call x1, Pallas kernels: 1.78 us -> 1.19 us  [per_device(): pl.pallas_call(lambda *refs: form(False, *refs), out_shape=(kernel_shape,...]
  transfers between devices with their start and end apart: 9 -> 9, of which waited for: 6 -> 5; matrix products, arithmetic and copies ran while one was open for 0% -> 0% of each run, Pallas kernels for 4% -> 4%
where the time goes in v4:
time: 57.1 us; the launch traced here: 56.4 us
  starting transfers between devices  23.8 us (42%)
  blocking collectives  15.2 us (27%)
  waiting for transfers between devices  9.07 us (16%)
  Pallas kernels  6.75 us (12%)
  local copies, waits for them, and re-layouts  0.7 us (1%)
  between operations  0.68 us (1%)
    all_to_all x1, blocking collectives, per_device(): arrived = lax.all_to_all(pieces, COLS, 0, 0, tiled=True)  15.2 us
    ppermute x8, starting transfers between devices, from_partner(): return lax.ppermute(value, axis, [(i, i ^ flip) for i in range(size)])  12 us
    all_to_all x1, starting transfers between devices, per_device(): own = lax.all_to_all(payload, COLS, 0, 0, tiled=True)  11.9 us
    ppermute x8, waiting for transfers between devices, from_partner(): return lax.ppermute(value, axis, [(i, i ^ flip) for i in range(size)])  7.78 us
    pallas_call x1, Pallas kernels, per_device(): pl.pallas_call(prepare, out_shape=(shaped(packed, BF16), shaped((16, blan...  1.82 us
    all_to_all x1, waiting for transfers between devices, per_device(): own = lax.all_to_all(payload, COLS, 0, 0, tiled=True)  1.28 us
    pallas_call x1, Pallas kernels, per_device(): pl.pallas_call(lambda *refs: form(True, *refs), out_shape=(kernel_shape,...  1.21 us
    pallas_call x1, Pallas kernels, per_device(): pl.pallas_call(lambda *refs: form(False, *refs), out_shape=(kernel_shape,...  1.19 us
  transfers between devices with their start and end apart: 9, of which 5 were waited for; matrix products, arithmetic and copies ran while one was open for 0% of the time, Pallas kernels for 4%

profile of v4, /device:TPU:1, one launch (start us, length us, event | category | flops | bytes accessed | tf_op | source)
XLA Modules:
  0.0 56.4 jit_solution(1717924778121192386)
XLA Ops:
  0.6 1.8 %prepare.1 = (bf16[32,24,128]{2,1,0:T(8,128)(2,1)}, f32[16,128]{1,0:T(8,128)}) custom-call(f32[3,2,8]{2,1,0:T(2,128)} %bitcast.9, f32[2,8]{1,0:T(2,128)} %bitcast.10, f32[3,40]{1,0:T(4,128)} %pos_ref.1, f32[1,40]{1,0:T(1,128)} %bitcast.11, bf16[40,64]{1,0:T(8,128)(2,1)} %bitcast.8, f32[3,128]{1,0:T(4,128)} %blank_ref.1, s32[1,128]{1,0:T(1,128)} %bitcast.12, ...), custom_call_target="tpu_custom_call" | custom-call | tf_op jit(solution)/shard_map/prepare/pallas_call | solution.py:224
  2.5 11.9 %all-to-all-start = ((bf16[32,24,128]{2,1,0:T(8,128)(2,1)}), bf16[32,24,128]{2,1,0:T(8,128)(2,1)S(1)}, u32[]{:S(2)}, u32[]{:S(2)}) async-start(bf16[32,24,128]{2,1,0:T(8,128)(2,1)} %get-tuple-element.18), calls=%async_computation | async-start | bytes 393216 | tf_op jit(solution)/shard_map/all_to_all | solution.py:239
  14.3 2.8 %collective-permute-start.2 = (f32[16,128]{1,0:T(8,128)}, f32[16,128]{1,0:T(8,128)S(1)}, u32[]{:S(2)}, u32[]{:S(2)}) collective-permute-start(f32[16,128]{1,0:T(8,128)} %get-tuple-element.19.refs_0_), channel_id=1, source_target_pairs={{0,12},{4,8},{8,4},{12,0},{1,13},{5,9},{9,5},{13,1},{2,14},{6,10},... | collective-permute-start | bytes 24584 | tf_op jit(solution)/shard_map/ppermute | solution.py:201
  17.1 0.3 collective-permute-start.1
  17.5 0.3 collective-permute-start
  17.8 0.6 %collective-permute-done.2.refs_3_ = f32[16,128]{1,0:T(8,128)S(1)} collective-permute-done((f32[16,128]{1,0:T(8,128)}, f32[16,128]{1,0:T(8,128)S(1)}, u32[]{:S(2)}, u32[]{:S(2)}) %collective-permute-start.2) | collective-permute-done | bytes 8224 | tf_op jit(solution)/shard_map/ppermute | solution.py:201
  18.4 3.3 %collective-permute-done.1.refs_2_ = f32[16,128]{1,0:T(8,128)S(1)} collective-permute-done((f32[16,128]{1,0:T(8,128)}, f32[16,128]{1,0:T(8,128)S(1)}, u32[]{:S(2)}, u32[]{:S(2)}) %collective-permute-start.1) | collective-permute-done | bytes 8224 | tf_op jit(solution)/shard_map/ppermute | solution.py:201
  21.7 0.7 %copy-done = f32[16,128]{1,0:T(8,128)S(1)} copy-done((f32[16,128]{1,0:T(8,128)S(1)}, f32[16,128]{1,0:T(8,128)}, u32[]{:S(2)}) %copy-start) | copy-done | bytes 8216
  22.4 0.1 blank_features.1
  22.4 1.3 %all-to-all-done.refs_0_ = bf16[32,24,128]{2,1,0:T(8,128)(2,1)S(1)} async-done(((bf16[32,24,128]{2,1,0:T(8,128)(2,1)}), bf16[32,24,128]{2,1,0:T(8,128)(2,1)S(1)}, u32[]{:S(2)}, u32[]{:S(2)}) %all-to-all-start) | async-done | bytes 196640 | tf_op jit(solution)/shard_map/all_to_all | solution.py:239
  23.7 2.8 %collective-permute-start.3 = (bf16[32,24,128]{2,1,0:T(8,128)(2,1)S(1)}, bf16[32,24,128]{2,1,0:T(8,128)(2,1)S(1)}, u32[]{:S(2)}, u32[]{:S(2)}) collective-permute-start(bf16[32,24,128]{2,1,0:T(8,128)(2,1)S(1)} %all-to-all-done.refs_0_), channel_id=1, source_target_pairs={{0,1},{1,0},{2,3},{3,2},{4,5},{5,4},{6,7},{7,6},{8,9},{9,8},{10,11... | collective-permute-start | bytes 589832 | tf_op jit(solution)/shard_map/ppermute | solution.py:201
  26.6 1.2 %form_own.1 = (bf16[5,256,512]{2,1,0:T(8,128)(2,1)S(1)}, f32[64,512]{1,0:T(8,128)S(1)}) custom-call(bf16[32,24,128]{2,1,0:T(8,128)(2,1)S(1)} %all-to-all-done.refs_0_, bf16[2,128,512]{2,1,0:T(8,128)(2,1)S(1)} %get-tuple-element.24.refs_1_, f32[16,512]{1,0:T(8,128)S(1)} %get-tuple-element.22.refs_2_.refs_0_), custom_call_target="tpu_custom_call" | custom-call | flops 503316480 | bytes 1638400 | tf_op jit(solution)/shard_map/form_own/pallas_call | solution.py:255
  27.8 1.2 %form_other.1 = (bf16[5,256,512]{2,1,0:T(8,128)(2,1)S(1)}, bf16[64,512]{1,0:T(8,128)(2,1)S(1)}) custom-call(bf16[32,24,128]{2,1,0:T(8,128)(2,1)S(1)} %collective-permute-done.3.refs_0_, bf16[2,128,512]{2,1,0:T(8,128)(2,1)S(1)} %get-tuple-element.24.refs_1_, f32[16,512]{1,0:T(8,128)S(1)} %get-tuple-element.22.refs_2_.refs_0_, ...), custom_call_target="tpu_custom_call" | custom-call | flops 503316480 | bytes 1638400 | tf_op jit(solution)/shard_map/form_other/pallas_call | solution.py:262
  29.0 2.8 %collective-permute-start.6 = (bf16[64,512]{1,0:T(8,128)(2,1)S(1)}, bf16[64,512]{1,0:T(8,128)(2,1)S(1)}, u32[]{:S(2)}, u32[]{:S(2)}) collective-permute-start(bf16[64,512]{1,0:T(8,128)(2,1)S(1)} %get-tuple-element.26.refs_1_), channel_id=1, source_target_pairs={{0,12},{4,8},{8,4},{12,0},{1,13},{5,9},{9,5},{13,1},{2,14},{6,10},... | collective-permute-start | bytes 196616 | tf_op jit(solution)/shard_map/ppermute | solution.py:201
  31.8 0.3 collective-permute-start.5
  32.1 0.3 collective-permute-start.4
  32.4 1.4 %collective-permute-done.6.refs_4_ = bf16[64,512]{1,0:T(8,128)(2,1)S(1)} collective-permute-done((bf16[64,512]{1,0:T(8,128)(2,1)S(1)}, bf16[64,512]{1,0:T(8,128)(2,1)S(1)}, u32[]{:S(2)}, u32[]{:S(2)}) %collective-permute-start.6) | collective-permute-done | bytes 65568 | tf_op jit(solution)/shard_map/ppermute | solution.py:201
  33.8 2.6 %collective-permute-done.5.refs_3_ = bf16[64,512]{1,0:T(8,128)(2,1)S(1)} collective-permute-done((bf16[64,512]{1,0:T(8,128)(2,1)S(1)}, bf16[64,512]{1,0:T(8,128)(2,1)S(1)}, u32[]{:S(2)}, u32[]{:S(2)}) %collective-permute-start.5) | collective-permute-done | bytes 65568 | tf_op jit(solution)/shard_map/ppermute | solution.py:201
  36.4 0.6 weigh.1
  37.0 2.2 %collective-permute-start.7 = (bf16[32,2,1280]{2,1,0:T(2,128)(2,1)S(1)}, bf16[32,2,1280]{2,1,0:T(2,128)(2,1)S(1)}, u32[]{:S(2)}, u32[]{:S(2)}) collective-permute-start(bf16[32,2,1280]{2,1,0:T(2,128)(2,1)S(1)} %get-tuple-element.33), channel_id=1, source_target_pairs={{0,1},{1,0},{2,3},{3,2},{4,5},{5,4},{6,7},{7,6},{8,9},{9,8},{10,11... | collective-permute-start | bytes 491528 | tf_op jit(solution)/shard_map/ppermute | solution.py:201
  39.1 1.0 %react.1 = (f32[32,2,1280]{2,1,0:T(2,128)S(1)}, bf16[64,128]{1,0:T(8,128)(2,1)}) custom-call(bf16[64,512]{1,0:T(8,128)(2,1)S(1)} %get-tuple-element.28.refs_0_, bf16[5,256,512]{2,1,0:T(8,128)(2,1)S(1)} %get-tuple-element.29.refs_1_, bf16[64,128]{1,0:T(8,128)(2,1)S(1)} %get-tuple-element.30.refs_2_), custom_call_target="tpu_custom_call" | custom-call | flops 83886080 | bytes 1638400 | tf_op jit(solution)/shard_map/react/pallas_call | solution.py:289
  40.2 0.2 add_convert_fusion
  40.4 15.2 %all_to_all.10.arrived_ref = bf16[32,2,1280]{2,1,0:T(2,128)(2,1)S(1)} all-to-all(bf16[32,2,1280]{2,1,0:T(2,128)(2,1)S(1)} %add_convert_fusion), channel_id=1, replica_groups=mesh['zh'=4,'zl'=2,'xh'=2,'y'=4,'xl'=2,'core'=2] {'xh','xl','zh','zl'}, dimensions={0} | all-to-all | bytes 327680 | tf_op jit(solution)/shard_map/all_to_all | solution.py:297
  55.5 0.8 %finish.1 = f32[40,64]{1,0:T(8,128)} custom-call(bf16[32,2,1280]{2,1,0:T(2,128)(2,1)S(1)} %all_to_all.10.arrived_ref), custom_call_target="tpu_custom_call" | custom-call | tf_op jit(solution)/shard_map/finish/pallas_call | solution.py:298
  (5 shorter events, 0.0 us)
Async XLA Ops:
  2.5 21.3 %all-to-all-start = ((bf16[32,24,128]{2,1,0:T(8,128)(2,1)}), bf16[32,24,128]{2,1,0:T(8,128)(2,1)S(1)}, u32[]{:S(2)}, u32[]{:S(2)}) async-start(bf16[32,24,128]{2,1,0:T(8,128)(2,1)} %get-tuple-element.18), calls=%async_computation | async-start | bytes 393216 | tf_op jit(solution)/shard_map/all_to_all | solution.py:239
  14.3 4.1 %collective-permute-start.2 = (f32[16,128]{1,0:T(8,128)}, f32[16,128]{1,0:T(8,128)S(1)}, u32[]{:S(2)}, u32[]{:S(2)}) collective-permute-start(f32[16,128]{1,0:T(8,128)} %get-tuple-element.19.refs_0_), channel_id=1, source_target_pairs={{0,12},{4,8},{8,4},{12,0},{1,13},{5,9},{9,5},{13,1},{2,14},{6,10},... | collective-permute-start | bytes 24584 | tf_op jit(solution)/shard_map/ppermute | solution.py:201
  17.1 4.5 %collective-permute-start.1 = (f32[16,128]{1,0:T(8,128)}, f32[16,128]{1,0:T(8,128)S(1)}, u32[]{:S(2)}, u32[]{:S(2)}) collective-permute-start(f32[16,128]{1,0:T(8,128)} %get-tuple-element.19.refs_0_), channel_id=1, source_target_pairs={{0,8},{4,12},{8,0},{12,4},{1,9},{5,13},{9,1},{13,5},{2,10},{6,14},... | collective-permute-start | bytes 24584 | tf_op jit(solution)/shard_map/ppermute | solution.py:201
  17.5 4.2 %collective-permute-start = (f32[16,128]{1,0:T(8,128)}, f32[16,128]{1,0:T(8,128)S(1)}, u32[]{:S(2)}, u32[]{:S(2)}) collective-permute-start(f32[16,128]{1,0:T(8,128)} %get-tuple-element.19.refs_0_), channel_id=1, source_target_pairs={{0,4},{4,0},{8,12},{12,8},{1,5},{5,1},{9,13},{13,9},{2,6},{6,2},{1... | collective-permute-start | bytes 24584 | tf_op jit(solution)/shard_map/ppermute | solution.py:201
  21.7 0.7 %copy-start = (f32[16,128]{1,0:T(8,128)S(1)}, f32[16,128]{1,0:T(8,128)}, u32[]{:S(2)}) copy-start(f32[16,128]{1,0:T(8,128)} %get-tuple-element.19.refs_0_) | copy-start | bytes 24580
  23.7 4.1 %collective-permute-start.3 = (bf16[32,24,128]{2,1,0:T(8,128)(2,1)S(1)}, bf16[32,24,128]{2,1,0:T(8,128)(2,1)S(1)}, u32[]{:S(2)}, u32[]{:S(2)}) collective-permute-start(bf16[32,24,128]{2,1,0:T(8,128)(2,1)S(1)} %all-to-all-done.refs_0_), channel_id=1, source_target_pairs={{0,1},{1,0},{2,3},{3,2},{4,5},{5,4},{6,7},{7,6},{8,9},{9,8},{10,11... | collective-permute-start | bytes 589832 | tf_op jit(solution)/shard_map/ppermute | solution.py:201
  29.0 4.8 %collective-permute-start.6 = (bf16[64,512]{1,0:T(8,128)(2,1)S(1)}, bf16[64,512]{1,0:T(8,128)(2,1)S(1)}, u32[]{:S(2)}, u32[]{:S(2)}) collective-permute-start(bf16[64,512]{1,0:T(8,128)(2,1)S(1)} %get-tuple-element.26.refs_1_), channel_id=1, source_target_pairs={{0,12},{4,8},{8,4},{12,0},{1,13},{5,9},{9,5},{13,1},{2,14},{6,10},... | collective-permute-start | bytes 196616 | tf_op jit(solution)/shard_map/ppermute | solution.py:201
  31.8 4.6 %collective-permute-start.5 = (bf16[64,512]{1,0:T(8,128)(2,1)S(1)}, bf16[64,512]{1,0:T(8,128)(2,1)S(1)}, u32[]{:S(2)}, u32[]{:S(2)}) collective-permute-start(bf16[64,512]{1,0:T(8,128)(2,1)S(1)} %get-tuple-element.26.refs_1_), channel_id=1, source_target_pairs={{0,8},{4,12},{8,0},{12,4},{1,9},{5,13},{9,1},{13,5},{2,10},{6,14},... | collective-permute-start | bytes 196616 | tf_op jit(solution)/shard_map/ppermute | solution.py:201
  32.1 4.3 %collective-permute-start.4 = (bf16[64,512]{1,0:T(8,128)(2,1)S(1)}, bf16[64,512]{1,0:T(8,128)(2,1)S(1)}, u32[]{:S(2)}, u32[]{:S(2)}) collective-permute-start(bf16[64,512]{1,0:T(8,128)(2,1)S(1)} %get-tuple-element.26.refs_1_), channel_id=1, source_target_pairs={{0,4},{4,0},{8,12},{12,8},{1,5},{5,1},{9,13},{13,9},{2,6},{6,2},{1... | collective-permute-start | bytes 196616 | tf_op jit(solution)/shard_map/ppermute | solution.py:201
  37.0 3.2 %collective-permute-start.7 = (bf16[32,2,1280]{2,1,0:T(2,128)(2,1)S(1)}, bf16[32,2,1280]{2,1,0:T(2,128)(2,1)S(1)}, u32[]{:S(2)}, u32[]{:S(2)}) collective-permute-start(bf16[32,2,1280]{2,1,0:T(2,128)(2,1)S(1)} %get-tuple-element.33), channel_id=1, source_target_pairs={{0,1},{1,0},{2,3},{3,2},{4,5},{5,4},{6,7},{7,6},{8,9},{9,8},{10,11... | collective-permute-start | bytes 491528 | tf_op jit(solution)/shard_map/ppermute | solution.py:201

commit v5 on v4

--- a/solution.py
+++ b/solution.py
@@ -221,12 +221,7 @@
     smem = pl.BlockSpec(memory_space=pltpu.SMEM)
     vmem = pl.BlockSpec(memory_space=pltpu.VMEM)
 
-    payload, tile = pl.pallas_call(
-        prepare,
-        out_shape=(shaped(packed, BF16), shaped((16, blanks), F32)),
-        in_specs=[smem, smem] + [vmem] * 6,
-        name="prepare",
-    )(
+    arguments = (
         quad_offset.transpose(0, 2, 1),
         quad_weight.T,
         coil_pos,
@@ -236,6 +231,13 @@
         blank_rule[None, :],
         blank_cond[None, :],
     )
+    payload, tile = pl.pallas_call(
+        prepare,
+        out_shape=(shaped(packed, BF16), shaped((16, blanks), F32)),
+        in_specs=[smem, smem] + [vmem] * 6,
+        compiler_params=ROOM,
+        name="prepare",
+    )(*(pltpu.with_memory_space_constraint(value, pltpu.HBM) for value in arguments))
     own = lax.all_to_all(payload, COLS, 0, 0, tiled=True)
     tiles = [tile] + [from_partner(tile, ROWS, flip) for flip in range(1, rows)]
     features, table = pl.pallas_call(

time: 57.1 us -> 56.2 us (0.984)
  blocking collectives: 15.2 us -> 14.2 us
  local copies, waits for them, and re-layouts: 0.7 us -> 0 us
  waiting for transfers between devices: 9.07 us -> 9.76 us
    all_to_all x1, blocking collectives: 15.2 us -> 14.2 us  [per_device(): arrived = lax.all_to_all(pieces, COLS, 0, 0, tiled=True)]
    all_to_all x1, waiting for transfers between devices: 1.28 us -> 2.19 us  [per_device(): own = lax.all_to_all(payload, COLS, 0, 0, tiled=True)]
    unnamed x2 -> x0, local copies, waits for them, and re-layouts: 0.7 us -> none
where the time goes in v5:
time: 56.2 us; the launch traced here: 55.5 us
  starting transfers between devices  23.9 us (43%)
  blocking collectives  14.2 us (25%)
  waiting for transfers between devices  9.76 us (17%)
  Pallas kernels  6.69 us (12%)
  between operations  0.67 us (1%)
    all_to_all x1, blocking collectives, per_device(): arrived = lax.all_to_all(pieces, COLS, 0, 0, tiled=True)  14.2 us
    ppermute x8, starting transfers between devices, from_partner(): return lax.ppermute(value, axis, [(i, i ^ flip) for i in range(size)])  12.1 us
    all_to_all x1, starting transfers between devices, per_device(): own = lax.all_to_all(payload, COLS, 0, 0, tiled=True)  11.9 us
    ppermute x8, waiting for transfers between devices, from_partner(): return lax.ppermute(value, axis, [(i, i ^ flip) for i in range(size)])  7.57 us
    all_to_all x1, waiting for transfers between devices, per_device(): own = lax.all_to_all(payload, COLS, 0, 0, tiled=True)  2.19 us
    pallas_call x1, Pallas kernels, per_device(): pl.pallas_call(prepare, out_shape=(shaped(packed, BF16), shaped((16, blan...  1.82 us
    pallas_call x1, Pallas kernels, per_device(): pl.pallas_call(lambda *refs: form(False, *refs), out_shape=(kernel_shape,...  1.18 us
    pallas_call x1, Pallas kernels, per_device(): pl.pallas_call(lambda *refs: form(True, *refs), out_shape=(kernel_shape,...  1.17 us
  transfers between devices with their start and end apart: 9, of which 5 were waited for; matrix products, arithmetic and copies ran while one was open for 0% of the time, Pallas kernels for 4%

profile of v5, /device:TPU:1, one launch (start us, length us, event | category | flops | bytes accessed | tf_op | source)
XLA Modules:
  0.0 55.5 jit_solution(15865741955018680661)
XLA Ops:
  0.6 1.8 %prepare.1 = (bf16[32,24,128]{2,1,0:T(8,128)(2,1)}, f32[16,128]{1,0:T(8,128)S(1)}) custom-call(f32[3,2,8]{2,1,0:T(2,128)} %bitcast.9, f32[2,8]{1,0:T(2,128)} %bitcast.10, f32[3,40]{1,0:T(4,128)} %pos_ref.1, f32[1,40]{1,0:T(1,128)} %bitcast.11, bf16[40,64]{1,0:T(8,128)(2,1)} %bitcast.8, f32[3,128]{1,0:T(4,128)} %blank_ref.1, s32[1,128]{1,0:T(1,128)} %bitcast.12, ...), custom_call_target="tpu_custom_call" | custom-call | tf_op jit(solution)/shard_map/prepare/pallas_call | solution.py:234
  2.5 11.9 %all-to-all-start = ((bf16[32,24,128]{2,1,0:T(8,128)(2,1)}), bf16[32,24,128]{2,1,0:T(8,128)(2,1)S(1)}, u32[]{:S(2)}, u32[]{:S(2)}) async-start(bf16[32,24,128]{2,1,0:T(8,128)(2,1)} %get-tuple-element.18), calls=%async_computation | async-start | bytes 393216 | tf_op jit(solution)/shard_map/all_to_all | solution.py:241
  14.3 2.8 %collective-permute-start.2 = (f32[16,128]{1,0:T(8,128)S(1)}, f32[16,128]{1,0:T(8,128)S(1)}, u32[]{:S(2)}, u32[]{:S(2)}) collective-permute-start(f32[16,128]{1,0:T(8,128)S(1)} %get-tuple-element.19.refs_0_), channel_id=1, source_target_pairs={{0,12},{4,8},{8,4},{12,0},{1,13},{5,9},{9,5},{13,1},{2,14},{6,10},... | collective-permute-start | bytes 24584 | tf_op jit(solution)/shard_map/ppermute | solution.py:201
  17.1 0.3 collective-permute-start.1
  17.5 0.3 collective-permute-start
  17.8 0.4 collective-permute-done.2.refs_3_
  18.2 3.3 %collective-permute-done.1.refs_2_ = f32[16,128]{1,0:T(8,128)S(1)} collective-permute-done((f32[16,128]{1,0:T(8,128)S(1)}, f32[16,128]{1,0:T(8,128)S(1)}, u32[]{:S(2)}, u32[]{:S(2)}) %collective-permute-start.1) | collective-permute-done | bytes 8224 | tf_op jit(solution)/shard_map/ppermute | solution.py:201
  21.4 0.0 collective-permute-done.refs_1_
  21.5 0.1 blank_features.1
  21.5 2.2 %all-to-all-done.refs_0_ = bf16[32,24,128]{2,1,0:T(8,128)(2,1)S(1)} async-done(((bf16[32,24,128]{2,1,0:T(8,128)(2,1)}), bf16[32,24,128]{2,1,0:T(8,128)(2,1)S(1)}, u32[]{:S(2)}, u32[]{:S(2)}) %all-to-all-start) | async-done | bytes 196640 | tf_op jit(solution)/shard_map/all_to_all | solution.py:241
  23.7 2.8 %collective-permute-start.3 = (bf16[32,24,128]{2,1,0:T(8,128)(2,1)S(1)}, bf16[32,24,128]{2,1,0:T(8,128)(2,1)S(1)}, u32[]{:S(2)}, u32[]{:S(2)}) collective-permute-start(bf16[32,24,128]{2,1,0:T(8,128)(2,1)S(1)} %all-to-all-done.refs_0_), channel_id=1, source_target_pairs={{0,1},{1,0},{2,3},{3,2},{4,5},{5,4},{6,7},{7,6},{8,9},{9,8},{10,11... | collective-permute-start | bytes 589832 | tf_op jit(solution)/shard_map/ppermute | solution.py:201
  26.6 1.2 %form_own.1 = (bf16[5,256,512]{2,1,0:T(8,128)(2,1)S(1)}, f32[64,512]{1,0:T(8,128)S(1)}) custom-call(bf16[32,24,128]{2,1,0:T(8,128)(2,1)S(1)} %all-to-all-done.refs_0_, bf16[2,128,512]{2,1,0:T(8,128)(2,1)S(1)} %get-tuple-element.24.refs_1_, f32[16,512]{1,0:T(8,128)S(1)} %get-tuple-element.22.refs_2_.refs_0_), custom_call_target="tpu_custom_call" | custom-call | flops 503316480 | bytes 1638400 | tf_op jit(solution)/shard_map/form_own/pallas_call | solution.py:257
  27.8 1.2 %form_other.1 = (bf16[5,256,512]{2,1,0:T(8,128)(2,1)S(1)}, bf16[64,512]{1,0:T(8,128)(2,1)S(1)}) custom-call(bf16[32,24,128]{2,1,0:T(8,128)(2,1)S(1)} %collective-permute-done.3.refs_0_, bf16[2,128,512]{2,1,0:T(8,128)(2,1)S(1)} %get-tuple-element.24.refs_1_, f32[16,512]{1,0:T(8,128)S(1)} %get-tuple-element.22.refs_2_.refs_0_, ...), custom_call_target="tpu_custom_call" | custom-call | flops 503316480 | bytes 1638400 | tf_op jit(solution)/shard_map/form_other/pallas_call | solution.py:264
  28.9 2.9 %collective-permute-start.6 = (bf16[64,512]{1,0:T(8,128)(2,1)S(1)}, bf16[64,512]{1,0:T(8,128)(2,1)S(1)}, u32[]{:S(2)}, u32[]{:S(2)}) collective-permute-start(bf16[64,512]{1,0:T(8,128)(2,1)S(1)} %get-tuple-element.26.refs_1_), channel_id=1, source_target_pairs={{0,12},{4,8},{8,4},{12,0},{1,13},{5,9},{9,5},{13,1},{2,14},{6,10},... | collective-permute-start | bytes 196616 | tf_op jit(solution)/shard_map/ppermute | solution.py:201
  31.8 0.3 collective-permute-start.5
  32.1 0.4 collective-permute-start.4
  32.5 1.4 %collective-permute-done.6.refs_4_ = bf16[64,512]{1,0:T(8,128)(2,1)S(1)} collective-permute-done((bf16[64,512]{1,0:T(8,128)(2,1)S(1)}, bf16[64,512]{1,0:T(8,128)(2,1)S(1)}, u32[]{:S(2)}, u32[]{:S(2)}) %collective-permute-start.6) | collective-permute-done | bytes 65568 | tf_op jit(solution)/shard_map/ppermute | solution.py:201
  33.9 2.5 %collective-permute-done.5.refs_3_ = bf16[64,512]{1,0:T(8,128)(2,1)S(1)} collective-permute-done((bf16[64,512]{1,0:T(8,128)(2,1)S(1)}, bf16[64,512]{1,0:T(8,128)(2,1)S(1)}, u32[]{:S(2)}, u32[]{:S(2)}) %collective-permute-start.5) | collective-permute-done | bytes 65568 | tf_op jit(solution)/shard_map/ppermute | solution.py:201
  36.4 0.6 %weigh.1 = (bf16[64,128]{1,0:T(8,128)(2,1)S(1)}, bf16[64,512]{1,0:T(8,128)(2,1)S(1)}, bf16[32,2,1280]{2,1,0:T(2,128)(2,1)S(1)}) custom-call(f32[16,512]{1,0:T(8,128)S(1)} %get-tuple-element.22.refs_2_.refs_0_, bf16[64,512]{1,0:T(8,128)(2,1)S(1)} %get-tuple-element.26.refs_1_, bf16[64,512]{1,0:T(8,128)(2,1)S(1)} %collective-permute-done.4.refs_2_, ...), custom_call_target="tpu_custom_call" | custom-call | flops 83886080 | bytes 1638400 | tf_op jit(solution)/shard_map/weigh/pallas_call | solution.py:279
  37.0 2.2 %collective-permute-start.7 = (bf16[32,2,1280]{2,1,0:T(2,128)(2,1)S(1)}, bf16[32,2,1280]{2,1,0:T(2,128)(2,1)S(1)}, u32[]{:S(2)}, u32[]{:S(2)}) collective-permute-start(bf16[32,2,1280]{2,1,0:T(2,128)(2,1)S(1)} %get-tuple-element.33), channel_id=1, source_target_pairs={{0,1},{1,0},{2,3},{3,2},{4,5},{5,4},{6,7},{7,6},{8,9},{9,8},{10,11... | collective-permute-start | bytes 491528 | tf_op jit(solution)/shard_map/ppermute | solution.py:201
  39.2 1.0 %react.1 = (f32[32,2,1280]{2,1,0:T(2,128)S(1)}, bf16[64,128]{1,0:T(8,128)(2,1)}) custom-call(bf16[64,512]{1,0:T(8,128)(2,1)S(1)} %get-tuple-element.28.refs_0_, bf16[5,256,512]{2,1,0:T(8,128)(2,1)S(1)} %get-tuple-element.29.refs_1_, bf16[64,128]{1,0:T(8,128)(2,1)S(1)} %get-tuple-element.30.refs_2_), custom_call_target="tpu_custom_call" | custom-call | flops 83886080 | bytes 1638400 | tf_op jit(solution)/shard_map/react/pallas_call | solution.py:291
  40.2 0.2 add_convert_fusion
  40.4 14.2 %all_to_all.10.arrived_ref = bf16[32,2,1280]{2,1,0:T(2,128)(2,1)S(1)} all-to-all(bf16[32,2,1280]{2,1,0:T(2,128)(2,1)S(1)} %add_convert_fusion), channel_id=1, replica_groups=mesh['zh'=4,'zl'=2,'xh'=2,'y'=4,'xl'=2,'core'=2] {'xh','xl','zh','zl'}, dimensions={0} | all-to-all | bytes 327680 | tf_op jit(solution)/shard_map/all_to_all | solution.py:299
  54.6 0.8 %finish.1 = f32[40,64]{1,0:T(8,128)} custom-call(bf16[32,2,1280]{2,1,0:T(2,128)(2,1)S(1)} %all_to_all.10.arrived_ref), custom_call_target="tpu_custom_call" | custom-call | tf_op jit(solution)/shard_map/finish/pallas_call | solution.py:300
  (3 shorter events, 0.0 us)
Async XLA Ops:
  2.5 21.3 %all-to-all-start = ((bf16[32,24,128]{2,1,0:T(8,128)(2,1)}), bf16[32,24,128]{2,1,0:T(8,128)(2,1)S(1)}, u32[]{:S(2)}, u32[]{:S(2)}) async-start(bf16[32,24,128]{2,1,0:T(8,128)(2,1)} %get-tuple-element.18), calls=%async_computation | async-start | bytes 393216 | tf_op jit(solution)/shard_map/all_to_all | solution.py:241
  14.3 3.9 %collective-permute-start.2 = (f32[16,128]{1,0:T(8,128)S(1)}, f32[16,128]{1,0:T(8,128)S(1)}, u32[]{:S(2)}, u32[]{:S(2)}) collective-permute-start(f32[16,128]{1,0:T(8,128)S(1)} %get-tuple-element.19.refs_0_), channel_id=1, source_target_pairs={{0,12},{4,8},{8,4},{12,0},{1,13},{5,9},{9,5},{13,1},{2,14},{6,10},... | collective-permute-start | bytes 24584 | tf_op jit(solution)/shard_map/ppermute | solution.py:201
  17.1 4.3 %collective-permute-start.1 = (f32[16,128]{1,0:T(8,128)S(1)}, f32[16,128]{1,0:T(8,128)S(1)}, u32[]{:S(2)}, u32[]{:S(2)}) collective-permute-start(f32[16,128]{1,0:T(8,128)S(1)} %get-tuple-element.19.refs_0_), channel_id=1, source_target_pairs={{0,8},{4,12},{8,0},{12,4},{1,9},{5,13},{9,1},{13,5},{2,10},{6,14},... | collective-permute-start | bytes 24584 | tf_op jit(solution)/shard_map/ppermute | solution.py:201
  17.5 4.0 %collective-permute-start = (f32[16,128]{1,0:T(8,128)S(1)}, f32[16,128]{1,0:T(8,128)S(1)}, u32[]{:S(2)}, u32[]{:S(2)}) collective-permute-start(f32[16,128]{1,0:T(8,128)S(1)} %get-tuple-element.19.refs_0_), channel_id=1, source_target_pairs={{0,4},{4,0},{8,12},{12,8},{1,5},{5,1},{9,13},{13,9},{2,6},{6,2},{1... | collective-permute-start | bytes 24584 | tf_op jit(solution)/shard_map/ppermute | solution.py:201
  23.7 4.0 %collective-permute-start.3 = (bf16[32,24,128]{2,1,0:T(8,128)(2,1)S(1)}, bf16[32,24,128]{2,1,0:T(8,128)(2,1)S(1)}, u32[]{:S(2)}, u32[]{:S(2)}) collective-permute-start(bf16[32,24,128]{2,1,0:T(8,128)(2,1)S(1)} %all-to-all-done.refs_0_), channel_id=1, source_target_pairs={{0,1},{1,0},{2,3},{3,2},{4,5},{5,4},{6,7},{7,6},{8,9},{9,8},{10,11... | collective-permute-start | bytes 589832 | tf_op jit(solution)/shard_map/ppermute | solution.py:201
  28.9 5.0 %collective-permute-start.6 = (bf16[64,512]{1,0:T(8,128)(2,1)S(1)}, bf16[64,512]{1,0:T(8,128)(2,1)S(1)}, u32[]{:S(2)}, u32[]{:S(2)}) collective-permute-start(bf16[64,512]{1,0:T(8,128)(2,1)S(1)} %get-tuple-element.26.refs_1_), channel_id=1, source_target_pairs={{0,12},{4,8},{8,4},{12,0},{1,13},{5,9},{9,5},{13,1},{2,14},{6,10},... | collective-permute-start | bytes 196616 | tf_op jit(solution)/shard_map/ppermute | solution.py:201
  31.8 4.6 %collective-permute-start.5 = (bf16[64,512]{1,0:T(8,128)(2,1)S(1)}, bf16[64,512]{1,0:T(8,128)(2,1)S(1)}, u32[]{:S(2)}, u32[]{:S(2)}) collective-permute-start(bf16[64,512]{1,0:T(8,128)(2,1)S(1)} %get-tuple-element.26.refs_1_), channel_id=1, source_target_pairs={{0,8},{4,12},{8,0},{12,4},{1,9},{5,13},{9,1},{13,5},{2,10},{6,14},... | collective-permute-start | bytes 196616 | tf_op jit(solution)/shard_map/ppermute | solution.py:201
  32.1 4.3 %collective-permute-start.4 = (bf16[64,512]{1,0:T(8,128)(2,1)S(1)}, bf16[64,512]{1,0:T(8,128)(2,1)S(1)}, u32[]{:S(2)}, u32[]{:S(2)}) collective-permute-start(bf16[64,512]{1,0:T(8,128)(2,1)S(1)} %get-tuple-element.26.refs_1_), channel_id=1, source_target_pairs={{0,4},{4,0},{8,12},{12,8},{1,5},{5,1},{9,13},{13,9},{2,6},{6,2},{1... | collective-permute-start | bytes 196616 | tf_op jit(solution)/shard_map/ppermute | solution.py:201
  37.0 3.2 %collective-permute-start.7 = (bf16[32,2,1280]{2,1,0:T(2,128)(2,1)S(1)}, bf16[32,2,1280]{2,1,0:T(2,128)(2,1)S(1)}, u32[]{:S(2)}, u32[]{:S(2)}) collective-permute-start(bf16[32,2,1280]{2,1,0:T(2,128)(2,1)S(1)} %get-tuple-element.33), channel_id=1, source_target_pairs={{0,1},{1,0},{2,3},{3,2},{4,5},{5,4},{6,7},{7,6},{8,9},{9,8},{10,11... | collective-permute-start | bytes 491528 | tf_op jit(solution)/shard_map/ppermute | solution.py:201

commit v6 on v5

--- a/solution.py
+++ b/solution.py
@@ -8,8 +8,8 @@
 
 AXES = ("zh", "zl", "xh", "y", "xl", "core")
 SIZES = (4, 2, 2, 4, 2, 2)
-ROWS = ("y",)
-COLS = ("xh", "xl", "zh", "zl")
+ROWS = ("xh", "xl")
+COLS = ("zl", "y", "zh")
 LANES = 128
 SUBLANES = 8
 SLOT = 32

time: 56.2 us -> 55.8 us (level)
    all_to_all x1, waiting for transfers between devices: 2.19 us -> 2.82 us  [per_device(): own = lax.all_to_all(payload, COLS, 0, 0, tiled=True)]
    ppermute x8, starting transfers between devices: 12.1 us -> 11.5 us  [from_partner(): return lax.ppermute(value, axis, [(i, i ^ flip) for i in range(size)])]
where the time goes in v6:
time: 55.8 us; the launch traced here: 55.5 us
  starting transfers between devices  23.5 us (42%)
  blocking collectives  14.3 us (26%)
  waiting for transfers between devices  10.2 us (18%)
  Pallas kernels  6.74 us (12%)
  between operations  0.68 us (1%)
    all_to_all x1, blocking collectives, per_device(): arrived = lax.all_to_all(pieces, COLS, 0, 0, tiled=True)  14.3 us
    all_to_all x1, starting transfers between devices, per_device(): own = lax.all_to_all(payload, COLS, 0, 0, tiled=True)  12 us
    ppermute x8, starting transfers between devices, from_partner(): return lax.ppermute(value, axis, [(i, i ^ flip) for i in range(size)])  11.5 us
    ppermute x8, waiting for transfers between devices, from_partner(): return lax.ppermute(value, axis, [(i, i ^ flip) for i in range(size)])  7.34 us
    all_to_all x1, waiting for transfers between devices, per_device(): own = lax.all_to_all(payload, COLS, 0, 0, tiled=True)  2.82 us
    pallas_call x1, Pallas kernels, per_device(): pl.pallas_call(prepare, out_shape=(shaped(packed, BF16), shaped((16, blan...  1.82 us
    pallas_call x1, Pallas kernels, per_device(): pl.pallas_call(lambda *refs: form(True, *refs), out_shape=(kernel_shape,...  1.21 us
    pallas_call x1, Pallas kernels, per_device(): pl.pallas_call(lambda *refs: form(False, *refs), out_shape=(kernel_shape,...  1.19 us
  transfers between devices with their start and end apart: 9, of which 5 were waited for; matrix products, arithmetic and copies ran while one was open for 0% of the time, Pallas kernels for 4%

profile of v6, /device:TPU:1, one launch (start us, length us, event | category | flops | bytes accessed | tf_op | source)
XLA Modules:
  0.0 55.5 jit_solution(968120749794742914)
XLA Ops:
  0.6 1.8 %prepare.1 = (bf16[32,24,128]{2,1,0:T(8,128)(2,1)}, f32[16,128]{1,0:T(8,128)S(1)}) custom-call(f32[3,2,8]{2,1,0:T(2,128)} %bitcast.9, f32[2,8]{1,0:T(2,128)} %bitcast.10, f32[3,40]{1,0:T(4,128)} %pos_ref.1, f32[1,40]{1,0:T(1,128)} %bitcast.11, bf16[40,64]{1,0:T(8,128)(2,1)} %bitcast.8, f32[3,128]{1,0:T(4,128)} %blank_ref.1, s32[1,128]{1,0:T(1,128)} %bitcast.12, ...), custom_call_target="tpu_custom_call" | custom-call | tf_op jit(solution)/shard_map/prepare/pallas_call | solution.py:234
  2.5 12.0 %all-to-all-start = ((bf16[32,24,128]{2,1,0:T(8,128)(2,1)}), bf16[32,24,128]{2,1,0:T(8,128)(2,1)S(1)}, u32[]{:S(2)}, u32[]{:S(2)}) async-start(bf16[32,24,128]{2,1,0:T(8,128)(2,1)} %get-tuple-element.18), calls=%async_computation | async-start | bytes 393216 | tf_op jit(solution)/shard_map/all_to_all | solution.py:241
  14.5 2.6 %collective-permute-start.2 = (f32[16,128]{1,0:T(8,128)S(1)}, f32[16,128]{1,0:T(8,128)S(1)}, u32[]{:S(2)}, u32[]{:S(2)}) collective-permute-start(f32[16,128]{1,0:T(8,128)S(1)} %get-tuple-element.19.refs_0_), channel_id=1, source_target_pairs={{0,18},{2,16},{16,2},{18,0},{1,19},{3,17},{17,3},{19,1},{4,22},{6,... | collective-permute-start | bytes 24584 | tf_op jit(solution)/shard_map/ppermute | solution.py:201
  17.1 0.5 collective-permute-start.1
  17.6 0.3 collective-permute-start
  17.8 0.5 collective-permute-done.2.refs_3_
  18.3 3.0 %collective-permute-done.1.refs_2_ = f32[16,128]{1,0:T(8,128)S(1)} collective-permute-done((f32[16,128]{1,0:T(8,128)S(1)}, f32[16,128]{1,0:T(8,128)S(1)}, u32[]{:S(2)}, u32[]{:S(2)}) %collective-permute-start.1) | collective-permute-done | bytes 8224 | tf_op jit(solution)/shard_map/ppermute | solution.py:201
  21.3 0.0 collective-permute-done.refs_1_
  21.3 0.1 blank_features.1
  21.4 2.8 %all-to-all-done.refs_0_ = bf16[32,24,128]{2,1,0:T(8,128)(2,1)S(1)} async-done(((bf16[32,24,128]{2,1,0:T(8,128)(2,1)}), bf16[32,24,128]{2,1,0:T(8,128)(2,1)S(1)}, u32[]{:S(2)}, u32[]{:S(2)}) %all-to-all-start) | async-done | bytes 196640 | tf_op jit(solution)/shard_map/all_to_all | solution.py:241
  24.2 2.6 %collective-permute-start.3 = (bf16[32,24,128]{2,1,0:T(8,128)(2,1)S(1)}, bf16[32,24,128]{2,1,0:T(8,128)(2,1)S(1)}, u32[]{:S(2)}, u32[]{:S(2)}) collective-permute-start(bf16[32,24,128]{2,1,0:T(8,128)(2,1)S(1)} %all-to-all-done.refs_0_), channel_id=1, source_target_pairs={{0,1},{1,0},{2,3},{3,2},{4,5},{5,4},{6,7},{7,6},{8,9},{9,8},{10,11... | collective-permute-start | bytes 589832 | tf_op jit(solution)/shard_map/ppermute | solution.py:201
  26.8 1.2 %form_own.1 = (bf16[5,256,512]{2,1,0:T(8,128)(2,1)S(1)}, f32[64,512]{1,0:T(8,128)S(1)}) custom-call(bf16[32,24,128]{2,1,0:T(8,128)(2,1)S(1)} %all-to-all-done.refs_0_, bf16[2,128,512]{2,1,0:T(8,128)(2,1)S(1)} %get-tuple-element.24.refs_1_, f32[16,512]{1,0:T(8,128)S(1)} %get-tuple-element.22.refs_2_.refs_0_), custom_call_target="tpu_custom_call" | custom-call | flops 503316480 | bytes 1638400 | tf_op jit(solution)/shard_map/form_own/pallas_call | solution.py:257
  28.1 1.2 %form_other.1 = (bf16[5,256,512]{2,1,0:T(8,128)(2,1)S(1)}, bf16[64,512]{1,0:T(8,128)(2,1)S(1)}) custom-call(bf16[32,24,128]{2,1,0:T(8,128)(2,1)S(1)} %collective-permute-done.3.refs_0_, bf16[2,128,512]{2,1,0:T(8,128)(2,1)S(1)} %get-tuple-element.24.refs_1_, f32[16,512]{1,0:T(8,128)S(1)} %get-tuple-element.22.refs_2_.refs_0_, ...), custom_call_target="tpu_custom_call" | custom-call | flops 503316480 | bytes 1638400 | tf_op jit(solution)/shard_map/form_other/pallas_call | solution.py:264
  29.3 2.6 %collective-permute-start.6 = (bf16[64,512]{1,0:T(8,128)(2,1)S(1)}, bf16[64,512]{1,0:T(8,128)(2,1)S(1)}, u32[]{:S(2)}, u32[]{:S(2)}) collective-permute-start(bf16[64,512]{1,0:T(8,128)(2,1)S(1)} %get-tuple-element.26.refs_1_), channel_id=1, source_target_pairs={{0,18},{2,16},{16,2},{18,0},{1,19},{3,17},{17,3},{19,1},{4,22},{6,... | collective-permute-start | bytes 196616 | tf_op jit(solution)/shard_map/ppermute | solution.py:201
  31.8 0.5 collective-permute-start.5
  32.3 0.3 collective-permute-start.4
  32.6 1.4 %collective-permute-done.6.refs_4_ = bf16[64,512]{1,0:T(8,128)(2,1)S(1)} collective-permute-done((bf16[64,512]{1,0:T(8,128)(2,1)S(1)}, bf16[64,512]{1,0:T(8,128)(2,1)S(1)}, u32[]{:S(2)}, u32[]{:S(2)}) %collective-permute-start.6) | collective-permute-done | bytes 65568 | tf_op jit(solution)/shard_map/ppermute | solution.py:201
  34.0 2.4 %collective-permute-done.5.refs_3_ = bf16[64,512]{1,0:T(8,128)(2,1)S(1)} collective-permute-done((bf16[64,512]{1,0:T(8,128)(2,1)S(1)}, bf16[64,512]{1,0:T(8,128)(2,1)S(1)}, u32[]{:S(2)}, u32[]{:S(2)}) %collective-permute-start.5) | collective-permute-done | bytes 65568 | tf_op jit(solution)/shard_map/ppermute | solution.py:201
  36.5 0.6 %weigh.1 = (bf16[64,128]{1,0:T(8,128)(2,1)S(1)}, bf16[64,512]{1,0:T(8,128)(2,1)S(1)}, bf16[32,2,1280]{2,1,0:T(2,128)(2,1)S(1)}) custom-call(f32[16,512]{1,0:T(8,128)S(1)} %get-tuple-element.22.refs_2_.refs_0_, bf16[64,512]{1,0:T(8,128)(2,1)S(1)} %get-tuple-element.26.refs_1_, bf16[64,512]{1,0:T(8,128)(2,1)S(1)} %collective-permute-done.4.refs_2_, ...), custom_call_target="tpu_custom_call" | custom-call | flops 83886080 | bytes 1638400 | tf_op jit(solution)/shard_map/weigh/pallas_call | solution.py:279
  37.0 2.2 %collective-permute-start.7 = (bf16[32,2,1280]{2,1,0:T(2,128)(2,1)S(1)}, bf16[32,2,1280]{2,1,0:T(2,128)(2,1)S(1)}, u32[]{:S(2)}, u32[]{:S(2)}) collective-permute-start(bf16[32,2,1280]{2,1,0:T(2,128)(2,1)S(1)} %get-tuple-element.33), channel_id=1, source_target_pairs={{0,1},{1,0},{2,3},{3,2},{4,5},{5,4},{6,7},{7,6},{8,9},{9,8},{10,11... | collective-permute-start | bytes 491528 | tf_op jit(solution)/shard_map/ppermute | solution.py:201
  39.2 1.0 %react.1 = (f32[32,2,1280]{2,1,0:T(2,128)S(1)}, bf16[64,128]{1,0:T(8,128)(2,1)}) custom-call(bf16[64,512]{1,0:T(8,128)(2,1)S(1)} %get-tuple-element.28.refs_0_, bf16[5,256,512]{2,1,0:T(8,128)(2,1)S(1)} %get-tuple-element.29.refs_1_, bf16[64,128]{1,0:T(8,128)(2,1)S(1)} %get-tuple-element.30.refs_2_), custom_call_target="tpu_custom_call" | custom-call | flops 83886080 | bytes 1638400 | tf_op jit(solution)/shard_map/react/pallas_call | solution.py:291
  40.2 0.2 add_convert_fusion
  40.4 14.3 %all_to_all.10.arrived_ref = bf16[32,2,1280]{2,1,0:T(2,128)(2,1)S(1)} all-to-all(bf16[32,2,1280]{2,1,0:T(2,128)(2,1)S(1)} %add_convert_fusion), channel_id=1, replica_groups=mesh['zh'=4,'zl'=2,'xh'=2,'y'=4,'xl'=2,'core'=2] {'zl','y','zh'}, dimensions={0} | all-to-all | bytes 327680 | tf_op jit(solution)/shard_map/all_to_all | solution.py:299
  54.7 0.8 %finish.1 = f32[40,64]{1,0:T(8,128)} custom-call(bf16[32,2,1280]{2,1,0:T(2,128)(2,1)S(1)} %all_to_all.10.arrived_ref), custom_call_target="tpu_custom_call" | custom-call | tf_op jit(solution)/shard_map/finish/pallas_call | solution.py:300
  (3 shorter events, 0.0 us)
Async XLA Ops:
  2.5 21.8 %all-to-all-start = ((bf16[32,24,128]{2,1,0:T(8,128)(2,1)}), bf16[32,24,128]{2,1,0:T(8,128)(2,1)S(1)}, u32[]{:S(2)}, u32[]{:S(2)}) async-start(bf16[32,24,128]{2,1,0:T(8,128)(2,1)} %get-tuple-element.18), calls=%async_computation | async-start | bytes 393216 | tf_op jit(solution)/shard_map/all_to_all | solution.py:241
  14.5 3.8 %collective-permute-start.2 = (f32[16,128]{1,0:T(8,128)S(1)}, f32[16,128]{1,0:T(8,128)S(1)}, u32[]{:S(2)}, u32[]{:S(2)}) collective-permute-start(f32[16,128]{1,0:T(8,128)S(1)} %get-tuple-element.19.refs_0_), channel_id=1, source_target_pairs={{0,18},{2,16},{16,2},{18,0},{1,19},{3,17},{17,3},{19,1},{4,22},{6,... | collective-permute-start | bytes 24584 | tf_op jit(solution)/shard_map/ppermute | solution.py:201
  17.1 4.3 %collective-permute-start.1 = (f32[16,128]{1,0:T(8,128)S(1)}, f32[16,128]{1,0:T(8,128)S(1)}, u32[]{:S(2)}, u32[]{:S(2)}) collective-permute-start(f32[16,128]{1,0:T(8,128)S(1)} %get-tuple-element.19.refs_0_), channel_id=1, source_target_pairs={{0,16},{2,18},{16,0},{18,2},{1,17},{3,19},{17,1},{19,3},{4,20},{6,... | collective-permute-start | bytes 24584 | tf_op jit(solution)/shard_map/ppermute | solution.py:201
  17.6 3.7 %collective-permute-start = (f32[16,128]{1,0:T(8,128)S(1)}, f32[16,128]{1,0:T(8,128)S(1)}, u32[]{:S(2)}, u32[]{:S(2)}) collective-permute-start(f32[16,128]{1,0:T(8,128)S(1)} %get-tuple-element.19.refs_0_), channel_id=1, source_target_pairs={{0,2},{2,0},{16,18},{18,16},{1,3},{3,1},{17,19},{19,17},{4,6},{6,4... | collective-permute-start | bytes 24584 | tf_op jit(solution)/shard_map/ppermute | solution.py:201
  24.2 3.8 %collective-permute-start.3 = (bf16[32,24,128]{2,1,0:T(8,128)(2,1)S(1)}, bf16[32,24,128]{2,1,0:T(8,128)(2,1)S(1)}, u32[]{:S(2)}, u32[]{:S(2)}) collective-permute-start(bf16[32,24,128]{2,1,0:T(8,128)(2,1)S(1)} %all-to-all-done.refs_0_), channel_id=1, source_target_pairs={{0,1},{1,0},{2,3},{3,2},{4,5},{5,4},{6,7},{7,6},{8,9},{9,8},{10,11... | collective-permute-start | bytes 589832 | tf_op jit(solution)/shard_map/ppermute | solution.py:201
  29.3 4.8 %collective-permute-start.6 = (bf16[64,512]{1,0:T(8,128)(2,1)S(1)}, bf16[64,512]{1,0:T(8,128)(2,1)S(1)}, u32[]{:S(2)}, u32[]{:S(2)}) collective-permute-start(bf16[64,512]{1,0:T(8,128)(2,1)S(1)} %get-tuple-element.26.refs_1_), channel_id=1, source_target_pairs={{0,18},{2,16},{16,2},{18,0},{1,19},{3,17},{17,3},{19,1},{4,22},{6,... | collective-permute-start | bytes 196616 | tf_op jit(solution)/shard_map/ppermute | solution.py:201
  31.8 4.6 %collective-permute-start.5 = (bf16[64,512]{1,0:T(8,128)(2,1)S(1)}, bf16[64,512]{1,0:T(8,128)(2,1)S(1)}, u32[]{:S(2)}, u32[]{:S(2)}) collective-permute-start(bf16[64,512]{1,0:T(8,128)(2,1)S(1)} %get-tuple-element.26.refs_1_), channel_id=1, source_target_pairs={{0,16},{2,18},{16,0},{18,2},{1,17},{3,19},{17,1},{19,3},{4,20},{6,... | collective-permute-start | bytes 196616 | tf_op jit(solution)/shard_map/ppermute | solution.py:201
  32.3 4.2 %collective-permute-start.4 = (bf16[64,512]{1,0:T(8,128)(2,1)S(1)}, bf16[64,512]{1,0:T(8,128)(2,1)S(1)}, u32[]{:S(2)}, u32[]{:S(2)}) collective-permute-start(bf16[64,512]{1,0:T(8,128)(2,1)S(1)} %get-tuple-element.26.refs_1_), channel_id=1, source_target_pairs={{0,2},{2,0},{16,18},{18,16},{1,3},{3,1},{17,19},{19,17},{4,6},{6,4... | collective-permute-start | bytes 196616 | tf_op jit(solution)/shard_map/ppermute | solution.py:201
  37.0 3.2 %collective-permute-start.7 = (bf16[32,2,1280]{2,1,0:T(2,128)(2,1)S(1)}, bf16[32,2,1280]{2,1,0:T(2,128)(2,1)S(1)}, u32[]{:S(2)}, u32[]{:S(2)}) collective-permute-start(bf16[32,2,1280]{2,1,0:T(2,128)(2,1)S(1)} %get-tuple-element.33), channel_id=1, source_target_pairs={{0,1},{1,0},{2,3},{3,2},{4,5},{5,4},{6,7},{7,6},{8,9},{9,8},{10,11... | collective-permute-start | bytes 491528 | tf_op jit(solution)/shard_map/ppermute | solution.py:201

commit v7 on v6

--- a/solution.py
+++ b/solution.py
@@ -187,7 +187,11 @@
 
 
 def finish(arrived_ref, out_ref):
-    total = jnp.sum(arrived_ref[...].astype(F32), 0)
+    parts = [arrived_ref[piece].astype(F32) for piece in range(arrived_ref.shape[0])]
+    while len(parts) > 1:
+        odd = parts[len(parts) // 2 * 2 :]
+        parts = [a + b for a, b in zip(parts[::2], parts[1::2], strict=False)] + odd
+    total = parts[0]
     rows = [total[:, LANES * pair : LANES * (pair + 1)] for pair in range(total.shape[1] // LANES)]
     rows = jnp.concatenate(rows, 0)
     samples = out_ref.shape[1]

time: 55.8 us -> 55.7 us (level)
  no operation moved by 1% of the time
where the time goes in v7:
time: 55.7 us; the launch traced here: 55.4 us
  starting transfers between devices  23.5 us (42%)
  blocking collectives  14.3 us (26%)
  waiting for transfers between devices  10.2 us (18%)
  Pallas kernels  6.62 us (12%)
  between operations  0.68 us (1%)
    all_to_all x1, blocking collectives, per_device(): arrived = lax.all_to_all(pieces, COLS, 0, 0, tiled=True)  14.3 us
    all_to_all x1, starting transfers between devices, per_device(): own = lax.all_to_all(payload, COLS, 0, 0, tiled=True)  12 us
    ppermute x8, starting transfers between devices, from_partner(): return lax.ppermute(value, axis, [(i, i ^ flip) for i in range(size)])  11.5 us
    ppermute x8, waiting for transfers between devices, from_partner(): return lax.ppermute(value, axis, [(i, i ^ flip) for i in range(size)])  7.34 us
    all_to_all x1, waiting for transfers between devices, per_device(): own = lax.all_to_all(payload, COLS, 0, 0, tiled=True)  2.82 us
    pallas_call x1, Pallas kernels, per_device(): pl.pallas_call(prepare, out_shape=(shaped(packed, BF16), shaped((16, blan...  1.82 us
    pallas_call x1, Pallas kernels, per_device(): pl.pallas_call(lambda *refs: form(True, *refs), out_shape=(kernel_shape,...  1.21 us
    pallas_call x1, Pallas kernels, per_device(): pl.pallas_call(lambda *refs: form(False, *refs), out_shape=(kernel_shape,...  1.19 us
  transfers between devices with their start and end apart: 9, of which 5 were waited for; matrix products, arithmetic and copies ran while one was open for 0% of the time, Pallas kernels for 4%

profile of v7, /device:TPU:1, one launch (start us, length us, event | category | flops | bytes accessed | tf_op | source)
XLA Modules:
  0.0 55.4 jit_solution(6584029376037957439)
XLA Ops:
  0.6 1.8 %prepare.1 = (bf16[32,24,128]{2,1,0:T(8,128)(2,1)}, f32[16,128]{1,0:T(8,128)S(1)}) custom-call(f32[3,2,8]{2,1,0:T(2,128)} %bitcast.9, f32[2,8]{1,0:T(2,128)} %bitcast.10, f32[3,40]{1,0:T(4,128)} %pos_ref.1, f32[1,40]{1,0:T(1,128)} %bitcast.11, bf16[40,64]{1,0:T(8,128)(2,1)} %bitcast.8, f32[3,128]{1,0:T(4,128)} %blank_ref.1, s32[1,128]{1,0:T(1,128)} %bitcast.12, ...), custom_call_target="tpu_custom_call" | custom-call | tf_op jit(solution)/shard_map/prepare/pallas_call | solution.py:238
  2.5 12.0 %all-to-all-start = ((bf16[32,24,128]{2,1,0:T(8,128)(2,1)}), bf16[32,24,128]{2,1,0:T(8,128)(2,1)S(1)}, u32[]{:S(2)}, u32[]{:S(2)}) async-start(bf16[32,24,128]{2,1,0:T(8,128)(2,1)} %get-tuple-element.18), calls=%async_computation | async-start | bytes 393216 | tf_op jit(solution)/shard_map/all_to_all | solution.py:245
  14.5 2.6 %collective-permute-start.2 = (f32[16,128]{1,0:T(8,128)S(1)}, f32[16,128]{1,0:T(8,128)S(1)}, u32[]{:S(2)}, u32[]{:S(2)}) collective-permute-start(f32[16,128]{1,0:T(8,128)S(1)} %get-tuple-element.19.refs_0_), channel_id=1, source_target_pairs={{0,18},{2,16},{16,2},{18,0},{1,19},{3,17},{17,3},{19,1},{4,22},{6,... | collective-permute-start | bytes 24584 | tf_op jit(solution)/shard_map/ppermute | solution.py:205
  17.1 0.5 collective-permute-start.1
  17.6 0.3 collective-permute-start
  17.8 0.5 collective-permute-done.2.refs_3_
  18.3 3.0 %collective-permute-done.1.refs_2_ = f32[16,128]{1,0:T(8,128)S(1)} collective-permute-done((f32[16,128]{1,0:T(8,128)S(1)}, f32[16,128]{1,0:T(8,128)S(1)}, u32[]{:S(2)}, u32[]{:S(2)}) %collective-permute-start.1) | collective-permute-done | bytes 8224 | tf_op jit(solution)/shard_map/ppermute | solution.py:205
  21.3 0.0 collective-permute-done.refs_1_
  21.3 0.1 blank_features.1
  21.4 2.8 %all-to-all-done.refs_0_ = bf16[32,24,128]{2,1,0:T(8,128)(2,1)S(1)} async-done(((bf16[32,24,128]{2,1,0:T(8,128)(2,1)}), bf16[32,24,128]{2,1,0:T(8,128)(2,1)S(1)}, u32[]{:S(2)}, u32[]{:S(2)}) %all-to-all-start) | async-done | bytes 196640 | tf_op jit(solution)/shard_map/all_to_all | solution.py:245
  24.2 2.6 %collective-permute-start.3 = (bf16[32,24,128]{2,1,0:T(8,128)(2,1)S(1)}, bf16[32,24,128]{2,1,0:T(8,128)(2,1)S(1)}, u32[]{:S(2)}, u32[]{:S(2)}) collective-permute-start(bf16[32,24,128]{2,1,0:T(8,128)(2,1)S(1)} %all-to-all-done.refs_0_), channel_id=1, source_target_pairs={{0,1},{1,0},{2,3},{3,2},{4,5},{5,4},{6,7},{7,6},{8,9},{9,8},{10,11... | collective-permute-start | bytes 589832 | tf_op jit(solution)/shard_map/ppermute | solution.py:205
  26.8 1.2 %form_own.1 = (bf16[5,256,512]{2,1,0:T(8,128)(2,1)S(1)}, f32[64,512]{1,0:T(8,128)S(1)}) custom-call(bf16[32,24,128]{2,1,0:T(8,128)(2,1)S(1)} %all-to-all-done.refs_0_, bf16[2,128,512]{2,1,0:T(8,128)(2,1)S(1)} %get-tuple-element.24.refs_1_, f32[16,512]{1,0:T(8,128)S(1)} %get-tuple-element.22.refs_2_.refs_0_), custom_call_target="tpu_custom_call" | custom-call | flops 503316480 | bytes 1638400 | tf_op jit(solution)/shard_map/form_own/pallas_call | solution.py:261
  28.1 1.2 %form_other.1 = (bf16[5,256,512]{2,1,0:T(8,128)(2,1)S(1)}, bf16[64,512]{1,0:T(8,128)(2,1)S(1)}) custom-call(bf16[32,24,128]{2,1,0:T(8,128)(2,1)S(1)} %collective-permute-done.3.refs_0_, bf16[2,128,512]{2,1,0:T(8,128)(2,1)S(1)} %get-tuple-element.24.refs_1_, f32[16,512]{1,0:T(8,128)S(1)} %get-tuple-element.22.refs_2_.refs_0_, ...), custom_call_target="tpu_custom_call" | custom-call | flops 503316480 | bytes 1638400 | tf_op jit(solution)/shard_map/form_other/pallas_call | solution.py:268
  29.3 2.6 %collective-permute-start.6 = (bf16[64,512]{1,0:T(8,128)(2,1)S(1)}, bf16[64,512]{1,0:T(8,128)(2,1)S(1)}, u32[]{:S(2)}, u32[]{:S(2)}) collective-permute-start(bf16[64,512]{1,0:T(8,128)(2,1)S(1)} %get-tuple-element.26.refs_1_), channel_id=1, source_target_pairs={{0,18},{2,16},{16,2},{18,0},{1,19},{3,17},{17,3},{19,1},{4,22},{6,... | collective-permute-start | bytes 196616 | tf_op jit(solution)/shard_map/ppermute | solution.py:205
  31.8 0.5 collective-permute-start.5
  32.3 0.3 collective-permute-start.4
  32.6 1.4 %collective-permute-done.6.refs_4_ = bf16[64,512]{1,0:T(8,128)(2,1)S(1)} collective-permute-done((bf16[64,512]{1,0:T(8,128)(2,1)S(1)}, bf16[64,512]{1,0:T(8,128)(2,1)S(1)}, u32[]{:S(2)}, u32[]{:S(2)}) %collective-permute-start.6) | collective-permute-done | bytes 65568 | tf_op jit(solution)/shard_map/ppermute | solution.py:205
  34.0 2.4 %collective-permute-done.5.refs_3_ = bf16[64,512]{1,0:T(8,128)(2,1)S(1)} collective-permute-done((bf16[64,512]{1,0:T(8,128)(2,1)S(1)}, bf16[64,512]{1,0:T(8,128)(2,1)S(1)}, u32[]{:S(2)}, u32[]{:S(2)}) %collective-permute-start.5) | collective-permute-done | bytes 65568 | tf_op jit(solution)/shard_map/ppermute | solution.py:205
  36.5 0.6 %weigh.1 = (bf16[64,128]{1,0:T(8,128)(2,1)S(1)}, bf16[64,512]{1,0:T(8,128)(2,1)S(1)}, bf16[32,2,1280]{2,1,0:T(2,128)(2,1)S(1)}) custom-call(f32[16,512]{1,0:T(8,128)S(1)} %get-tuple-element.22.refs_2_.refs_0_, bf16[64,512]{1,0:T(8,128)(2,1)S(1)} %get-tuple-element.26.refs_1_, bf16[64,512]{1,0:T(8,128)(2,1)S(1)} %collective-permute-done.4.refs_2_, ...), custom_call_target="tpu_custom_call" | custom-call | flops 83886080 | bytes 1638400 | tf_op jit(solution)/shard_map/weigh/pallas_call | solution.py:283
  37.0 2.2 %collective-permute-start.7 = (bf16[32,2,1280]{2,1,0:T(2,128)(2,1)S(1)}, bf16[32,2,1280]{2,1,0:T(2,128)(2,1)S(1)}, u32[]{:S(2)}, u32[]{:S(2)}) collective-permute-start(bf16[32,2,1280]{2,1,0:T(2,128)(2,1)S(1)} %get-tuple-element.33), channel_id=1, source_target_pairs={{0,1},{1,0},{2,3},{3,2},{4,5},{5,4},{6,7},{7,6},{8,9},{9,8},{10,11... | collective-permute-start | bytes 491528 | tf_op jit(solution)/shard_map/ppermute | solution.py:205
  39.2 1.0 %react.1 = (f32[32,2,1280]{2,1,0:T(2,128)S(1)}, bf16[64,128]{1,0:T(8,128)(2,1)}) custom-call(bf16[64,512]{1,0:T(8,128)(2,1)S(1)} %get-tuple-element.28.refs_0_, bf16[5,256,512]{2,1,0:T(8,128)(2,1)S(1)} %get-tuple-element.29.refs_1_, bf16[64,128]{1,0:T(8,128)(2,1)S(1)} %get-tuple-element.30.refs_2_), custom_call_target="tpu_custom_call" | custom-call | flops 83886080 | bytes 1638400 | tf_op jit(solution)/shard_map/react/pallas_call | solution.py:295
  40.2 0.2 add_convert_fusion
  40.4 14.3 %all_to_all.10.arrived_ref = bf16[32,2,1280]{2,1,0:T(2,128)(2,1)S(1)} all-to-all(bf16[32,2,1280]{2,1,0:T(2,128)(2,1)S(1)} %add_convert_fusion), channel_id=1, replica_groups=mesh['zh'=4,'zl'=2,'xh'=2,'y'=4,'xl'=2,'core'=2] {'zl','y','zh'}, dimensions={0} | all-to-all | bytes 327680 | tf_op jit(solution)/shard_map/all_to_all | solution.py:303
  54.7 0.7 %finish.1 = f32[40,64]{1,0:T(8,128)} custom-call(bf16[32,2,1280]{2,1,0:T(2,128)(2,1)S(1)} %all_to_all.10.arrived_ref), custom_call_target="tpu_custom_call" | custom-call | tf_op jit(solution)/shard_map/finish/pallas_call | solution.py:304
  (3 shorter events, 0.0 us)
Async XLA Ops:
  2.5 21.8 %all-to-all-start = ((bf16[32,24,128]{2,1,0:T(8,128)(2,1)}), bf16[32,24,128]{2,1,0:T(8,128)(2,1)S(1)}, u32[]{:S(2)}, u32[]{:S(2)}) async-start(bf16[32,24,128]{2,1,0:T(8,128)(2,1)} %get-tuple-element.18), calls=%async_computation | async-start | bytes 393216 | tf_op jit(solution)/shard_map/all_to_all | solution.py:245
  14.5 3.8 %collective-permute-start.2 = (f32[16,128]{1,0:T(8,128)S(1)}, f32[16,128]{1,0:T(8,128)S(1)}, u32[]{:S(2)}, u32[]{:S(2)}) collective-permute-start(f32[16,128]{1,0:T(8,128)S(1)} %get-tuple-element.19.refs_0_), channel_id=1, source_target_pairs={{0,18},{2,16},{16,2},{18,0},{1,19},{3,17},{17,3},{19,1},{4,22},{6,... | collective-permute-start | bytes 24584 | tf_op jit(solution)/shard_map/ppermute | solution.py:205
  17.1 4.3 %collective-permute-start.1 = (f32[16,128]{1,0:T(8,128)S(1)}, f32[16,128]{1,0:T(8,128)S(1)}, u32[]{:S(2)}, u32[]{:S(2)}) collective-permute-start(f32[16,128]{1,0:T(8,128)S(1)} %get-tuple-element.19.refs_0_), channel_id=1, source_target_pairs={{0,16},{2,18},{16,0},{18,2},{1,17},{3,19},{17,1},{19,3},{4,20},{6,... | collective-permute-start | bytes 24584 | tf_op jit(solution)/shard_map/ppermute | solution.py:205
  17.6 3.7 %collective-permute-start = (f32[16,128]{1,0:T(8,128)S(1)}, f32[16,128]{1,0:T(8,128)S(1)}, u32[]{:S(2)}, u32[]{:S(2)}) collective-permute-start(f32[16,128]{1,0:T(8,128)S(1)} %get-tuple-element.19.refs_0_), channel_id=1, source_target_pairs={{0,2},{2,0},{16,18},{18,16},{1,3},{3,1},{17,19},{19,17},{4,6},{6,4... | collective-permute-start | bytes 24584 | tf_op jit(solution)/shard_map/ppermute | solution.py:205
  24.2 3.8 %collective-permute-start.3 = (bf16[32,24,128]{2,1,0:T(8,128)(2,1)S(1)}, bf16[32,24,128]{2,1,0:T(8,128)(2,1)S(1)}, u32[]{:S(2)}, u32[]{:S(2)}) collective-permute-start(bf16[32,24,128]{2,1,0:T(8,128)(2,1)S(1)} %all-to-all-done.refs_0_), channel_id=1, source_target_pairs={{0,1},{1,0},{2,3},{3,2},{4,5},{5,4},{6,7},{7,6},{8,9},{9,8},{10,11... | collective-permute-start | bytes 589832 | tf_op jit(solution)/shard_map/ppermute | solution.py:205
  29.3 4.8 %collective-permute-start.6 = (bf16[64,512]{1,0:T(8,128)(2,1)S(1)}, bf16[64,512]{1,0:T(8,128)(2,1)S(1)}, u32[]{:S(2)}, u32[]{:S(2)}) collective-permute-start(bf16[64,512]{1,0:T(8,128)(2,1)S(1)} %get-tuple-element.26.refs_1_), channel_id=1, source_target_pairs={{0,18},{2,16},{16,2},{18,0},{1,19},{3,17},{17,3},{19,1},{4,22},{6,... | collective-permute-start | bytes 196616 | tf_op jit(solution)/shard_map/ppermute | solution.py:205
  31.8 4.6 %collective-permute-start.5 = (bf16[64,512]{1,0:T(8,128)(2,1)S(1)}, bf16[64,512]{1,0:T(8,128)(2,1)S(1)}, u32[]{:S(2)}, u32[]{:S(2)}) collective-permute-start(bf16[64,512]{1,0:T(8,128)(2,1)S(1)} %get-tuple-element.26.refs_1_), channel_id=1, source_target_pairs={{0,16},{2,18},{16,0},{18,2},{1,17},{3,19},{17,1},{19,3},{4,20},{6,... | collective-permute-start | bytes 196616 | tf_op jit(solution)/shard_map/ppermute | solution.py:205
  32.3 4.2 %collective-permute-start.4 = (bf16[64,512]{1,0:T(8,128)(2,1)S(1)}, bf16[64,512]{1,0:T(8,128)(2,1)S(1)}, u32[]{:S(2)}, u32[]{:S(2)}) collective-permute-start(bf16[64,512]{1,0:T(8,128)(2,1)S(1)} %get-tuple-element.26.refs_1_), channel_id=1, source_target_pairs={{0,2},{2,0},{16,18},{18,16},{1,3},{3,1},{17,19},{19,17},{4,6},{6,4... | collective-permute-start | bytes 196616 | tf_op jit(solution)/shard_map/ppermute | solution.py:205
  37.0 3.2 %collective-permute-start.7 = (bf16[32,2,1280]{2,1,0:T(2,128)(2,1)S(1)}, bf16[32,2,1280]{2,1,0:T(2,128)(2,1)S(1)}, u32[]{:S(2)}, u32[]{:S(2)}) collective-permute-start(bf16[32,2,1280]{2,1,0:T(2,128)(2,1)S(1)} %get-tuple-element.33), channel_id=1, source_target_pairs={{0,1},{1,0},{2,3},{3,2},{4,5},{5,4},{6,7},{7,6},{8,9},{9,8},{10,11... | collective-permute-start | bytes 491528 | tf_op jit(solution)/shard_map/ppermute | solution.py:205

commit v8 on v7

--- a/solution.py
+++ b/solution.py
@@ -181,12 +181,12 @@
     store_rows(out_ref, [scale * part for part in contract(kernel_ref, weighted)])
 
 
-def react(scale, weighted_ref, kernel_ref, current_ref, out_ref, blank_ref):
+def react(scale, weighted_ref, kernel_ref, out_ref):
     store_rows(out_ref, [scale * part for part in contract(kernel_ref, weighted_ref[...])])
+
+
+def finish(arrived_ref, current_ref, out_ref, blank_ref):
     blank_ref[...] = current_ref[...]
-
-
-def finish(arrived_ref, out_ref):
     parts = [arrived_ref[piece].astype(F32) for piece in range(arrived_ref.shape[0])]
     while len(parts) > 1:
         odd = parts[len(parts) // 2 * 2 :]
@@ -292,21 +292,21 @@
         name="weigh",
     )(table, *arrivals, other_kernel)
     crossed = from_partner(reaction, "core", 1)
-    reaction, blank_current = pl.pallas_call(
+    reaction = pl.pallas_call(
         lambda *refs: react(scale, *refs),
-        out_shape=(shaped(dense, F32), shaped((samples, blanks), BF16)),
+        out_shape=shaped(dense, F32),
         compiler_params=ROOM,
         cost_estimate=react_cost,
         name="react",
-    )(weighted, own_kernel, blank_current)
+    )(weighted, own_kernel)
     pieces = (reaction + crossed.astype(F32)).astype(BF16)
     arrived = lax.all_to_all(pieces, COLS, 0, 0, tiled=True)
-    coil_reaction = pl.pallas_call(
+    coil_reaction, blank_current = pl.pallas_call(
         finish,
-        out_shape=shaped((coils, samples), F32),
+        out_shape=(shaped((coils, samples), F32), shaped((samples, blanks), BF16)),
         compiler_params=ROOM,
         name="finish",
-    )(arrived)
+    )(arrived, blank_current)
     return (blank_current, coil_reaction.T)
 
 

time: 55.7 us -> 55.7 us (level)
  Pallas kernels: 6.62 us -> 6.04 us
  transfers between devices with their start and end apart: 9 -> 9, of which waited for: 5 -> 6; matrix products, arithmetic and copies ran while one was open for 0% -> 0% of each run, Pallas kernels for 4% -> 3%
where the time goes in v8:
time: 55.7 us; the launch traced here: 55.4 us
  starting transfers between devices  23.5 us (42%)
  blocking collectives  14.3 us (26%)
  waiting for transfers between devices  10.7 us (19%)
  Pallas kernels  6.04 us (11%)
  between operations  0.69 us (1%)
    all_to_all x1, blocking collectives, per_device(): arrived = lax.all_to_all(pieces, COLS, 0, 0, tiled=True)  14.3 us
    all_to_all x1, starting transfers between devices, per_device(): own = lax.all_to_all(payload, COLS, 0, 0, tiled=True)  12 us
    ppermute x8, starting transfers between devices, from_partner(): return lax.ppermute(value, axis, [(i, i ^ flip) for i in range(size)])  11.5 us
    ppermute x8, waiting for transfers between devices, from_partner(): return lax.ppermute(value, axis, [(i, i ^ flip) for i in range(size)])  7.9 us
    all_to_all x1, waiting for transfers between devices, per_device(): own = lax.all_to_all(payload, COLS, 0, 0, tiled=True)  2.82 us
    pallas_call x1, Pallas kernels, per_device(): pl.pallas_call(prepare, out_shape=(shaped(packed, BF16), shaped((16, blan...  1.82 us
    pallas_call x1, Pallas kernels, per_device(): pl.pallas_call(lambda *refs: form(False, *refs), out_shape=(kernel_shape,...  1.19 us
    pallas_call x1, Pallas kernels, per_device(): pl.pallas_call(lambda *refs: form(True, *refs), out_shape=(kernel_shape,...  1.17 us
  transfers between devices with their start and end apart: 9, of which 6 were waited for; matrix products, arithmetic and copies ran while one was open for 0% of the time, Pallas kernels for 3%

profile of v8, /device:TPU:1, one launch (start us, length us, event | category | flops | bytes accessed | tf_op | source)
XLA Modules:
  0.0 55.4 jit_solution(4998712412606456733)
XLA Ops:
  0.6 1.8 %prepare.1 = (bf16[32,24,128]{2,1,0:T(8,128)(2,1)}, f32[16,128]{1,0:T(8,128)S(1)}) custom-call(f32[3,2,8]{2,1,0:T(2,128)} %bitcast.8, f32[2,8]{1,0:T(2,128)} %bitcast.9, f32[3,40]{1,0:T(4,128)} %pos_ref.1, f32[1,40]{1,0:T(1,128)} %bitcast.10, bf16[40,64]{1,0:T(8,128)(2,1)} %bitcast.7, f32[3,128]{1,0:T(4,128)} %blank_ref.1, s32[1,128]{1,0:T(1,128)} %bitcast.11, ...), custom_call_target="tpu_custom_call" | custom-call | tf_op jit(solution)/shard_map/prepare/pallas_call | solution.py:238
  2.5 12.0 %all-to-all-start = ((bf16[32,24,128]{2,1,0:T(8,128)(2,1)}), bf16[32,24,128]{2,1,0:T(8,128)(2,1)S(1)}, u32[]{:S(2)}, u32[]{:S(2)}) async-start(bf16[32,24,128]{2,1,0:T(8,128)(2,1)} %get-tuple-element.18), calls=%async_computation | async-start | bytes 393216 | tf_op jit(solution)/shard_map/all_to_all | solution.py:245
  14.5 2.6 %collective-permute-start.2 = (f32[16,128]{1,0:T(8,128)S(1)}, f32[16,128]{1,0:T(8,128)S(1)}, u32[]{:S(2)}, u32[]{:S(2)}) collective-permute-start(f32[16,128]{1,0:T(8,128)S(1)} %get-tuple-element.19.refs_0_), channel_id=1, source_target_pairs={{0,18},{2,16},{16,2},{18,0},{1,19},{3,17},{17,3},{19,1},{4,22},{6,... | collective-permute-start | bytes 24584 | tf_op jit(solution)/shard_map/ppermute | solution.py:205
  17.1 0.5 collective-permute-start.1
  17.6 0.3 collective-permute-start
  17.8 0.5 collective-permute-done.2.refs_3_
  18.3 3.0 %collective-permute-done.1.refs_2_ = f32[16,128]{1,0:T(8,128)S(1)} collective-permute-done((f32[16,128]{1,0:T(8,128)S(1)}, f32[16,128]{1,0:T(8,128)S(1)}, u32[]{:S(2)}, u32[]{:S(2)}) %collective-permute-start.1) | collective-permute-done | bytes 8224 | tf_op jit(solution)/shard_map/ppermute | solution.py:205
  21.3 0.1 blank_features.1
  21.4 2.8 %all-to-all-done.refs_0_ = bf16[32,24,128]{2,1,0:T(8,128)(2,1)S(1)} async-done(((bf16[32,24,128]{2,1,0:T(8,128)(2,1)}), bf16[32,24,128]{2,1,0:T(8,128)(2,1)S(1)}, u32[]{:S(2)}, u32[]{:S(2)}) %all-to-all-start) | async-done | bytes 196640 | tf_op jit(solution)/shard_map/all_to_all | solution.py:245
  24.2 2.6 %collective-permute-start.3 = (bf16[32,24,128]{2,1,0:T(8,128)(2,1)S(1)}, bf16[32,24,128]{2,1,0:T(8,128)(2,1)S(1)}, u32[]{:S(2)}, u32[]{:S(2)}) collective-permute-start(bf16[32,24,128]{2,1,0:T(8,128)(2,1)S(1)} %all-to-all-done.refs_0_), channel_id=1, source_target_pairs={{0,1},{1,0},{2,3},{3,2},{4,5},{5,4},{6,7},{7,6},{8,9},{9,8},{10,11... | collective-permute-start | bytes 589832 | tf_op jit(solution)/shard_map/ppermute | solution.py:205
  26.8 1.2 %form_own.1 = (bf16[5,256,512]{2,1,0:T(8,128)(2,1)S(1)}, f32[64,512]{1,0:T(8,128)S(1)}) custom-call(bf16[32,24,128]{2,1,0:T(8,128)(2,1)S(1)} %all-to-all-done.refs_0_, bf16[2,128,512]{2,1,0:T(8,128)(2,1)S(1)} %get-tuple-element.24.refs_1_, f32[16,512]{1,0:T(8,128)S(1)} %get-tuple-element.22.refs_2_.refs_0_), custom_call_target="tpu_custom_call" | custom-call | flops 503316480 | bytes 1638400 | tf_op jit(solution)/shard_map/form_own/pallas_call | solution.py:261
  28.0 1.2 %form_other.1 = (bf16[5,256,512]{2,1,0:T(8,128)(2,1)S(1)}, bf16[64,512]{1,0:T(8,128)(2,1)S(1)}) custom-call(bf16[32,24,128]{2,1,0:T(8,128)(2,1)S(1)} %collective-permute-done.3.refs_0_, bf16[2,128,512]{2,1,0:T(8,128)(2,1)S(1)} %get-tuple-element.24.refs_1_, f32[16,512]{1,0:T(8,128)S(1)} %get-tuple-element.22.refs_2_.refs_0_, ...), custom_call_target="tpu_custom_call" | custom-call | flops 503316480 | bytes 1638400 | tf_op jit(solution)/shard_map/form_other/pallas_call | solution.py:268
  29.2 2.6 %collective-permute-start.6 = (bf16[64,512]{1,0:T(8,128)(2,1)S(1)}, bf16[64,512]{1,0:T(8,128)(2,1)S(1)}, u32[]{:S(2)}, u32[]{:S(2)}) collective-permute-start(bf16[64,512]{1,0:T(8,128)(2,1)S(1)} %get-tuple-element.26.refs_1_), channel_id=1, source_target_pairs={{0,18},{2,16},{16,2},{18,0},{1,19},{3,17},{17,3},{19,1},{4,22},{6,... | collective-permute-start | bytes 196616 | tf_op jit(solution)/shard_map/ppermute | solution.py:205
  31.8 0.5 collective-permute-start.5
  32.3 0.2 collective-permute-start.4
  32.6 1.1 %collective-permute-done.6.refs_4_ = bf16[64,512]{1,0:T(8,128)(2,1)S(1)} collective-permute-done((bf16[64,512]{1,0:T(8,128)(2,1)S(1)}, bf16[64,512]{1,0:T(8,128)(2,1)S(1)}, u32[]{:S(2)}, u32[]{:S(2)}) %collective-permute-start.6) | collective-permute-done | bytes 65568 | tf_op jit(solution)/shard_map/ppermute | solution.py:205
  33.6 2.8 %collective-permute-done.5.refs_3_ = bf16[64,512]{1,0:T(8,128)(2,1)S(1)} collective-permute-done((bf16[64,512]{1,0:T(8,128)(2,1)S(1)}, bf16[64,512]{1,0:T(8,128)(2,1)S(1)}, u32[]{:S(2)}, u32[]{:S(2)}) %collective-permute-start.5) | collective-permute-done | bytes 65568 | tf_op jit(solution)/shard_map/ppermute | solution.py:205
  36.5 0.6 %weigh.1 = (bf16[64,128]{1,0:T(8,128)(2,1)S(1)}, bf16[64,512]{1,0:T(8,128)(2,1)S(1)}, bf16[32,2,1280]{2,1,0:T(2,128)(2,1)S(1)}) custom-call(f32[16,512]{1,0:T(8,128)S(1)} %get-tuple-element.22.refs_2_.refs_0_, bf16[64,512]{1,0:T(8,128)(2,1)S(1)} %get-tuple-element.26.refs_1_, bf16[64,512]{1,0:T(8,128)(2,1)S(1)} %collective-permute-done.4.refs_2_, ...), custom_call_target="tpu_custom_call" | custom-call | flops 83886080 | bytes 1638400 | tf_op jit(solution)/shard_map/weigh/pallas_call | solution.py:283
  37.0 2.2 %collective-permute-start.7 = (bf16[32,2,1280]{2,1,0:T(2,128)(2,1)S(1)}, bf16[32,2,1280]{2,1,0:T(2,128)(2,1)S(1)}, u32[]{:S(2)}, u32[]{:S(2)}) collective-permute-start(bf16[32,2,1280]{2,1,0:T(2,128)(2,1)S(1)} %get-tuple-element.30), channel_id=1, source_target_pairs={{0,1},{1,0},{2,3},{3,2},{4,5},{5,4},{6,7},{7,6},{8,9},{9,8},{10,11... | collective-permute-start | bytes 491528 | tf_op jit(solution)/shard_map/ppermute | solution.py:205
  39.2 0.5 react.1
  39.7 0.5 collective-permute-done.7
  40.2 0.2 add_convert_fusion
  40.4 14.3 %all_to_all.10.arrived_ref = bf16[32,2,1280]{2,1,0:T(2,128)(2,1)S(1)} all-to-all(bf16[32,2,1280]{2,1,0:T(2,128)(2,1)S(1)} %add_convert_fusion), channel_id=1, replica_groups=mesh['zh'=4,'zl'=2,'xh'=2,'y'=4,'xl'=2,'core'=2] {'zl','y','zh'}, dimensions={0} | all-to-all | bytes 327680 | tf_op jit(solution)/shard_map/all_to_all | solution.py:303
  54.7 0.7 %finish.1 = (f32[40,64]{1,0:T(8,128)}, bf16[64,128]{1,0:T(8,128)(2,1)}) custom-call(bf16[32,2,1280]{2,1,0:T(2,128)(2,1)S(1)} %all_to_all.10.arrived_ref, bf16[64,128]{1,0:T(8,128)(2,1)S(1)} %get-tuple-element.31.current_ref), custom_call_target="tpu_custom_call" | custom-call | tf_op jit(solution)/shard_map/finish/pallas_call | solution.py:304
  (3 shorter events, 0.0 us)
Async XLA Ops:
  2.5 21.8 %all-to-all-start = ((bf16[32,24,128]{2,1,0:T(8,128)(2,1)}), bf16[32,24,128]{2,1,0:T(8,128)(2,1)S(1)}, u32[]{:S(2)}, u32[]{:S(2)}) async-start(bf16[32,24,128]{2,1,0:T(8,128)(2,1)} %get-tuple-element.18), calls=%async_computation | async-start | bytes 393216 | tf_op jit(solution)/shard_map/all_to_all | solution.py:245
  14.5 3.8 %collective-permute-start.2 = (f32[16,128]{1,0:T(8,128)S(1)}, f32[16,128]{1,0:T(8,128)S(1)}, u32[]{:S(2)}, u32[]{:S(2)}) collective-permute-start(f32[16,128]{1,0:T(8,128)S(1)} %get-tuple-element.19.refs_0_), channel_id=1, source_target_pairs={{0,18},{2,16},{16,2},{18,0},{1,19},{3,17},{17,3},{19,1},{4,22},{6,... | collective-permute-start | bytes 24584 | tf_op jit(solution)/shard_map/ppermute | solution.py:205
  17.1 4.3 %collective-permute-start.1 = (f32[16,128]{1,0:T(8,128)S(1)}, f32[16,128]{1,0:T(8,128)S(1)}, u32[]{:S(2)}, u32[]{:S(2)}) collective-permute-start(f32[16,128]{1,0:T(8,128)S(1)} %get-tuple-element.19.refs_0_), channel_id=1, source_target_pairs={{0,16},{2,18},{16,0},{18,2},{1,17},{3,19},{17,1},{19,3},{4,20},{6,... | collective-permute-start | bytes 24584 | tf_op jit(solution)/shard_map/ppermute | solution.py:205
  17.6 3.7 %collective-permute-start = (f32[16,128]{1,0:T(8,128)S(1)}, f32[16,128]{1,0:T(8,128)S(1)}, u32[]{:S(2)}, u32[]{:S(2)}) collective-permute-start(f32[16,128]{1,0:T(8,128)S(1)} %get-tuple-element.19.refs_0_), channel_id=1, source_target_pairs={{0,2},{2,0},{16,18},{18,16},{1,3},{3,1},{17,19},{19,17},{4,6},{6,4... | collective-permute-start | bytes 24584 | tf_op jit(solution)/shard_map/ppermute | solution.py:205
  24.2 3.8 %collective-permute-start.3 = (bf16[32,24,128]{2,1,0:T(8,128)(2,1)S(1)}, bf16[32,24,128]{2,1,0:T(8,128)(2,1)S(1)}, u32[]{:S(2)}, u32[]{:S(2)}) collective-permute-start(bf16[32,24,128]{2,1,0:T(8,128)(2,1)S(1)} %all-to-all-done.refs_0_), channel_id=1, source_target_pairs={{0,1},{1,0},{2,3},{3,2},{4,5},{5,4},{6,7},{7,6},{8,9},{9,8},{10,11... | collective-permute-start | bytes 589832 | tf_op jit(solution)/shard_map/ppermute | solution.py:205
  29.2 4.4 %collective-permute-start.6 = (bf16[64,512]{1,0:T(8,128)(2,1)S(1)}, bf16[64,512]{1,0:T(8,128)(2,1)S(1)}, u32[]{:S(2)}, u32[]{:S(2)}) collective-permute-start(bf16[64,512]{1,0:T(8,128)(2,1)S(1)} %get-tuple-element.26.refs_1_), channel_id=1, source_target_pairs={{0,18},{2,16},{16,2},{18,0},{1,19},{3,17},{17,3},{19,1},{4,22},{6,... | collective-permute-start | bytes 196616 | tf_op jit(solution)/shard_map/ppermute | solution.py:205
  31.8 4.6 %collective-permute-start.5 = (bf16[64,512]{1,0:T(8,128)(2,1)S(1)}, bf16[64,512]{1,0:T(8,128)(2,1)S(1)}, u32[]{:S(2)}, u32[]{:S(2)}) collective-permute-start(bf16[64,512]{1,0:T(8,128)(2,1)S(1)} %get-tuple-element.26.refs_1_), channel_id=1, source_target_pairs={{0,16},{2,18},{16,0},{18,2},{1,17},{3,19},{17,1},{19,3},{4,20},{6,... | collective-permute-start | bytes 196616 | tf_op jit(solution)/shard_map/ppermute | solution.py:205
  32.3 4.1 %collective-permute-start.4 = (bf16[64,512]{1,0:T(8,128)(2,1)S(1)}, bf16[64,512]{1,0:T(8,128)(2,1)S(1)}, u32[]{:S(2)}, u32[]{:S(2)}) collective-permute-start(bf16[64,512]{1,0:T(8,128)(2,1)S(1)} %get-tuple-element.26.refs_1_), channel_id=1, source_target_pairs={{0,2},{2,0},{16,18},{18,16},{1,3},{3,1},{17,19},{19,17},{4,6},{6,4... | collective-permute-start | bytes 196616 | tf_op jit(solution)/shard_map/ppermute | solution.py:205
  37.0 3.2 %collective-permute-start.7 = (bf16[32,2,1280]{2,1,0:T(2,128)(2,1)S(1)}, bf16[32,2,1280]{2,1,0:T(2,128)(2,1)S(1)}, u32[]{:S(2)}, u32[]{:S(2)}) collective-permute-start(bf16[32,2,1280]{2,1,0:T(2,128)(2,1)S(1)} %get-tuple-element.30), channel_id=1, source_target_pairs={{0,1},{1,0},{2,3},{3,2},{4,5},{5,4},{6,7},{7,6},{8,9},{9,8},{10,11... | collective-permute-start | bytes 491528 | tf_op jit(solution)/shard_map/ppermute | solution.py:205
